TPU v7x, 32 devices: a whole 2x2x4 slice. The times are simulated.
32 devices in a mesh: dp: 2 (over y), row: 4 (over x, core), col: 4 (over z).
Axes of the slice: x: 2, y: 2, z: 4, core: 2. Of those that a mesh axis runs over, the one named last changes fastest.
Arguments:
- features: bfloat16 [2, 32, 512, 256], P('dp', 'row', 'col'), may hold values from -6 to 6
- reduce_weight: bfloat16 [256, 128], replicated, may hold values from -0.375 to 0.375
- scale_one: float32 [128], replicated, may hold values from 0.25 to 1.75
- shift_one: float32 [128], replicated, may hold values from -3 to 3
- group_weight: bfloat16 [3, 3, 4, 128], replicated, may hold values from -1 to 1
- scale_two: float32 [128], replicated, may hold values from 0.25 to 1.75
- shift_two: float32 [128], replicated, may hold values from -3 to 3
- expand_weight: bfloat16 [128, 256], replicated, may hold values from -0.5 to 0.5
- scale_three: float32 [256], replicated, may hold values from 0.25 to 1.75
- shift_three: float32 [256], replicated, may hold values from -3 to 3
- cotangent: bfloat16 [2, 32, 512, 256], P('dp', 'row', 'col'), may hold values from -6 to 6
Outputs:
- input_grad: bfloat16 [2, 32, 512, 256], P('dp', 'row', 'col')
- reduce_grad: float32 [256, 128], P('dp')
- group_grad: float32 [128, 3, 3, 4], P('dp')
- expand_grad: float32 [128, 256], P('dp')
All inputs are finite; a program needn't handle non-finite values.
Results may differ from a plain program's by a relative error of at most 0.0069.
Values may be sent and summed in bfloat16 or wider, within the bound.
No kernel may reach another device: no remote copies, remote signals or barrier semaphores. Data moves between devices by JAX's collectives and lax.ppermute only.
A program may use at most 128 MiB of HBM per device.

v0:
```python
import jax
import jax.numpy as jnp
from jax import lax
from jax.sharding import PartitionSpec as P


def extended(block, sides, width):
    for axis, dim in sides:
        count = lax.axis_size(axis)
        forward = [(i, i + 1) for i in range(count - 1)]
        backward = [(target, source) for source, target in forward]
        low = lax.ppermute(
            lax.slice_in_dim(block, block.shape[dim] - width, None, axis=dim), axis, forward
        )
        high = lax.ppermute(lax.slice_in_dim(block, 0, width, axis=dim), axis, backward)
        block = jnp.concatenate([low, block, high], axis=dim)
    return block


def dsilu(value):
    sg = jax.nn.sigmoid(value)
    return sg * (1.0 + value * (1.0 - sg))


def group_conv(inputs, kernel):
    groups = kernel.shape[3] // kernel.shape[2]
    return lax.conv_general_dilated(
        inputs,
        kernel,
        (1, 1),
        ((0, 0), (0, 0)),
        dimension_numbers=("NHWC", "HWIO", "NHWC"),
        feature_group_count=groups,
        preferred_element_type=jnp.float32,
    )


def body(
    features,
    reduce_weight,
    scale_one,
    shift_one,
    group_weight,
    scale_two,
    shift_two,
    expand_weight,
    scale_three,
    shift_three,
    cotangent,
):
    rows = features.shape[1]
    cols = features.shape[2]
    chans = features.shape[3]
    inner = reduce_weight.shape[1]
    group_ch = group_weight.shape[2]
    groups = inner // group_ch
    flat = features.reshape(-1, chans)
    pre_one = (
        jnp.dot(flat, reduce_weight, preferred_element_type=jnp.float32) * scale_one + shift_one
    )
    act_one = jax.nn.silu(pre_one).astype(jnp.bfloat16)
    img_one = act_one.reshape(1, rows, cols, inner)
    padded_act = extended(img_one, (("row", 1), ("col", 2)), 1)
    pre_two = group_conv(padded_act, group_weight).reshape(-1, inner) * scale_two + shift_two
    act_two = jax.nn.silu(pre_two).astype(jnp.bfloat16)
    pre_three = (
        jnp.dot(act_two, expand_weight, preferred_element_type=jnp.float32) * scale_three
        + shift_three
        + flat.astype(jnp.float32)
    )
    back_three = cotangent.reshape(-1, chans).astype(jnp.float32) * dsilu(pre_three)
    grad_three = (back_three * scale_three).astype(jnp.bfloat16)
    gw_three = lax.dot_general(
        act_two, grad_three, (((0,), (0,)), ((), ())), preferred_element_type=jnp.float32
    )
    grad_two = (
        jnp.dot(grad_three, expand_weight.T, preferred_element_type=jnp.float32)
        * dsilu(pre_two)
        * scale_two
    ).astype(jnp.bfloat16)
    padded_grad = extended(grad_two.reshape(1, rows, cols, inner), (("row", 1), ("col", 2)), 1)
    flipped = group_weight[::-1, ::-1].reshape(3, 3, group_ch, groups, group_ch)
    flipped = jnp.transpose(flipped, (0, 1, 4, 3, 2)).reshape(3, 3, group_ch, inner)
    back_one = group_conv(padded_grad, flipped)
    tap_terms = []
    for tap_h in range(3):
        for tap_w in range(3):
            window = padded_act[0, tap_h : tap_h + rows, tap_w : tap_w + cols, :].reshape(-1, inner)
            dense = lax.dot_general(
                window, grad_two, (((0,), (0,)), ((), ())), preferred_element_type=jnp.float32
            )
            blocks = dense.reshape(groups, group_ch, groups, group_ch)
            diag = jnp.diagonal(blocks, axis1=0, axis2=2)
            tap_terms.append(jnp.transpose(diag, (2, 1, 0)).reshape(inner, group_ch))
    gw_two_out = jnp.stack(tap_terms, axis=1).reshape(inner, 3, 3, group_ch)
    grad_one = (back_one.reshape(-1, inner) * dsilu(pre_one) * scale_one).astype(jnp.bfloat16)
    input_grad = (
        jnp.dot(grad_one, reduce_weight.T, preferred_element_type=jnp.float32) + back_three
    ).astype(jnp.bfloat16)
    gw_one = lax.dot_general(
        flat, grad_one, (((0,), (0,)), ((), ())), preferred_element_type=jnp.float32
    )
    summed = lax.psum((gw_one, gw_two_out, gw_three), ("row", "col"))
    shares = (
        lax.psum_scatter(summed[0], "dp", scatter_dimension=0, tiled=True),
        lax.psum_scatter(summed[1], "dp", scatter_dimension=0, tiled=True),
        lax.psum_scatter(summed[2], "dp", scatter_dimension=0, tiled=True),
    )
    total = rows * cols * lax.axis_size("dp") * lax.axis_size("row") * lax.axis_size("col")
    factor = 1.0 / jnp.sqrt(jnp.float32(total))
    return (
        input_grad.reshape(1, rows, cols, chans),
        shares[0] * factor,
        shares[1] * factor,
        shares[2] * factor,
    )


def solution(mesh):
    return jax.shard_map(
        body,
        mesh=mesh,
        in_specs=(
            P("dp", "row", "col", None),
            P(),
            P(),
            P(),
            P(),
            P(),
            P(),
            P(),
            P(),
            P(),
            P("dp", "row", "col", None),
        ),
        out_specs=(
            P("dp", "row", "col", None),
            P("dp", None),
            P("dp", None, None, None),
            P("dp", None),
        ),
        check_vma=False,
    )
```

profile of v0, /device:TPU:0, one launch (start us, length us, event | category | flops | bytes accessed | tf_op | source)
XLA Modules:
  0.0 1004.2 jit_solution(9380093568484053856)
XLA Ops:
  8.0 2.1 multiply_convert_fusion.3
  10.4 2.4 collective-permute-start
  18.2 3.5 collective-permute-start.2
  25.2 2.8 collective-permute-done.2
  28.0 4.7 collective-permute-done.3
  33.3 36.1 %copy.89 = bf16[1,10,130,32,4]{4,0,3,2,1:T(2,128)(2,1)} copy(bf16[1,10,130,32,4]{2,4,3,1,0:T(4,128)(2,1)S(1)} %concatenate.46) | data formatting | bytes 665600 | tf_op jit(solution)/shard_map/concatenate | solution.py:16
  69.5 234.4 %convolution_reduce_fusion.1 = f32[8,128,32,4]{3,2,1,0:T(8,128)} fusion(bf16[1,10,130,32,4]{4,0,3,2,1:T(2,128)(2,1)} %copy.89, bf16[3,3,4,32,4]{4,3,2,1,0:T(8,128)(2,1)S(1)} %shard_map.140), kind=kOutput, calls=%fused_computation.10 | convolution fusion | flops 9437184 | bytes 866304 | tf_op jit(solution)/shard_map/conv_general_dilated | solution.py:27
  303.9 14.9 %reshape.158 = f32[1024,128]{1,0:T(8,128)S(1)} reshape(f32[8,128,32,4]{3,2,1,0:T(8,128)} %convolution_reduce_fusion.1) | data formatting | bytes 1048576 | tf_op jit(solution)/shard_map/reshape | solution.py:64
  324.3 1.9 copy.104
  329.0 2.1 convolution_bitcast_fusion.6
  331.1 1.9 copy.110
  336.6 2.1 convolution_bitcast_fusion.5
  346.3 2.2 reshape.85
  348.5 3.2 copy.242
  351.6 2.3 gather_fusion.4
  366.5 3.2 collective-permute-start.4
  380.1 3.5 collective-permute-start.6
  386.7 4.0 collective-permute-done.6
  390.7 4.7 collective-permute-done.7
  396.1 36.1 %copy.96 = bf16[1,10,130,32,4]{4,0,3,2,1:T(2,128)(2,1)} copy(bf16[1,10,130,32,4]{2,4,3,1,0:T(4,128)(2,1)S(1)} %concatenate.49) | data formatting | bytes 665600 | tf_op jit(solution)/shard_map/concatenate | solution.py:16
  432.2 398.5 %convolution_reduce_fusion = f32[8,128,32,4]{3,2,1,0:T(8,128)} fusion(bf16[1,10,130,32,4]{4,0,3,2,1:T(2,128)(2,1)} %copy.96, bf16[3,3,4,32,4]{4,3,2,1,0:T(8,128)(2,1)S(1)} %copy-done.22), kind=kOutput, calls=%fused_computation.9 | convolution fusion | flops 9437184 | bytes 866304 | tf_op jit(solution)/shard_map/conv_general_dilated | solution.py:27
  830.7 14.9 %reshape.159 = f32[1024,128]{1,0:T(8,128)S(1)} reshape(f32[8,128,32,4]{3,2,1,0:T(8,128)} %convolution_reduce_fusion) | data formatting | bytes 1048576 | tf_op jit(solution)/shard_map/reshape | solution.py:96
  849.1 59.4 %psum.25 = f32[64,3,3,4]{0,3,2,1:T(4,128)S(1)} all-reduce(f32[64,3,3,4]{0,3,2,1:T(4,128)S(1)} %copy.175), channel_id=1, replica_groups=mesh['dp'=2,'row'=4,'col'=4] {'row','col'}, use_global_device_ids=true, to_apply=%region_2.3 | all-reduce | flops 2304 | bytes 18432 | tf_op jit(solution)/shard_map/psum | solution.py:103
  909.1 85.1 %all-reduce.3.cloned.1.call-done = (f32[128,128]{0,1:T(8,128)}, f32[64,256]{1,0:T(8,128)}) async-done(((f32[128,128]{0,1:T(8,128)}, f32[64,256]{1,0:T(8,128)}), (f32[128,128]{0,1:T(8,128)}, f32[64,256]{1,0:T(8,128)})) %all-reduce.3.cloned.1.call-update) | async-done | bytes 131088 | tf_op jit(solution)/shard_map/psum | solution.py:103
  (194 shorter events, 63.3 us)
Async XLA Ops:
  7.2 840.7 %reduce-scatter.10.cloned.1.call-start = ((), (), s32[]{:S(2)}) async-start(), calls=%async_computation.5 | async-start | bytes 98304
  10.3 22.4 %copy-start.2 = (bf16[1,8,128,128]{2,3,1,0:T(8,128)(2,1)}, bf16[1,8,128,128]{2,3,1,0:T(8,128)(2,1)S(1)}, u32[]{:S(2)}) copy-start(bf16[1,8,128,128]{2,3,1,0:T(8,128)(2,1)S(1)} %copy.86) | copy-start | bytes 786436
  10.4 6.2 collective-permute-start
  12.7 5.2 collective-permute-start.1
  16.5 16.2 %copy-start.13 = (bf16[1,1,128,128]{2,3,1,0:T(8,128)(2,1)}, bf16[1,1,128,128]{2,3,1,0:T(8,128)(2,1)S(1)}, u32[]{:S(2)}) copy-start(bf16[1,1,128,128]{2,3,1,0:T(8,128)(2,1)S(1)} %collective-permute-done) | copy-start | bytes 98308
  18.2 9.8 collective-permute-start.2
  21.7 11.0 %collective-permute-start.3 = (bf16[1,10,1,128]{2,3,1,0:T(8,128)(2,1)S(1)}, bf16[1,10,1,128]{2,3,1,0:T(8,128)(2,1)S(1)}, u32[]{:S(2)}, u32[]{:S(2)}) collective-permute-start(bf16[1,10,1,128]{2,3,1,0:T(8,128)(2,1)S(1)} %get-tuple-element.29), channel_id=1, source_target_pairs={{1,0},{2,1},{3,2},{5,4},{6,5},{7,6},{9,8},{10,9},{11,10},{13,12},{... | collective-permute-start | bytes 7688 | tf_op jit(solution)/shard_map/ppermute | solution.py:15
  28.0 41.5 %copy-start.6 = (bf16[1,10,1,128]{2,3,1,0:T(8,128)(2,1)}, bf16[1,10,1,128]{2,3,1,0:T(8,128)(2,1)S(1)}, u32[]{:S(2)}) copy-start(bf16[1,10,1,128]{2,3,1,0:T(8,128)(2,1)S(1)} %collective-permute-done.2) | copy-start | bytes 7684
  32.7 36.7 %copy-start.8 = (bf16[1,10,1,128]{2,3,1,0:T(8,128)(2,1)}, bf16[1,10,1,128]{2,3,1,0:T(8,128)(2,1)S(1)}, u32[]{:S(2)}) copy-start(bf16[1,10,1,128]{2,3,1,0:T(8,128)(2,1)S(1)} %collective-permute-done.3) | copy-start | bytes 7684
  303.9 14.9 %copy-start.30 = (f32[256]{0:T(256)S(1)}, f32[256]{0:T(256)}, u32[]{:S(2)}) copy-start(f32[256]{0:T(256)} %param.20) | copy-start | bytes 3076
  303.9 15.0 %copy-start.31 = (f32[256]{0:T(256)S(1)}, f32[256]{0:T(256)}, u32[]{:S(2)}) copy-start(f32[256]{0:T(256)} %param.19) | copy-start | bytes 3076
  303.9 15.0 %copy-start.32 = (f32[128]{0:T(128)S(1)}, f32[128]{0:T(128)}, u32[]{:S(2)}) copy-start(f32[128]{0:T(128)} %param.17) | copy-start | bytes 1540
  303.9 15.0 %copy-start.33 = (f32[128]{0:T(128)S(1)}, f32[128]{0:T(128)}, u32[]{:S(2)}) copy-start(f32[128]{0:T(128)} %param.16) | copy-start | bytes 1540
  365.5 19.3 %copy-start.11 = (f32[1024,256]{1,0:T(8,128)S(1)}, f32[1024,256]{1,0:T(8,128)}, u32[]{:S(2)}) copy-start(f32[1024,256]{1,0:T(8,128)} %copy-done.10) | copy-start | bytes 3145732
  366.2 18.7 %copy-start.19 = (f32[1024,128]{1,0:T(8,128)S(1)}, f32[1024,128]{1,0:T(8,128)}, u32[]{:S(2)}) copy-start(f32[1024,128]{1,0:T(8,128)} %copy-done.18) | copy-start | bytes 1572868
  366.5 13.3 %collective-permute-start.4 = (bf16[1,1,128,128]{2,3,1,0:T(8,128)(2,1)S(1)}, bf16[1,1,128,128]{2,3,1,0:T(8,128)(2,1)S(1)}, u32[]{:S(2)}, u32[]{:S(2)}) collective-permute-start(bf16[1,1,128,128]{2,3,1,0:T(8,128)(2,1)S(1)} %get-tuple-element.32), channel_id=1, source_target_pairs={{0,4},{4,8},{8,12},{1,5},{5,9},{9,13},{2,6},{6,10},{10,14},{3,7},{... | collective-permute-start | bytes 98312 | tf_op jit(solution)/shard_map/ppermute | solution.py:12
  369.7 10.1 %collective-permute-start.5 = (bf16[1,1,128,128]{2,3,1,0:T(8,128)(2,1)S(1)}, bf16[1,1,128,128]{2,3,1,0:T(8,128)(2,1)S(1)}, u32[]{:S(2)}, u32[]{:S(2)}) collective-permute-start(bf16[1,1,128,128]{2,3,1,0:T(8,128)(2,1)S(1)} %get-tuple-element.33), channel_id=1, source_target_pairs={{4,0},{8,4},{12,8},{5,1},{9,5},{13,9},{6,2},{10,6},{14,10},{7,3},{... | collective-permute-start | bytes 98312 | tf_op jit(solution)/shard_map/ppermute | solution.py:15
  379.8 528.6 %reduce-scatter.8.cloned.1.call-start = ((), (), s32[]{:S(2)}) async-start(), calls=%async_computation.4 | async-start | bytes 196608 | tf_op jit(solution)/shard_map/reduce_scatter | solution.py:107
  380.1 10.6 %collective-permute-start.6 = (bf16[1,10,1,128]{2,3,1,0:T(8,128)(2,1)S(1)}, bf16[1,10,1,128]{2,3,1,0:T(8,128)(2,1)S(1)}, u32[]{:S(2)}, u32[]{:S(2)}) collective-permute-start(bf16[1,10,1,128]{2,3,1,0:T(8,128)(2,1)S(1)} %get-tuple-element.26), channel_id=1, source_target_pairs={{0,1},{1,2},{2,3},{4,5},{5,6},{6,7},{8,9},{9,10},{10,11},{12,13},{... | collective-permute-start | bytes 7688 | tf_op jit(solution)/shard_map/ppermute | solution.py:12
  383.6 11.9 %collective-permute-start.7 = (bf16[1,10,1,128]{2,3,1,0:T(8,128)(2,1)S(1)}, bf16[1,10,1,128]{2,3,1,0:T(8,128)(2,1)S(1)}, u32[]{:S(2)}, u32[]{:S(2)}) collective-permute-start(bf16[1,10,1,128]{2,3,1,0:T(8,128)(2,1)S(1)} %get-tuple-element.27), channel_id=1, source_target_pairs={{1,0},{2,1},{3,2},{5,4},{6,5},{7,6},{9,8},{10,9},{11,10},{13,12},{... | collective-permute-start | bytes 7688 | tf_op jit(solution)/shard_map/ppermute | solution.py:15
  386.7 521.8 %reduce-scatter.6.cloned.1.call-start = ((), (), s32[]{:S(2)}) async-start(), calls=%async_computation.3 | async-start | bytes 196608 | tf_op jit(solution)/shard_map/reduce_scatter | solution.py:105
  396.1 36.1 %copy-start.22 = (bf16[3,3,4,32,4]{4,3,2,1,0:T(8,128)(2,1)S(1)}, bf16[3,3,4,32,4]{4,3,2,1,0:T(8,128)(2,1)}, u32[]{:S(2)}) copy-start(bf16[3,3,4,32,4]{4,3,2,1,0:T(8,128)(2,1)} %reshape.82) | copy-start | bytes 27652
  830.7 15.1 %copy-start.21 = (bf16[1,8,128,256]{3,2,1,0:T(8,128)(2,1)S(1)}, bf16[1,8,128,256]{3,2,1,0:T(8,128)(2,1)}, u32[]{:S(2)}) copy-start(bf16[1,8,128,256]{3,2,1,0:T(8,128)(2,1)} %param.11) | copy-start | bytes 1572868
  846.8 147.4 %all-reduce.3.cloned.1.call-start = ((), (), s32[]{:S(2)}) async-start(), calls=%async_computation.6 | async-start | bytes 262144 | tf_op jit(solution)/shard_map/psum | solution.py:103
  (22 other events, 138.0 us)
Sparse Core Ops, SparseCore 0:
  379.9 12.1 reduce-scatter.9
  394.3 10.2 reduce-scatter.7
  846.9 9.6 reduce-scatter.5
  908.6 85.5 all-reduce.2
where the time goes:
time: 1010 us; the launch traced here: 1000 us
  matrix products  648 us (64%)
  local copies, waits for them, and re-layouts  156 us (15%)
  waiting for transfers between devices  103 us (10%)
  blocking collectives  59.4 us (6%)
  starting transfers between devices  17.8 us (2%)
  between operations  15.1 us (1%)
    conv_general_dilated x2, matrix products, group_conv(): lax.conv_general_dilated(inputs, kernel, (1, 1), ((0, 0), (0, 0)), dimens...  633 us
    psum x1, waiting for transfers between devices, body(): summed = lax.psum((gw_one, gw_two_out, gw_three), ('row', 'col'))  85.1 us
    concatenate x4, local copies, waits for them, and re-layouts, extended(): block = jnp.concatenate([low, block, high], axis=dim)  72.6 us
    psum x1, blocking collectives, body(): summed = lax.psum((gw_one, gw_two_out, gw_three), ('row', 'col'))  59.4 us
  transfers between devices with their start and end apart: 12, of which 6 were waited for; matrix products, arithmetic and copies ran while one was open for 47% of the time, Pallas kernels for 0%

commit v1 on v0

v1 whole, which is shorter than its diff:
```python
import functools

import jax
import jax.numpy as jnp
from jax import lax
from jax.experimental import pallas as pl
from jax.experimental.pallas import tpu as pltpu
from jax.sharding import PartitionSpec as P

BF = jnp.bfloat16
F32 = jnp.float32
SIDE = 8
GROUP_ROWS = 40


def pairings(count):
    out = []
    for start in (0, 1):
        perm = []
        for i in range(count):
            other = ((i - start) ^ 1) + start
            perm.append((i, other if i >= start and other < count else i))
        out.append(perm)
    return out


def swap_edges(pick, axis):
    even, odd = pairings(lax.axis_size(axis))
    is_odd = lax.axis_index(axis) % 2
    got_even = lax.ppermute(pick(is_odd == 0), axis, even)
    got_odd = lax.ppermute(pick(is_odd == 1), axis, odd)
    return got_even, got_odd


def dot(a, b):
    return jnp.dot(a, b, preferred_element_type=F32)


def gate(v):
    return 0.5 + 0.5 * jnp.tanh(0.5 * v)


def unit_kernel(
    pos, x_ref, c_ref, row_even, row_odd, col_even, col_odd, w1_ref, s1_ref, b1_ref, gw_ref, s2_ref, b2_ref,
    w3_ref, s3_ref, b3_ref, out_ref, share_ref, xs, cs, acts, gcat, d1, back, act2, g3, w2, w2t,
    *, rows, cols, chans, inner, group_ch,
):
    wide = cols + 2 * SIDE
    row_odd_p, col_odd_p = pos[0], pos[1]
    has_low_row, has_high_row, has_low_col, has_high_col = (pos[i].astype(F32) for i in range(2, 6))
    sub = lax.broadcasted_iota(jnp.int32, (inner, inner), 0)
    lane = lax.broadcasted_iota(jnp.int32, (inner, inner), 1)
    diag = jnp.where(sub // group_ch == lane // group_ch, 1.0, 0.0).astype(F32)
    for t in range(9):
        four = gw_ref[t * group_ch : (t + 1) * group_ch, :]
        eight = jnp.concatenate([four, four], axis=0)
        tiled = jnp.broadcast_to(eight[None], (inner // 8, 8, inner)).reshape(inner, inner)
        dense = tiled * diag
        w2[t * inner : (t + 1) * inner, :] = dense.astype(BF)
        w2t[(8 - t) * inner : (9 - t) * inner, :] = dense.T.astype(BF)
    def row_halo(i, low):
        a, b = row_even[i].astype(F32), row_odd[i].astype(F32)
        take_odd = (row_odd_p == 0) if low else (row_odd_p == 1)
        return jnp.where(take_odd, b, a).astype(BF)

    def col_halo(i):
        a, b = col_even[i].astype(F32), col_odd[i].astype(F32)
        odd = col_odd_p == 1
        return jnp.concatenate([jnp.where(odd, b, a), jnp.where(odd, a, b)], axis=0).astype(BF)

    for r in range(rows + 4):
        if r < 2:
            main = row_halo(r, True)
        elif r < rows + 2:
            main = x_ref[r - 2]
        else:
            main = row_halo(r - rows - 2, False)
        xs[r, 0:cols, :] = main
        xs[r, cols:wide, :] = col_halo(r)
    for r in range(rows + 2):
        if r < 1:
            main = row_halo(2, True)
        elif r < rows + 1:
            main = c_ref[r - 1]
        else:
            main = row_halo(2, False)
        cs[r, 0:cols, :] = main
        cs[r, cols:wide, :] = col_halo(rows + 4 + r)
    spot = lax.broadcasted_iota(jnp.int32, (wide, inner), 0)
    col_ok = jnp.where(spot < cols, 1.0, jnp.where(spot < cols + SIDE, has_high_col, has_low_col))

    def spread(ref, r, v):
        ref[r, :, 0:inner] = pltpu.roll(v, 1, 0).astype(BF)
        ref[r, :, inner : 2 * inner] = v.astype(BF)
        ref[r, :, 2 * inner :] = pltpu.roll(v, wide - 1, 0).astype(BF)

    s1, b1, w1 = s1_ref[...], b1_ref[...], w1_ref[...]
    step = 2
    for r0 in range(0, rows + 4, step):
        pre = dot(xs[r0 : r0 + step].reshape(step * wide, chans), w1) * s1 + b1
        sg = gate(pre)
        act = pre * sg
        for k in range(step):
            r = r0 + k
            a = act[k * wide : (k + 1) * wide] * col_ok
            if r < 2:
                a = a * has_low_row
            if r >= rows + 2:
                a = a * has_high_row
            spread(acts, r, a)
            if 2 <= r < rows + 2:
                at = slice(k * wide, k * wide + cols)
                d1[(r - 2) * cols : (r - 1) * cols, :] = (sg[at] + act[at] * (1.0 - sg[at])) * s1
    s2, b2, w3, s3, b3 = s2_ref[...], b2_ref[...], w3_ref[...], s3_ref[...], b3_ref[...]
    w3t = w3.T
    for q0 in range(0, rows + 2, step):
        conv = jnp.zeros((step * wide, inner), F32)
        for dh in range(3):
            conv = conv + dot(
                acts[q0 + dh : q0 + dh + step].reshape(step * wide, 3 * inner),
                w2[dh * 3 * inner : (dh + 1) * 3 * inner, :],
            )
        pre2 = conv * s2 + b2
        sg2 = gate(pre2)
        silu2 = pre2 * sg2
        a2 = silu2.astype(BF)
        dd2 = (sg2 + silu2 * (1.0 - sg2)) * s2
        skip = xs[q0 + 1 : q0 + 1 + step].reshape(step * wide, chans).astype(F32)
        pre3 = dot(a2, w3) * s3 + b3 + skip
        sg3 = gate(pre3)
        ct = cs[q0 : q0 + step].reshape(step * wide, chans).astype(F32)
        back3 = ct * (sg3 + pre3 * sg3 * (1.0 - sg3))
        grad3 = (back3 * s3).astype(BF)
        grad2 = dot(grad3, w3t) * dd2
        for k in range(step):
            q = q0 + k
            g = grad2[k * wide : (k + 1) * wide] * col_ok
            if q < 1:
                g = g * has_low_row
            if q >= rows + 1:
                g = g * has_high_row
            spread(gcat, q, g)
            if 1 <= q < rows + 1:
                at = slice(k * wide, k * wide + cols)
                to = slice((q - 1) * cols, q * cols)
                back[to, :] = back3[at]
                act2[to, :] = a2[at]
                g3[to, :] = grad3[at]
    n_dp = share_ref.shape[0]
    gw3 = dot(act2[...].T, g3[...])
    own_g = gcat[1 : rows + 1, 0:cols, inner : 2 * inner].reshape(rows * cols, inner)
    own_gt = own_g.T
    pick_sub = lax.broadcasted_iota(jnp.int32, (3 * inner, inner), 0)
    pick_lane = lax.broadcasted_iota(jnp.int32, (3 * inner, inner), 1)
    compact = jnp.zeros((inner, inner), F32)
    diag3 = jnp.concatenate([diag, diag, diag], axis=1)
    for dh in range(3):
        near = acts[dh + 1 : dh + 1 + rows, 0:cols, :].reshape(rows * cols, 3 * inner)
        full = (dot(own_gt, near) * diag3).astype(BF)
        place = (dh * 3 + pick_sub // inner) * group_ch + pick_sub % group_ch
        compact = compact + dot(full, jnp.where(pick_lane == place, 1.0, 0.0).astype(BF))
    gw2 = compact.T[0:GROUP_ROWS]
    w1t = w1.T
    gw1t = jnp.zeros((inner, chans), F32)
    for p0 in range(0, rows, step):
        conv = jnp.zeros((step * cols, inner), F32)
        for dh in range(3):
            conv = conv + dot(
                gcat[p0 + dh : p0 + dh + step, 0:cols, :].reshape(step * cols, 3 * inner),
                w2t[dh * 3 * inner : (dh + 1) * 3 * inner, :],
            )
        at = slice(p0 * cols, (p0 + step) * cols)
        g1 = (conv * d1[at, :]).astype(BF)
        gw1t = gw1t + dot(g1.T, x_ref[p0 : p0 + step].reshape(step * cols, chans))
        out = dot(g1, w1t) + back[at, :]
        out_ref[p0 : p0 + step] = out.astype(BF).reshape(step, cols, chans)
    gw1 = gw1t.T
    one, three = chans // n_dp, inner // n_dp
    for h in range(n_dp):
        share_ref[h, 0:one, :] = gw1[h * one : (h + 1) * one].astype(BF)
        for k in range(chans // inner):
            share_ref[h, one + k * three : one + (k + 1) * three, :] = gw3[
                h * three : (h + 1) * three, k * inner : (k + 1) * inner
            ].astype(BF)
        base = one + three * (chans // inner)
        share_ref[h, base : base + GROUP_ROWS, :] = gw2.astype(BF)


def swap_sum(value, axis, bit):
    count = lax.axis_size(axis)
    other = lax.ppermute(value, axis, [(i, i ^ bit) for i in range(count)])
    return (value.astype(F32) + other.astype(F32)).astype(value.dtype)


def body(
    features, reduce_weight, scale_one, shift_one, group_weight, scale_two, shift_two, expand_weight, scale_three,
    shift_three, cotangent,
):
    _, rows, cols, chans = features.shape
    inner = reduce_weight.shape[1]
    group_ch = group_weight.shape[2]
    x, c = features[0], cotangent[0]
    n_dp, n_row, n_col = (lax.axis_size(a) for a in ("dp", "row", "col"))
    dp, row, col = (lax.axis_index(a) for a in ("dp", "row", "col"))

    def row_edge(high):
        edge = lax.dynamic_slice_in_dim(x, jnp.where(high, rows - 2, 0), 2, axis=0)
        cot = lax.dynamic_slice_in_dim(c, jnp.where(high, rows - 1, 0), 1, axis=0)
        return jnp.concatenate([edge, cot], axis=0)

    row_even, row_odd = swap_edges(row_edge, "row")

    def col_edge(high):
        def cut(v):
            return lax.dynamic_slice_in_dim(v, jnp.where(high, cols - SIDE, 0), SIDE, axis=1)

        even, odd = cut(row_even), cut(row_odd)
        low = jnp.where(row % 2 == 0, odd, even)
        top = jnp.where(row % 2 == 0, even, odd)
        return jnp.concatenate([low[0:2], cut(x), top[0:2], low[2:3], cut(c), top[2:3]], axis=0)

    col_even, col_odd = swap_edges(col_edge, "col")
    pos = jnp.stack([row % 2, col % 2, row > 0, row < n_row - 1, col > 0, col < n_col - 1]).astype(jnp.int32)
    wide = cols + 2 * SIDE
    share_rows = chans // n_dp + (inner // n_dp) * (chans // inner) + GROUP_ROWS
    vmem = pl.BlockSpec(memory_space=pltpu.VMEM)
    input_grad, shares = pl.pallas_call(
        functools.partial(unit_kernel, rows=rows, cols=cols, chans=chans, inner=inner, group_ch=group_ch),
        out_shape=(
            jax.ShapeDtypeStruct((rows, cols, chans), BF),
            jax.ShapeDtypeStruct((n_dp, share_rows, inner), BF),
        ),
        in_specs=[pl.BlockSpec(memory_space=pltpu.SMEM)] + [vmem] * 15,
        out_specs=(vmem, vmem),
        scratch_shapes=[
            pltpu.VMEM((rows + 4, wide, chans), BF),
            pltpu.VMEM((rows + 2, wide, chans), BF),
            pltpu.VMEM((rows + 4, wide, 3 * inner), BF),
            pltpu.VMEM((rows + 2, wide, 3 * inner), BF),
            pltpu.VMEM((rows * cols, inner), F32),
            pltpu.VMEM((rows * cols, chans), F32),
            pltpu.VMEM((rows * cols, inner), BF),
            pltpu.VMEM((rows * cols, chans), BF),
            pltpu.VMEM((9 * inner, inner), BF),
            pltpu.VMEM((9 * inner, inner), BF),
        ],
        compiler_params=pltpu.CompilerParams(vmem_limit_bytes=40 << 20),
        name="unit",
    )(
        pos, x, c, row_even, row_odd, col_even, col_odd, reduce_weight, scale_one[None], shift_one[None],
        group_weight.astype(F32).reshape(9 * group_ch, inner), scale_two[None], shift_two[None], expand_weight,
        scale_three[None], shift_three[None],
    )
    held = n_dp
    while held > 1:
        half = held // 2
        bit = (dp // half) % 2
        mine = lax.dynamic_slice_in_dim(shares, bit * half, half, axis=0)
        theirs = lax.dynamic_slice_in_dim(shares, (1 - bit) * half, half, axis=0)
        other = lax.ppermute(theirs, "dp", [(i, i ^ half) for i in range(n_dp)])
        shares = (mine.astype(F32) + other.astype(F32)).astype(BF)
        held = half
    total = shares[0]
    steps = [(a, 1 << k) for a, n in (("row", n_row), ("col", n_col)) for k in range(n.bit_length() - 1)]
    for axis, bit in steps[:-1]:
        total = swap_sum(total, axis, bit)
    axis, bit = steps[-1]
    other = lax.ppermute(total, axis, [(i, i ^ bit) for i in range(lax.axis_size(axis))])
    pixels = rows * cols * n_dp * n_row * n_col
    total = (total.astype(F32) + other.astype(F32)) * (1.0 / jnp.sqrt(F32(pixels)))
    one, three = chans // n_dp, inner // n_dp
    base = one + three * (chans // inner)
    expand_grad = jnp.concatenate(
        [total[one + k * three : one + (k + 1) * three] for k in range(chans // inner)], axis=1
    )
    group = lax.dynamic_slice_in_dim(total[base : base + 9 * group_ch], dp * three, three, axis=1)
    group_grad = jnp.transpose(group.reshape(3, 3, group_ch, three), (3, 0, 1, 2))
    return input_grad[None], total[0:one], group_grad, expand_grad


def solution(mesh):
    image = P("dp", "row", "col", None)
    return jax.shard_map(
        body,
        mesh=mesh,
        in_specs=(image,) + (P(),) * 9 + (image,),
        out_specs=(image, P("dp", None), P("dp", None, None, None), P("dp", None)),
        check_vma=False,
    )
```

time: 1010 us -> 47.6 us (0.05)
  matrix products: 648 us -> 0 us
  local copies, waits for them, and re-layouts: 156 us -> 2.71 us
  waiting for transfers between devices: 103 us -> 16.6 us
  blocking collectives: 59.4 us -> 0 us
  between operations: 15.1 us -> 0.96 us
    conv_general_dilated x2 -> x0, matrix products: 633 us -> none  [group_conv(): lax.conv_general_dilated(inputs, kernel, (1, 1), ((0, 0), (0, 0)), dimens...]
    psum x1 -> x0, waiting for transfers between devices: 85.1 us -> none  [body(): summed = lax.psum((gw_one, gw_two_out, gw_three), ('row', 'col'))]
    concatenate x4 -> x2, local copies, waits for them, and re-layouts: 72.6 us -> 0.01 us  [col_edge(): jnp.concatenate([low[0:2], cut(x), top[0:2], low[2:3], cut(c), top[2:3]],...]
    psum x1 -> x0, blocking collectives: 59.4 us -> none  [body(): summed = lax.psum((gw_one, gw_two_out, gw_three), ('row', 'col'))]
    reshape x7 -> x2, local copies, waits for them, and re-layouts: 36.7 us -> 0.63 us  [the longest x1 0.62 us: body(): group.reshape(3, 3, group_ch, three)]
    dot_general x15 -> x0, matrix products: 15.3 us -> none  [the longest x9 8.38 us: body(): lax.dot_general(window, grad_two, (((0,), (0,)), ((), ())), preferred_ele...]
    transpose x17 -> x0, local copies, waits for them, and re-layouts: 13.6 us -> none  [the longest x8 11 us: body(): diag = jnp.diagonal(blocks, axis1=0, axis2=2)]
    unnamed x87 -> x29, local copies, waits for them, and re-layouts: 12.6 us -> 0.2 us
  transfers between devices with their start and end apart: 12 -> 9, of which waited for: 6 -> 7; matrix products, arithmetic and copies ran while one was open for 47% -> 0% of each run, Pallas kernels for 0% -> 0%
where the time goes in v1:
time: 47.6 us; the launch traced here: 47.4 us
  starting transfers between devices  19.3 us (41%)
  waiting for transfers between devices  16.6 us (35%)
  Pallas kernels  7.06 us (15%)
  local copies, waits for them, and re-layouts  2.71 us (6%)
  between operations  0.96 us (2%)
  other arithmetic  0.81 us (2%)
    ppermute x2, starting transfers between devices, swap_edges(): got_even = lax.ppermute(pick(is_odd == 0), axis, even)  8.81 us
    pallas_call x1, Pallas kernels, body(): pl.pallas_call(functools.partial(unit_kernel, rows=rows, cols=cols, chans...  7.06 us
    ppermute x3, waiting for transfers between devices, swap_sum(): other = lax.ppermute(value, axis, [(i, i ^ bit) for i in range(count)])  6.14 us
    ppermute x3, starting transfers between devices, swap_sum(): other = lax.ppermute(value, axis, [(i, i ^ bit) for i in range(count)])  5.37 us
    ppermute x1, waiting for transfers between devices, body(): other = lax.ppermute(theirs, 'dp', [(i, i ^ half) for i in range(n_dp)])  3.62 us
    ppermute x2, waiting for transfers between devices, swap_edges(): got_even = lax.ppermute(pick(is_odd == 0), axis, even)  3.46 us
    ppermute x1, waiting for transfers between devices, body(): lax.ppermute(total, axis, [(i, i ^ bit) for i in range(lax.axis_size(axis...  3.37 us
    ppermute x1, starting transfers between devices, body(): lax.ppermute(total, axis, [(i, i ^ bit) for i in range(lax.axis_size(axis...  1.97 us
  transfers between devices with their start and end apart: 9, of which 7 were waited for; matrix products, arithmetic and copies ran while one was open for 0% of the time, Pallas kernels for 0%

profile of v1, /device:TPU:0, one launch (start us, length us, event | category | flops | bytes accessed | tf_op | source)
XLA Modules:
  0.0 47.4 jit_solution(12070886909811536331)
XLA Ops:
  0.7 1.0 %dynamic-slice_bitcast_fusion = (bf16[2,128,256]{2,1,0:T(8,128)(2,1)S(1)}, bf16[2,128,256]{2,1,0:T(8,128)(2,1)S(1)}) fusion(bf16[1,8,128,256]{3,2,1,0:T(8,128)(2,1)} %param.11, s32[]{:T(128)S(6)} %select_n.99, s32[]{:T(128)S(6)} %select_n.97), kind=kLoop, calls=%fused_computation.7 | loop fusion | bytes 524296 | tf_op jit(solution)/shard_map/dynamic_slice | solution.py:207
  1.7 0.1 copy-done.1
  1.9 0.8 %collective-permute-start.1 = (bf16[3,128,256]{2,1,0:T(8,128)(2,1)S(1)}, bf16[3,128,256]{2,1,0:T(8,128)(2,1)S(1)}, u32[]{:S(2)}, u32[]{:S(2)}) collective-permute-start(bf16[3,128,256]{2,1,0:T(8,128)(2,1)S(1)} %pad_maximum_fusion.1), channel_id=1, source_target_pairs={{0,0},{4,8},{8,4},{12,12},{1,1},{5,9},{9,5},{13,13},{2,2},{6,10},{... | collective-permute-start | bytes 589832 | tf_op jit(solution)/shard_map/ppermute | solution.py:31
  2.7 4.4 %collective-permute-start = (bf16[3,128,256]{2,1,0:T(8,128)(2,1)S(1)}, bf16[3,128,256]{2,1,0:T(8,128)(2,1)S(1)}, u32[]{:S(2)}, u32[]{:S(2)}) collective-permute-start(bf16[3,128,256]{2,1,0:T(8,128)(2,1)S(1)} %pad_maximum_fusion), channel_id=1, source_target_pairs={{0,4},{4,0},{8,12},{12,8},{1,5},{5,1},{9,13},{13,9},{2,6},{6,2},{1... | collective-permute-start | bytes 589832 | tf_op jit(solution)/shard_map/ppermute | solution.py:30
  7.1 1.1 %collective-permute-done.row_even = bf16[3,128,256]{2,1,0:T(8,128)(2,1)S(1)} collective-permute-done((bf16[3,128,256]{2,1,0:T(8,128)(2,1)S(1)}, bf16[3,128,256]{2,1,0:T(8,128)(2,1)S(1)}, u32[]{:S(2)}, u32[]{:S(2)}) %collective-permute-start) | collective-permute-done | bytes 196640 | tf_op jit(solution)/shard_map/ppermute | solution.py:30
  8.4 0.8 %collective-permute-start.3 = (bf16[22,8,256]{2,1,0:T(8,128)(2,1)S(1)}, bf16[22,8,256]{2,1,0:T(8,128)(2,1)S(1)}, u32[]{:S(2)}, u32[]{:S(2)}) collective-permute-start(bf16[22,8,256]{2,1,0:T(8,128)(2,1)S(1)} %constant_dynamic-update-slice_fusion.4), channel_id=1, source_target_pairs={{0,0},{1,2},{2,1},{3,3},{4,4},{5,6},{6,5},{7,7},{8,8},{9,10},{10,9... | collective-permute-start | bytes 270344 | tf_op jit(solution)/shard_map/ppermute | solution.py:31
  9.2 4.5 %collective-permute-start.2 = (bf16[22,8,256]{2,1,0:T(8,128)(2,1)S(1)}, bf16[22,8,256]{2,1,0:T(8,128)(2,1)S(1)}, u32[]{:S(2)}, u32[]{:S(2)}) collective-permute-start(bf16[22,8,256]{2,1,0:T(8,128)(2,1)S(1)} %constant_dynamic-update-slice_fusion), channel_id=1, source_target_pairs={{0,1},{1,0},{2,3},{3,2},{4,5},{5,4},{6,7},{7,6},{8,9},{9,8},{10,11... | collective-permute-start | bytes 270344 | tf_op jit(solution)/shard_map/ppermute | solution.py:30
  13.7 0.1 stack.43.pos
  13.8 2.4 %collective-permute-done.2.col_even = bf16[22,8,256]{2,1,0:T(8,128)(2,1)S(1)} collective-permute-done((bf16[22,8,256]{2,1,0:T(8,128)(2,1)S(1)}, bf16[22,8,256]{2,1,0:T(8,128)(2,1)S(1)}, u32[]{:S(2)}, u32[]{:S(2)}) %collective-permute-start.2) | collective-permute-done | bytes 90144 | tf_op jit(solution)/shard_map/ppermute | solution.py:30
  16.2 7.1 %unit.1 = (bf16[8,128,256]{2,1,0:T(8,128)(2,1)}, bf16[2,296,128]{2,1,0:T(8,128)(2,1)S(1)}) custom-call(s32[6]{0:T(128)S(1)} %stack.43.pos, bf16[8,128,256]{2,1,0:T(8,128)(2,1)S(1)} %bitcast.34, bf16[8,128,256]{2,1,0:T(8,128)(2,1)S(1)} %bitcast.35, bf16[3,128,256]{2,1,0:T(8,128)(2,1)S(1)} %collective-permute-done.row_even, ...), custom_call_target="tpu_custom_call" | custom-call | tf_op jit(solution)/shard_map/unit/pallas_call | solution.py:227
  23.3 1.5 %collective-permute-start.4 = (bf16[1,296,128]{2,1,0:T(8,128)(2,1)S(1)}, bf16[1,296,128]{2,1,0:T(8,128)(2,1)S(1)}, u32[]{:S(2)}, u32[]{:S(2)}) collective-permute-start(bf16[1,296,128]{2,1,0:T(8,128)(2,1)S(1)} %constant_dynamic-slice_fusion.1), channel_id=1, source_target_pairs={{0,16},{16,0},{1,17},{17,1},{2,18},{18,2},{3,19},{19,3},{4,20},{20... | collective-permute-start | bytes 227336 | tf_op jit(solution)/shard_map/ppermute | solution.py:260
  24.8 3.6 %collective-permute-done.4 = bf16[1,296,128]{2,1,0:T(8,128)(2,1)S(1)} collective-permute-done((bf16[1,296,128]{2,1,0:T(8,128)(2,1)S(1)}, bf16[1,296,128]{2,1,0:T(8,128)(2,1)S(1)}, u32[]{:S(2)}, u32[]{:S(2)}) %collective-permute-start.4) | collective-permute-done | bytes 75808 | tf_op jit(solution)/shard_map/ppermute | solution.py:260
  28.4 0.2 collective-permute-start.5
  28.6 1.2 %collective-permute-done.5 = bf16[296,128]{1,0:T(8,128)(2,1)S(1)} collective-permute-done((bf16[296,128]{1,0:T(8,128)(2,1)S(1)}, bf16[296,128]{1,0:T(8,128)(2,1)S(1)}, u32[]{:S(2)}, u32[]{:S(2)}) %collective-permute-start.5) | collective-permute-done | bytes 75808 | tf_op jit(solution)/shard_map/ppermute | solution.py:191
  29.8 3.1 %collective-permute-start.6 = (bf16[296,128]{1,0:T(8,128)(2,1)S(1)}, bf16[296,128]{1,0:T(8,128)(2,1)S(1)}, u32[]{:S(2)}, u32[]{:S(2)}) collective-permute-start(bf16[296,128]{1,0:T(8,128)(2,1)S(1)} %add_convert_fusion.2), channel_id=1, source_target_pairs={{0,8},{4,12},{8,0},{12,4},{1,9},{5,13},{9,1},{13,5},{2,10},{6,14},... | collective-permute-start | bytes 227336 | tf_op jit(solution)/shard_map/ppermute | solution.py:191
  32.9 2.6 %collective-permute-done.6 = bf16[296,128]{1,0:T(8,128)(2,1)S(1)} collective-permute-done((bf16[296,128]{1,0:T(8,128)(2,1)S(1)}, bf16[296,128]{1,0:T(8,128)(2,1)S(1)}, u32[]{:S(2)}, u32[]{:S(2)}) %collective-permute-start.6) | collective-permute-done | bytes 75808 | tf_op jit(solution)/shard_map/ppermute | solution.py:191
  35.6 2.1 %collective-permute-start.7 = (bf16[296,128]{1,0:T(8,128)(2,1)S(1)}, bf16[296,128]{1,0:T(8,128)(2,1)S(1)}, u32[]{:S(2)}, u32[]{:S(2)}) collective-permute-start(bf16[296,128]{1,0:T(8,128)(2,1)S(1)} %add_convert_fusion.1), channel_id=1, source_target_pairs={{0,1},{1,0},{2,3},{3,2},{4,5},{5,4},{6,7},{7,6},{8,9},{9,8},{10,11... | collective-permute-start | bytes 227336 | tf_op jit(solution)/shard_map/ppermute | solution.py:191
  37.7 2.4 %collective-permute-done.7 = bf16[296,128]{1,0:T(8,128)(2,1)S(1)} collective-permute-done((bf16[296,128]{1,0:T(8,128)(2,1)S(1)}, bf16[296,128]{1,0:T(8,128)(2,1)S(1)}, u32[]{:S(2)}, u32[]{:S(2)}) %collective-permute-start.7) | collective-permute-done | bytes 75808 | tf_op jit(solution)/shard_map/ppermute | solution.py:191
  40.0 2.0 %collective-permute-start.8 = (bf16[296,128]{1,0:T(8,128)(2,1)S(1)}, bf16[296,128]{1,0:T(8,128)(2,1)S(1)}, u32[]{:S(2)}, u32[]{:S(2)}) collective-permute-start(bf16[296,128]{1,0:T(8,128)(2,1)S(1)} %add_convert_fusion), channel_id=1, source_target_pairs={{0,2},{1,3},{2,0},{3,1},{4,6},{5,7},{6,4},{7,5},{8,10},{9,11},{10,... | collective-permute-start | bytes 227336 | tf_op jit(solution)/shard_map/ppermute | solution.py:268
  42.0 3.4 %collective-permute-done.8 = bf16[296,128]{1,0:T(8,128)(2,1)S(1)} collective-permute-done((bf16[296,128]{1,0:T(8,128)(2,1)S(1)}, bf16[296,128]{1,0:T(8,128)(2,1)S(1)}, u32[]{:S(2)}, u32[]{:S(2)}) %collective-permute-start.8) | collective-permute-done | bytes 75808 | tf_op jit(solution)/shard_map/ppermute | solution.py:268
  45.4 0.6 %slice.56 = f32[128,128]{1,0:T(8,128)} slice(f32[296,128]{1,0:T(8,128)S(1)} %add_multiply_fusion), slice={[0:128], [0:128]} | slice | bytes 131072 | tf_op jit(solution)/shard_map/slice | solution.py:278
  46.1 0.1 constant_dynamic-slice_fusion
  46.1 0.6 %reshape.26 = f32[3,3,4,64]{3,2,1,0:T(4,128)} reshape(f32[36,64]{1,0:T(8,128)S(1)} %constant_dynamic-slice_fusion) | data formatting | bytes 18432 | tf_op jit(solution)/shard_map/reshape | solution.py:277
  46.8 0.6 %pad_maximum_fusion.2 = f32[64,256]{1,0:T(8,128)} fusion(f32[64,128]{1,0:T(8,128)S(1)} %get-tuple-element.21, f32[64,128]{1,0:T(8,128)S(1)} %get-tuple-element.20), kind=kLoop, calls=%fused_computation.10 | loop fusion | flops 16384 | bytes 131072 | tf_op jit(solution)/shard_map/concatenate | solution.py:273
  (45 shorter events, 0.3 us)
Async XLA Ops:
  0.6 1.2 %copy-start.1 = (bf16[1,8,128,256]{3,2,1,0:T(8,128)(2,1)S(1)}, bf16[1,8,128,256]{3,2,1,0:T(8,128)(2,1)}, u32[]{:S(2)}) copy-start(bf16[1,8,128,256]{3,2,1,0:T(8,128)(2,1)} %param.21) | copy-start | bytes 1572868
  1.8 6.3 %copy-start = (bf16[1,8,128,256]{3,2,1,0:T(8,128)(2,1)S(1)}, bf16[1,8,128,256]{3,2,1,0:T(8,128)(2,1)}, u32[]{:S(2)}) copy-start(bf16[1,8,128,256]{3,2,1,0:T(8,128)(2,1)} %param.11) | copy-start | bytes 1572868
  1.9 5.2 %collective-permute-start.1 = (bf16[3,128,256]{2,1,0:T(8,128)(2,1)S(1)}, bf16[3,128,256]{2,1,0:T(8,128)(2,1)S(1)}, u32[]{:S(2)}, u32[]{:S(2)}) collective-permute-start(bf16[3,128,256]{2,1,0:T(8,128)(2,1)S(1)} %pad_maximum_fusion.1), channel_id=1, source_target_pairs={{0,0},{4,8},{8,4},{12,12},{1,1},{5,9},{9,5},{13,13},{2,2},{6,10},{... | collective-permute-start | bytes 589832 | tf_op jit(solution)/shard_map/ppermute | solution.py:31
  2.7 5.4 %collective-permute-start = (bf16[3,128,256]{2,1,0:T(8,128)(2,1)S(1)}, bf16[3,128,256]{2,1,0:T(8,128)(2,1)S(1)}, u32[]{:S(2)}, u32[]{:S(2)}) collective-permute-start(bf16[3,128,256]{2,1,0:T(8,128)(2,1)S(1)} %pad_maximum_fusion), channel_id=1, source_target_pairs={{0,4},{4,0},{8,12},{12,8},{1,5},{5,1},{9,13},{13,9},{2,6},{6,2},{1... | collective-permute-start | bytes 589832 | tf_op jit(solution)/shard_map/ppermute | solution.py:30
  8.2 5.4 %copy-start.10 = (bf16[3,3,4,128]{3,2,1,0:T(4,128)(2,1)S(1)}, bf16[3,3,4,128]{3,2,1,0:T(4,128)(2,1)}, u32[]{:S(2)}) copy-start(bf16[3,3,4,128]{3,2,1,0:T(4,128)(2,1)} %param.15) | copy-start | bytes 27652
  8.2 7.9 %copy-start.4 = (f32[256]{0:T(256)S(1)}, f32[256]{0:T(256)}, u32[]{:S(2)}) copy-start(f32[256]{0:T(256)} %param.19) | copy-start | bytes 3076
  8.3 7.9 %copy-start.5 = (f32[256]{0:T(256)S(1)}, f32[256]{0:T(256)}, u32[]{:S(2)}) copy-start(f32[256]{0:T(256)} %param.20) | copy-start | bytes 3076
  8.3 7.9 %copy-start.6 = (f32[128]{0:T(128)S(1)}, f32[128]{0:T(128)}, u32[]{:S(2)}) copy-start(f32[128]{0:T(128)} %param.13) | copy-start | bytes 1540
  8.3 7.9 %copy-start.7 = (f32[128]{0:T(128)S(1)}, f32[128]{0:T(128)}, u32[]{:S(2)}) copy-start(f32[128]{0:T(128)} %param.14) | copy-start | bytes 1540
  8.3 7.9 %copy-start.8 = (f32[128]{0:T(128)S(1)}, f32[128]{0:T(128)}, u32[]{:S(2)}) copy-start(f32[128]{0:T(128)} %param.16) | copy-start | bytes 1540
  8.3 7.9 %copy-start.9 = (f32[128]{0:T(128)S(1)}, f32[128]{0:T(128)}, u32[]{:S(2)}) copy-start(f32[128]{0:T(128)} %param.17) | copy-start | bytes 1540
  8.3 7.9 %copy-start.2 = (bf16[256,128]{1,0:T(8,128)(2,1)S(1)}, bf16[256,128]{1,0:T(8,128)(2,1)}, u32[]{:S(2)}) copy-start(bf16[256,128]{1,0:T(8,128)(2,1)} %w1_ref.1) | copy-start | bytes 196612
  8.4 7.9 %copy-start.3 = (bf16[128,256]{1,0:T(8,128)(2,1)S(1)}, bf16[128,256]{1,0:T(8,128)(2,1)}, u32[]{:S(2)}) copy-start(bf16[128,256]{1,0:T(8,128)(2,1)} %w3_ref.1) | copy-start | bytes 196612
  8.4 5.4 %collective-permute-start.3 = (bf16[22,8,256]{2,1,0:T(8,128)(2,1)S(1)}, bf16[22,8,256]{2,1,0:T(8,128)(2,1)S(1)}, u32[]{:S(2)}, u32[]{:S(2)}) collective-permute-start(bf16[22,8,256]{2,1,0:T(8,128)(2,1)S(1)} %constant_dynamic-update-slice_fusion.4), channel_id=1, source_target_pairs={{0,0},{1,2},{2,1},{3,3},{4,4},{5,6},{6,5},{7,7},{8,8},{9,10},{10,9... | collective-permute-start | bytes 270344 | tf_op jit(solution)/shard_map/ppermute | solution.py:31
  9.2 7.0 %collective-permute-start.2 = (bf16[22,8,256]{2,1,0:T(8,128)(2,1)S(1)}, bf16[22,8,256]{2,1,0:T(8,128)(2,1)S(1)}, u32[]{:S(2)}, u32[]{:S(2)}) collective-permute-start(bf16[22,8,256]{2,1,0:T(8,128)(2,1)S(1)} %constant_dynamic-update-slice_fusion), channel_id=1, source_target_pairs={{0,1},{1,0},{2,3},{3,2},{4,5},{5,4},{6,7},{7,6},{8,9},{9,8},{10,11... | collective-permute-start | bytes 270344 | tf_op jit(solution)/shard_map/ppermute | solution.py:30
  23.3 5.1 %collective-permute-start.4 = (bf16[1,296,128]{2,1,0:T(8,128)(2,1)S(1)}, bf16[1,296,128]{2,1,0:T(8,128)(2,1)S(1)}, u32[]{:S(2)}, u32[]{:S(2)}) collective-permute-start(bf16[1,296,128]{2,1,0:T(8,128)(2,1)S(1)} %constant_dynamic-slice_fusion.1), channel_id=1, source_target_pairs={{0,16},{16,0},{1,17},{17,1},{2,18},{18,2},{3,19},{19,3},{4,20},{20... | collective-permute-start | bytes 227336 | tf_op jit(solution)/shard_map/ppermute | solution.py:260
  28.4 1.3 %collective-permute-start.5 = (bf16[296,128]{1,0:T(8,128)(2,1)S(1)}, bf16[296,128]{1,0:T(8,128)(2,1)S(1)}, u32[]{:S(2)}, u32[]{:S(2)}) collective-permute-start(bf16[296,128]{1,0:T(8,128)(2,1)S(1)} %fusion), channel_id=1, source_target_pairs={{0,4},{4,0},{8,12},{12,8},{1,5},{5,1},{9,13},{13,9},{2,6},{6,2},{1... | collective-permute-start | bytes 227336 | tf_op jit(solution)/shard_map/ppermute | solution.py:191
  29.8 5.7 %collective-permute-start.6 = (bf16[296,128]{1,0:T(8,128)(2,1)S(1)}, bf16[296,128]{1,0:T(8,128)(2,1)S(1)}, u32[]{:S(2)}, u32[]{:S(2)}) collective-permute-start(bf16[296,128]{1,0:T(8,128)(2,1)S(1)} %add_convert_fusion.2), channel_id=1, source_target_pairs={{0,8},{4,12},{8,0},{12,4},{1,9},{5,13},{9,1},{13,5},{2,10},{6,14},... | collective-permute-start | bytes 227336 | tf_op jit(solution)/shard_map/ppermute | solution.py:191
  35.6 4.4 %collective-permute-start.7 = (bf16[296,128]{1,0:T(8,128)(2,1)S(1)}, bf16[296,128]{1,0:T(8,128)(2,1)S(1)}, u32[]{:S(2)}, u32[]{:S(2)}) collective-permute-start(bf16[296,128]{1,0:T(8,128)(2,1)S(1)} %add_convert_fusion.1), channel_id=1, source_target_pairs={{0,1},{1,0},{2,3},{3,2},{4,5},{5,4},{6,7},{7,6},{8,9},{9,8},{10,11... | collective-permute-start | bytes 227336 | tf_op jit(solution)/shard_map/ppermute | solution.py:191
  40.0 5.3 %collective-permute-start.8 = (bf16[296,128]{1,0:T(8,128)(2,1)S(1)}, bf16[296,128]{1,0:T(8,128)(2,1)S(1)}, u32[]{:S(2)}, u32[]{:S(2)}) collective-permute-start(bf16[296,128]{1,0:T(8,128)(2,1)S(1)} %add_convert_fusion), channel_id=1, source_target_pairs={{0,2},{1,3},{2,0},{3,1},{4,6},{5,7},{6,4},{7,5},{8,10},{9,11},{10,... | collective-permute-start | bytes 227336 | tf_op jit(solution)/shard_map/ppermute | solution.py:268

commit v2 on v1

v2 whole, which is shorter than its diff:
```python
import functools

import jax
import jax.numpy as jnp
from jax import lax
from jax.experimental import pallas as pl
from jax.experimental.pallas import tpu as pltpu
from jax.sharding import PartitionSpec as P

BF = jnp.bfloat16
F32 = jnp.float32
EDGE = 2
STRIP = 16
GROUP_ROWS = 24


def pairings(count):
    out = []
    for start in (0, 1):
        perm = []
        for i in range(count):
            other = ((i - start) ^ 1) + start
            perm.append((i, other if i >= start and other < count else i))
        out.append(perm)
    return out


def swap_edges(pick, axis):
    even, odd = pairings(lax.axis_size(axis))
    is_odd = lax.axis_index(axis) % 2
    got_even = lax.ppermute(pick(is_odd == 0), axis, even)
    got_odd = lax.ppermute(pick(is_odd == 1), axis, odd)
    return got_even, got_odd


def dot(a, b):
    return jnp.dot(a, b, preferred_element_type=F32)


def gate(v):
    return 0.5 + 0.5 * jnp.tanh(0.5 * v)


def column_mask(pos, wide, cols, inner):
    spot = lax.broadcasted_iota(jnp.int32, (wide, inner), 0)
    has_low, has_high = pos[3].astype(F32), pos[4].astype(F32)
    return jnp.where(spot < cols, 1.0, jnp.where(spot < cols + STRIP // 2, has_high, has_low))


def vectors(ref, inner):
    return [ref[i : i + 1, 0:inner] for i in range(4)] + [ref[4:5, :], ref[5:6, :]]


def spread(ref, r, v):
    wide, inner = v.shape
    ref[r, :, 0:inner] = pltpu.roll(v, 1, 0).astype(BF)
    ref[r, :, inner : 2 * inner] = v.astype(BF)
    ref[r, :, 2 * inner :] = pltpu.roll(v, wide - 1, 0).astype(BF)


def conv3(windows, w_ref):
    n = w_ref.shape[0] // 3
    out = dot(windows(0), w_ref[0:n, :])
    for dh in (1, 2):
        out = out + dot(windows(dh), w_ref[dh * n : (dh + 1) * n, :])
    return out


def reduce_act(x, w1, s1, b1):
    pre = dot(x, w1) * s1 + b1
    sg = gate(pre)
    return pre * sg, sg


def through(conv, skip, ct, s2, b2, w3, w3t, s3, b3):
    pre2 = conv * s2 + b2
    sg2 = gate(pre2)
    silu2 = pre2 * sg2
    a2 = silu2.astype(BF)
    pre3 = dot(a2, w3) * s3 + b3 + skip.astype(F32)
    sg3 = gate(pre3)
    back3 = ct.astype(F32) * (sg3 + pre3 * sg3 * (1.0 - sg3))
    grad3 = (back3 * s3).astype(BF)
    grad2 = dot(grad3, w3t) * ((sg2 + silu2 * (1.0 - sg2)) * s2)
    return a2, grad3, back3, grad2


def weights_kernel(gw_ref, w3_ref, w2, w2t, w3t, *, inner, group_ch):
    sub = lax.broadcasted_iota(jnp.int32, (inner, inner), 0)
    lane = lax.broadcasted_iota(jnp.int32, (inner, inner), 1)
    diag = jnp.where(sub // group_ch == lane // group_ch, 1.0, 0.0).astype(F32)
    for t in range(9):
        four = gw_ref[t * group_ch : (t + 1) * group_ch, :]
        eight = jnp.concatenate([four, four], axis=0)
        tiled = jnp.broadcast_to(eight[None], (inner // 8, 8, inner)).reshape(inner, inner)
        dense = tiled * diag
        w2[t * inner : (t + 1) * inner, :] = dense.astype(BF)
        w2t[(8 - t) * inner : (9 - t) * inner, :] = dense.T.astype(BF)
    w3t[...] = w3_ref[...].T


def inner_kernel(
    pos, x_ref, c_ref, strip_ref, w1_ref, vec_ref, w2, w2t, w3_ref, w3t_ref,
    acts, gcat, d1, back, g1, gw3_ref, full_ref, gw1t_ref, xs, cs,
    *, rows, cols, chans, inner,
):
    wide = cols + STRIP
    step = 2
    col_ok = column_mask(pos, wide, cols, inner)
    s1, b1, s2, b2, s3, b3 = vectors(vec_ref, inner)
    w1 = w1_ref[...]
    for r in range(rows):
        xs[r, 0:cols, :] = x_ref[r]
        xs[r, cols:wide, :] = strip_ref[r]
        cs[r, 0:cols, :] = c_ref[r]
        cs[r, cols:wide, :] = strip_ref[rows + r]
    for r0 in range(0, rows, step):
        act, sg = reduce_act(xs[r0 : r0 + step].reshape(step * wide, chans), w1, s1, b1)
        slope = (sg + act * (1.0 - sg)) * s1
        for k in range(step):
            r = r0 + k
            spread(acts, r, act[k * wide : (k + 1) * wide] * col_ok)
            d1[r * cols : (r + 1) * cols, :] = slope[k * wide : k * wide + cols]
    rest = (s2, b2, w3_ref[...], w3t_ref[...], s3, b3)
    gw3 = jnp.zeros((inner, chans), F32)
    for p0 in range(1, rows - 1, step):
        conv = conv3(lambda dh: acts[p0 - 1 + dh : p0 - 1 + dh + step].reshape(step * wide, 3 * inner), w2)
        skip = xs[p0 : p0 + step].reshape(step * wide, chans)
        ct = cs[p0 : p0 + step].reshape(step * wide, chans)
        a2, grad3, back3, grad2 = through(conv, skip, ct, *rest)
        for k in range(step):
            spread(gcat, p0 - 1 + k, grad2[k * wide : (k + 1) * wide] * col_ok)
            back[(p0 - 1 + k) * cols : (p0 + k) * cols, :] = back3[k * wide : k * wide + cols]
        own = [slice(k * wide, k * wide + cols) for k in range(step)]
        gw3 = gw3 + dot(
            jnp.concatenate([a2[at] for at in own], axis=0).T, jnp.concatenate([grad3[at] for at in own], axis=0)
        )
    gw3_ref[...] = gw3
    n = (rows - 2) * cols
    own_gt = gcat[:, 0:cols, inner : 2 * inner].reshape(n, inner).T
    for dh in range(3):
        full_ref[dh] = dot(own_gt, acts[dh : dh + rows - 2, 0:cols, :].reshape(n, 3 * inner))
    gw1t = jnp.zeros((inner, chans), F32)
    for p0 in range(2, rows - 2, step):
        conv = conv3(lambda dh: gcat[p0 - 2 + dh : p0 - 2 + dh + step, 0:cols, :].reshape(step * cols, 3 * inner), w2t)
        g = (conv * d1[p0 * cols : (p0 + step) * cols, :]).astype(BF)
        g1[(p0 - 2) * cols : (p0 - 2 + step) * cols, :] = g
        gw1t = gw1t + dot(g.T, x_ref[p0 : p0 + step].reshape(step * cols, chans))
    gw1t_ref[...] = gw1t


def rim_kernel(
    pos, x_ref, c_ref, strip_ref, row_even, row_odd, w1_ref, vec_ref, w2, w2t, w3_ref, w3t_ref,
    acts, gcat, d1, gw3_ref, full_ref, gw1t_ref,
    share_ref, g1, back, hacts, hgrad,
    *, rows, cols, chans, inner, group_ch,
):
    wide = cols + STRIP
    col_ok = column_mask(pos, wide, cols, inner)
    s1, b1, s2, b2, s3, b3 = vectors(vec_ref, inner)
    row_is_odd = pos[0]
    has_low, has_high = pos[1].astype(F32), pos[2].astype(F32)

    def halo(i, low):
        a, b = row_even[i].astype(F32), row_odd[i].astype(F32)
        take_odd = (row_is_odd == 0) if low else (row_is_odd == 1)
        return jnp.where(take_odd, b, a).astype(BF)

    def wider(ref, r, base):
        return jnp.concatenate([ref[r], strip_ref[base + r]], axis=0)

    far = [halo(0, True), halo(1, True), halo(0, False), halo(1, False)]
    act, _ = reduce_act(jnp.concatenate(far, axis=0), w1_ref[...], s1, b1)
    for k in range(4):
        spread(hacts, k, act[k * wide : (k + 1) * wide] * (col_ok * (has_low if k < 2 else has_high)))
    def act_row(r):
        return hacts[r] if r < 2 else acts[r - 2] if r < rows + 2 else hacts[r - rows]

    mids = (0, 1, rows, rows + 1)
    conv = conv3(lambda dh: jnp.concatenate([act_row(q + dh) for q in mids], axis=0), w2)
    skip = jnp.concatenate([far[1], wider(x_ref, 0, 0), wider(x_ref, rows - 1, 0), far[2]], axis=0)
    ct = jnp.concatenate([halo(2, True), wider(c_ref, 0, rows), wider(c_ref, rows - 1, rows), halo(2, False)], axis=0)
    a2, grad3, back3, grad2 = through(conv, skip, ct, s2, b2, w3_ref[...], w3t_ref[...], s3, b3)
    for k in range(4):
        g = grad2[k * wide : (k + 1) * wide] * col_ok
        spread(hgrad, k, g * has_low if k == 0 else g * has_high if k == 3 else g)
    own = [slice(k * wide, k * wide + cols) for k in (1, 2)]
    for k in range(2):
        back[k * cols : (k + 1) * cols, :] = back3[own[k]]
    gw3 = gw3_ref[...] + dot(
        jnp.concatenate([a2[at] for at in own], axis=0).T, jnp.concatenate([grad3[at] for at in own], axis=0)
    )
    own_gt = jnp.concatenate([hgrad[k, 0:cols, inner : 2 * inner] for k in (1, 2)], axis=0).T
    sub = lax.broadcasted_iota(jnp.int32, (inner, 3 * inner), 0)
    lane = lax.broadcasted_iota(jnp.int32, (inner, 3 * inner), 1)
    same = jnp.where(sub // group_ch == (lane % inner) // group_ch, 1.0, 0.0).astype(F32)
    pick_sub = lax.broadcasted_iota(jnp.int32, (3 * inner, inner), 0)
    pick_lane = lax.broadcasted_iota(jnp.int32, (3 * inner, inner), 1)
    compact = jnp.zeros((inner, inner), F32)
    for dh in range(3):
        near = jnp.concatenate([act_row(q + dh)[0:cols] for q in (1, rows)], axis=0)
        full = ((full_ref[dh] + dot(own_gt, near)) * same).astype(BF)
        place = (dh * 3 + pick_sub // inner) * group_ch + pick_sub % group_ch
        compact = compact + dot(full, jnp.where(pick_lane == place, 1.0, 0.0).astype(BF))
    gw2 = compact.T

    def grad_row(q):
        return (hgrad[q] if q < 2 else gcat[q - 2] if q < rows else hgrad[q - rows + 2])[0:cols]

    outs = (0, 1, rows - 2, rows - 1)
    conv = conv3(lambda dh: jnp.concatenate([grad_row(p + dh) for p in outs], axis=0), w2t)
    slope = jnp.concatenate([d1[0 : 2 * cols, :], d1[(rows - 2) * cols :, :]], axis=0)
    g = (conv * slope).astype(BF)
    g1[...] = g
    gw1 = (gw1t_ref[...] + dot(g.T, jnp.concatenate([x_ref[p] for p in outs], axis=0))).T
    n_dp = share_ref.shape[1]
    one, three = chans // n_dp, inner // n_dp
    for h in range(n_dp):
        share_ref[0, h, 0:one, :] = gw1[h * one : (h + 1) * one]
        for k in range(chans // inner):
            share_ref[1, h, k * three : (k + 1) * three, :] = gw3[
                h * three : (h + 1) * three, k * inner : (k + 1) * inner
            ]
        group = gw2 if h == 0 else pltpu.roll(gw2, inner - h * three, 1)
        share_ref[0, h, one : one + GROUP_ROWS, :] = group[0:GROUP_ROWS]
        share_ref[1, h, one : one + GROUP_ROWS, :] = group[GROUP_ROWS : 2 * GROUP_ROWS]


def out_kernel(g1_in, g1_rim, back_in, back_rim, w1_ref, out_ref, *, rows, cols, chans):
    w1t = w1_ref[...].T
    for p in range(rows):
        if 2 <= p < rows - 2:
            g = g1_in[(p - 2) * cols : (p - 1) * cols, :]
        else:
            k = p if p < 2 else p - rows + 4
            g = g1_rim[k * cols : (k + 1) * cols, :]
        if 1 <= p < rows - 1:
            b = back_in[(p - 1) * cols : p * cols, :]
        else:
            b = back_rim[0:cols, :] if p == 0 else back_rim[cols:, :]
        out_ref[p] = (dot(g, w1t) + b).astype(BF)


def last_kernel(
    pos, a_ref, b_ref, r_out, g_out, e_out, r_ref, g_ref, e_ref, sems, *, scale, one, three, chans, inner, group_ch
):
    other_first = pos[5] == 1
    first = jnp.where(other_first, b_ref[...], a_ref[...]) * scale
    second = jnp.where(other_first, a_ref[...], b_ref[...]) * scale
    r_ref[...] = first[0:one]
    for k in range(chans // inner):
        e_ref[:, k * inner : (k + 1) * inner] = second[k * three : (k + 1) * three]
    for t in range(9):
        at = t * group_ch
        part = first[one + at : one + at + group_ch] if at < GROUP_ROWS else second[
            one + at - GROUP_ROWS : one + at - GROUP_ROWS + group_ch]
        g_ref[t // 3, t % 3] = part[:, 0:three]
    copies = [
        pltpu.make_async_copy(src, dst, sems.at[i])
        for i, (src, dst) in enumerate(((r_ref, r_out), (e_ref, e_out), (g_ref, g_out)))
    ]
    for copy in copies:
        copy.start()
    for copy in copies:
        copy.wait()


def crossed(value, axis, bit):
    n_row = lax.axis_size("row")
    if axis == "row":
        return lax.ppermute(value, "row", [(i, i ^ bit ^ 1) for i in range(n_row)])
    count = lax.axis_size(axis)
    pairs = [(i, j, i ^ bit, j ^ 1) for i in range(count) for j in range(n_row)]
    if axis == "dp":
        return lax.ppermute(value, ("dp", "row"), [(i * n_row + j, k * n_row + m) for i, j, k, m in pairs])
    return lax.ppermute(value, ("row", "col"), [(j * count + i, m * count + k) for i, j, k, m in pairs])


def body(
    features, reduce_weight, scale_one, shift_one, group_weight, scale_two, shift_two, expand_weight, scale_three,
    shift_three, cotangent,
):
    _, rows, cols, chans = features.shape
    inner = reduce_weight.shape[1]
    group_ch = group_weight.shape[2]
    x, c = features[0], cotangent[0]
    n_dp, n_row, n_col = (lax.axis_size(a) for a in ("dp", "row", "col"))
    dp, row, col = (lax.axis_index(a) for a in ("dp", "row", "col"))

    def col_edge(high):
        start = jnp.where(high, cols - EDGE, 0)
        return jnp.concatenate([lax.dynamic_slice_in_dim(v, start, EDGE, axis=1) for v in (x, c)], axis=0)

    col_even, col_odd = swap_edges(col_edge, "col")
    from_high = jnp.where(col % 2 == 0, col_even, col_odd)
    from_low = jnp.where(col % 2 == 0, col_odd, col_even)
    gap = jnp.zeros((2 * rows, STRIP - 2 * EDGE, chans), BF)
    strip = jnp.concatenate([from_high, gap, from_low], axis=1)

    def row_edge(high):
        def cut(v, at, n, base=0):
            return lax.dynamic_slice_in_dim(v, base + jnp.where(high, rows - n, 0), n, axis=0)

        main = jnp.concatenate([cut(x, 0, 2), cut(c, 0, 1)], axis=0)
        side = jnp.concatenate([cut(strip, 0, 2), cut(strip, 0, 1, rows)], axis=0)
        return jnp.concatenate([main, side], axis=1)

    row_even, row_odd = swap_edges(row_edge, "row")
    parity = (dp ^ (dp >> 1) ^ (dp >> 2) ^ (dp >> 3) ^ row ^ (row >> 1) ^ (row >> 2) ^ col ^ (col >> 1) ^ (col >> 2)) & 1
    pos = jnp.stack([row % 2, row > 0, row < n_row - 1, col > 0, col < n_col - 1, parity]).astype(jnp.int32)
    wide = cols + STRIP
    one, three = chans // n_dp, inner // n_dp
    half_rows = one + GROUP_ROWS
    vmem = pl.BlockSpec(memory_space=pltpu.VMEM)
    smem = pl.BlockSpec(memory_space=pltpu.SMEM)
    params = pltpu.CompilerParams(vmem_limit_bytes=8 << 20)
    sizes = dict(rows=rows, cols=cols, chans=chans)
    shape = jax.ShapeDtypeStruct
    w2, w2t, w3t = pl.pallas_call(
        functools.partial(weights_kernel, inner=inner, group_ch=group_ch),
        out_shape=(shape((9 * inner, inner), BF), shape((9 * inner, inner), BF), shape((chans, inner), BF)),
        in_specs=[vmem] * 2,
        out_specs=(vmem,) * 3,
        compiler_params=params,
        name="weights",
    )(group_weight.astype(F32).reshape(9 * group_ch, inner), expand_weight)
    narrow = jnp.stack([scale_one, shift_one, scale_two, shift_two])
    vecs = jnp.concatenate(
        [jnp.pad(narrow, ((0, 0), (0, chans - inner))), scale_three[None], shift_three[None]], axis=0
    )
    shared = (reduce_weight, vecs, w2, w2t, expand_weight, w3t)
    acts, gcat, d1, back_in, g1_in, gw3, full, gw1t = pl.pallas_call(
        functools.partial(inner_kernel, inner=inner, **sizes),
        out_shape=(
            shape((rows, wide, 3 * inner), BF),
            shape((rows - 2, wide, 3 * inner), BF),
            shape((rows * cols, inner), F32),
            shape(((rows - 2) * cols, chans), F32),
            shape(((rows - 4) * cols, inner), BF),
            shape((inner, chans), F32),
            shape((3, inner, 3 * inner), F32),
            shape((inner, chans), F32),
        ),
        in_specs=[smem] + [vmem] * 9,
        out_specs=(vmem,) * 8,
        scratch_shapes=[pltpu.VMEM((rows, wide, chans), BF), pltpu.VMEM((rows, wide, chans), BF)],
        compiler_params=params,
        name="inner",
    )(pos, x, c, strip, *shared)
    shares, g1_rim, back_rim = pl.pallas_call(
        functools.partial(rim_kernel, inner=inner, group_ch=group_ch, **sizes),
        out_shape=(
            shape((2, n_dp, half_rows, inner), F32),
            shape((4 * cols, inner), BF),
            shape((2 * cols, chans), F32),
        ),
        in_specs=[smem] + [vmem] * 17,
        out_specs=(vmem,) * 3,
        scratch_shapes=[pltpu.VMEM((4, wide, 3 * inner), BF), pltpu.VMEM((4, wide, 3 * inner), BF)],
        compiler_params=params,
        name="rim",
    )(pos, x, c, strip, row_even, row_odd, *shared, acts, gcat, d1, gw3, full, gw1t)
    mine = lax.dynamic_index_in_dim(shares, parity, axis=0, keepdims=False)
    theirs = lax.dynamic_index_in_dim(shares, 1 - parity, axis=0, keepdims=False)
    near = [(i, i ^ 1) for i in range(n_row)]
    shares = (mine + lax.ppermute(theirs, "row", near)).astype(BF)
    g1_rim, shares = lax.optimization_barrier((g1_rim, shares))
    input_grad = pl.pallas_call(
        functools.partial(out_kernel, **sizes),
        out_shape=shape((rows, cols, chans), BF),
        in_specs=[vmem] * 5,
        out_specs=vmem,
        compiler_params=params,
        name="out",
    )(g1_in, g1_rim, back_in, back_rim, reduce_weight)
    held = n_dp
    while held > 1:
        half = held // 2
        bit = (dp // half) % 2
        mine = lax.dynamic_slice_in_dim(shares, bit * half, half, axis=0)
        theirs = lax.dynamic_slice_in_dim(shares, (1 - bit) * half, half, axis=0)
        shares = (mine.astype(F32) + crossed(theirs, "dp", half).astype(F32)).astype(BF)
        held = half
    total = shares[0]
    steps = [("row", 1 << k) for k in range(1, n_row.bit_length() - 1)]
    steps += [("col", 1 << k) for k in range(n_col.bit_length() - 1)]
    for axis, bit in steps:
        other = crossed(total, axis, bit)
        if (axis, bit) == steps[0]:
            input_grad, other = lax.optimization_barrier((input_grad, other))
        summed = total.astype(F32) + other.astype(F32)
        total = summed.astype(BF)
    pixels = rows * cols * n_dp * n_row * n_col
    reduce_grad, group_grad, expand_grad = pl.pallas_call(
        functools.partial(
            last_kernel, scale=pixels**-0.5, one=one, three=three, chans=chans, inner=inner, group_ch=group_ch
        ),
        out_shape=(
            jax.ShapeDtypeStruct((one, inner), F32),
            jax.ShapeDtypeStruct((3, 3, group_ch, three), F32),
            jax.ShapeDtypeStruct((three, chans), F32),
        ),
        in_specs=[smem, vmem, vmem],
        out_specs=(pl.BlockSpec(memory_space=pl.ANY),) * 3,
        scratch_shapes=[
            pltpu.VMEM((one, inner), F32),
            pltpu.VMEM((3, 3, group_ch, three), F32),
            pltpu.VMEM((three, chans), F32),
            pltpu.SemaphoreType.DMA((3,)),
        ],
        compiler_params=pltpu.CompilerParams(vmem_limit_bytes=2 << 20),
        name="last",
    )(pos, summed, lax.ppermute(summed, "row", near))
    return input_grad[None], reduce_grad, jnp.transpose(group_grad, (3, 0, 1, 2)), expand_grad


def solution(mesh):
    image = P("dp", "row", "col", None)
    return jax.shard_map(
        body,
        mesh=mesh,
        in_specs=(image,) + (P(),) * 9 + (image,),
        out_specs=(image, P("dp", None), P("dp", None, None, None), P("dp", None)),
        check_vma=False,
    )
```

time: 47.6 us -> 41.3 us (0.87)
  waiting for transfers between devices: 16.6 us -> 10.3 us
  starting transfers between devices: 19.3 us -> 16.2 us
  Pallas kernels: 7.06 us -> 9.15 us
  local copies, waits for them, and re-layouts: 2.71 us -> 4.2 us
  other arithmetic: 0.81 us -> 0.28 us
    ppermute x2, waiting for transfers between devices: 3.46 us -> 0.01 us  [swap_edges(): got_even = lax.ppermute(pick(is_odd == 0), axis, even)]
    ppermute x5 -> x6, waiting for transfers between devices: 13.1 us -> 10.3 us  [the longest x2 4.75 us: crossed(): lax.ppermute(value, ('row', 'col'), [(j * count + i, m * count + k) for i...]
    ppermute x2, starting transfers between devices: 8.81 us -> 5.98 us  [swap_edges(): got_even = lax.ppermute(pick(is_odd == 0), axis, even)]
    pallas_call x1 -> x5, Pallas kernels: 7.06 us -> 9.15 us  [the longest x1 3.78 us: body(): pl.pallas_call(functools.partial(inner_kernel, inner=inner, **sizes), out...]
    unnamed x29 -> x22, local copies, waits for them, and re-layouts: 0.2 us -> 2.06 us
    dynamic_slice x3 -> x5, local copies, waits for them, and re-layouts: 1.12 us -> 1.93 us  [the longest x4 1.03 us: cut(): lax.dynamic_slice_in_dim(v, base + jnp.where(high, rows - n, 0), n, axis=0)]
    slice x3 -> x0, local copies, waits for them, and re-layouts: 0.65 us -> none  [the longest x1 0.63 us: body(): return (input_grad[None], total[0:one], group_grad, expand_grad)]
    reshape x1 -> x0, local copies, waits for them, and re-layouts: 0.62 us -> none  [body(): group.reshape(3, 3, group_ch, three)]
  transfers between devices with their start and end apart: 9 -> 10, of which waited for: 7 -> 6; matrix products, arithmetic and copies ran while one was open for 0% -> 3% of each run, Pallas kernels for 0% -> 12%
where the time goes in v2:
time: 41.3 us; the launch traced here: 41 us
  starting transfers between devices  16.2 us (39%)
  waiting for transfers between devices  10.3 us (25%)
  Pallas kernels  9.15 us (22%)
  local copies, waits for them, and re-layouts  4.2 us (10%)
  between operations  0.97 us (2%)
    ppermute x2, starting transfers between devices, swap_edges(): got_even = lax.ppermute(pick(is_odd == 0), axis, even)  5.98 us
    ppermute x2, waiting for transfers between devices, crossed(): lax.ppermute(value, ('row', 'col'), [(j * count + i, m * count + k) for i...  4.75 us
    pallas_call x1, Pallas kernels, body(): pl.pallas_call(functools.partial(inner_kernel, inner=inner, **sizes), out...  3.78 us
    ppermute x2, starting transfers between devices, crossed(): lax.ppermute(value, ('row', 'col'), [(j * count + i, m * count + k) for i...  3.09 us
    ppermute x1, starting transfers between devices, body(): shares = (mine + lax.ppermute(theirs, 'row', near)).astype(BF)  2.9 us
    pallas_call x1, Pallas kernels, body(): pl.pallas_call(functools.partial(rim_kernel, inner=inner, group_ch=group_...  2.88 us
    unnamed x22, local copies, waits for them, and re-layouts  2.06 us
    ppermute x1, waiting for transfers between devices, crossed(): lax.ppermute(value, ('dp', 'row'), [(i * n_row + j, k * n_row + m) for i,...  1.93 us
  transfers between devices with their start and end apart: 10, of which 6 were waited for; matrix products, arithmetic and copies ran while one was open for 3% of the time, Pallas kernels for 12%

profile of v2, /device:TPU:0, one launch (start us, length us, event | category | flops | bytes accessed | tf_op | source)
XLA Modules:
  0.0 41.0 jit_solution(10562267905906920097)
XLA Ops:
  0.7 0.9 %dynamic-slice_bitcast_fusion.7 = (bf16[8,2,256]{2,1,0:T(2,128)(2,1)S(1)}, bf16[8,2,256]{2,1,0:T(2,128)(2,1)S(1)}, bf16[8,2,256]{2,1,0:T(2,128)(2,1)S(1)}, bf16[8,2,256]{2,1,0:T(2,128)(2,1)S(1)}) fusion(bf16[1,8,128,256]{3,2,1,0:T(8,128)(2,1)} %param.21, s32[]{:T(128)S(6)} %select_n.90, s32[]{:T(128)S(6)} %select_n.91, bf16[1,8,128,256]{3,2,1,0:T(8,128)(2,1)} %param.11), kind=kLoop, calls=%fused_computation.22 | loop fusion | bytes 65544 | tf_op jit(solution)/shard_map/dynamic_slice | solution.py:292
  1.6 0.7 %collective-permute-start.1 = (bf16[16,2,256]{2,1,0:T(2,128)(2,1)S(1)}, bf16[16,2,256]{2,1,0:T(2,128)(2,1)S(1)}, u32[]{:S(2)}, u32[]{:S(2)}) collective-permute-start(bf16[16,2,256]{2,1,0:T(2,128)(2,1)S(1)} %pad_maximum_fusion.2), channel_id=1, source_target_pairs={{0,0},{1,2},{2,1},{3,3},{4,4},{5,6},{6,5},{7,7},{8,8},{9,10},{10,9... | collective-permute-start | bytes 49160 | tf_op jit(solution)/shard_map/ppermute | solution.py:32
  2.3 5.9 %collective-permute-start = (bf16[16,2,256]{2,1,0:T(2,128)(2,1)S(1)}, bf16[16,2,256]{2,1,0:T(2,128)(2,1)S(1)}, u32[]{:S(2)}, u32[]{:S(2)}) collective-permute-start(bf16[16,2,256]{2,1,0:T(2,128)(2,1)S(1)} %pad_maximum_fusion.1), channel_id=1, source_target_pairs={{0,1},{1,0},{2,3},{3,2},{4,5},{5,4},{6,7},{7,6},{8,9},{9,8},{10,11... | collective-permute-start | bytes 49160 | tf_op jit(solution)/shard_map/ppermute | solution.py:31
  8.2 1.0 %dynamic-slice_bitcast_fusion.1 = (bf16[2,128,256]{2,1,0:T(8,128)(2,1)S(1)}, bf16[2,128,256]{2,1,0:T(8,128)(2,1)S(1)}) fusion(bf16[1,8,128,256]{3,2,1,0:T(8,128)(2,1)} %param.11, s32[]{:T(128)S(6)} %select_n.97, s32[]{:T(128)S(6)} %select_n.94), kind=kLoop, calls=%fused_computation.6 | loop fusion | bytes 524296 | tf_op jit(solution)/shard_map/dynamic_slice | solution.py:302
  9.3 0.6 %copy-done.4 = bf16[3,3,4,128]{3,2,1,0:T(4,128)(2,1)S(1)} copy-done((bf16[3,3,4,128]{3,2,1,0:T(4,128)(2,1)S(1)}, bf16[3,3,4,128]{3,2,1,0:T(4,128)(2,1)}, u32[]{:S(2)}) %copy-start.4) | copy-done | bytes 9240
  10.7 0.8 %collective-permute-start.3 = (bf16[3,144,256]{2,1,0:T(8,128)(2,1)S(1)}, bf16[3,144,256]{2,1,0:T(8,128)(2,1)S(1)}, u32[]{:S(2)}, u32[]{:S(2)}) collective-permute-start(bf16[3,144,256]{2,1,0:T(8,128)(2,1)S(1)} %maximum_maximum_fusion.1), channel_id=1, source_target_pairs={{0,0},{4,8},{8,4},{12,12},{1,1},{5,9},{9,5},{13,13},{2,2},{6,10},{... | collective-permute-start | bytes 663560 | tf_op jit(solution)/shard_map/ppermute | solution.py:32
  11.6 0.6 %copy-done.7 = f32[128]{0:T(128)S(1)} copy-done((f32[128]{0:T(128)S(1)}, f32[128]{0:T(128)}, u32[]{:S(2)}) %copy-start.7) | copy-done | bytes 536
  12.2 0.7 %copy-done.5 = f32[256]{0:T(256)S(1)} copy-done((f32[256]{0:T(256)S(1)}, f32[256]{0:T(256)}, u32[]{:S(2)}) %copy-start.5) | copy-done | bytes 1048
  12.9 3.8 %inner.1 = (bf16[8,144,384]{2,1,0:T(8,128)(2,1)S(1)}, bf16[6,144,384]{2,1,0:T(8,128)(2,1)S(1)}, f32[1024,128]{1,0:T(8,128)S(1)}, f32[768,256]{1,0:T(8,128)S(1)},...) custom-call(s32[6]{0:T(128)S(1)} %stack.58.pos, ...), custom_call_target="tpu_custom_call" | custom-call | tf_op jit(solution)/shard_map/inner/pallas_call | solution.py:332
  16.7 2.9 %rim.1 = (f32[2,2,152,128]{3,2,1,0:T(8,128)S(1)}, bf16[512,128]{1,0:T(8,128)(2,1)S(1)}, f32[256,256]{1,0:T(8,128)S(1)}) custom-call(s32[6]{0:T(128)S(1)} %stack.58.pos, bf16[8,128,256]{2,1,0:T(8,128)(2,1)S(1)} %bitcast.45, bf16[8,128,256]{2,1,0:T(8,128)(2,1)S(1)} %bitcast.47, bf16[16,16,256]{2,1,0:T(8,128)(2,1)S(1)} %pad_maximum_fusion.strip_ref, ...), custom_call_target="tpu_custom_call" | custom-call | tf_op jit(solution)/shard_map/rim/pallas_call | solution.py:350
  19.6 2.9 %collective-permute-start.4 = (f32[2,152,128]{2,1,0:T(8,128)S(1)}, f32[2,152,128]{2,1,0:T(8,128)S(1)}, u32[]{:S(2)}, u32[]{:S(2)}) collective-permute-start(f32[2,152,128]{2,1,0:T(8,128)S(1)} %dynamic-slice_bitcast_fusion), channel_id=1, source_target_pairs={{0,4},{4,0},{8,12},{12,8},{1,5},{5,1},{9,13},{13,9},{2,6},{6,2},{1... | collective-permute-start | bytes 466952 | tf_op jit(solution)/shard_map/ppermute | solution.py:366
  22.5 1.0 %collective-permute-done.4 = f32[2,152,128]{2,1,0:T(8,128)S(1)} collective-permute-done((f32[2,152,128]{2,1,0:T(8,128)S(1)}, f32[2,152,128]{2,1,0:T(8,128)S(1)}, u32[]{:S(2)}, u32[]{:S(2)}) %collective-permute-start.4) | collective-permute-done | bytes 155680 | tf_op jit(solution)/shard_map/ppermute | solution.py:366
  23.6 1.6 %collective-permute-start.5 = (bf16[1,152,128]{2,1,0:T(8,128)(2,1)S(1)}, bf16[1,152,128]{2,1,0:T(8,128)(2,1)S(1)}, u32[]{:S(2)}, u32[]{:S(2)}) collective-permute-start(bf16[1,152,128]{2,1,0:T(8,128)(2,1)S(1)} %constant_dynamic-slice_fusion), channel_id=1, source_target_pairs={{0,20},{4,16},{8,28},{12,24},{16,4},{20,0},{24,12},{28,8},{1,21},{... | collective-permute-start | bytes 116744 | tf_op jit(solution)/shard_map/ppermute | solution.py:275
  25.1 1.9 %collective-permute-done.5 = bf16[1,152,128]{2,1,0:T(8,128)(2,1)S(1)} collective-permute-done((bf16[1,152,128]{2,1,0:T(8,128)(2,1)S(1)}, bf16[1,152,128]{2,1,0:T(8,128)(2,1)S(1)}, u32[]{:S(2)}, u32[]{:S(2)}) %collective-permute-start.5) | collective-permute-done | bytes 38944 | tf_op jit(solution)/shard_map/ppermute | solution.py:275
  27.1 0.7 %collective-permute-start.6 = (bf16[152,128]{1,0:T(8,128)(2,1)S(1)}, bf16[152,128]{1,0:T(8,128)(2,1)S(1)}, u32[]{:S(2)}, u32[]{:S(2)}) collective-permute-start(bf16[152,128]{1,0:T(8,128)(2,1)S(1)} %fusion.1), channel_id=1, source_target_pairs={{0,12},{4,8},{8,4},{12,0},{1,13},{5,9},{9,5},{13,1},{2,14},{6,10},... | collective-permute-start | bytes 116744 | tf_op jit(solution)/shard_map/ppermute | solution.py:271
  27.8 1.1 %out.1 = bf16[8,128,256]{2,1,0:T(8,128)(2,1)} custom-call(bf16[512,128]{1,0:T(8,128)(2,1)S(1)} %get-tuple-element.28.g1_in, bf16[512,128]{1,0:T(8,128)(2,1)S(1)} %get-tuple-element.37.g1_rim, f32[768,256]{1,0:T(8,128)S(1)} %get-tuple-element.38.back_in, f32[256,256]{1,0:T(8,128)S(1)} %get-tuple-element.39.back_rim, bf16[256,128]{1,0:T(8,128)(2,1)S(1)} %copy-done.3), custom_call_target="tpu_custom_call" | custom-call | tf_op jit(solution)/shard_map/out/pallas_call | solution.py:368
  28.9 1.6 %collective-permute-done.6 = bf16[152,128]{1,0:T(8,128)(2,1)S(1)} collective-permute-done((bf16[152,128]{1,0:T(8,128)(2,1)S(1)}, bf16[152,128]{1,0:T(8,128)(2,1)S(1)}, u32[]{:S(2)}, u32[]{:S(2)}) %collective-permute-start.6) | collective-permute-done | bytes 38944 | tf_op jit(solution)/shard_map/ppermute | solution.py:271
  30.6 1.6 %collective-permute-start.7 = (bf16[152,128]{1,0:T(8,128)(2,1)S(1)}, bf16[152,128]{1,0:T(8,128)(2,1)S(1)}, u32[]{:S(2)}, u32[]{:S(2)}) collective-permute-start(bf16[152,128]{1,0:T(8,128)(2,1)S(1)} %add_convert_fusion.1), channel_id=1, source_target_pairs={{0,5},{4,1},{8,13},{12,9},{1,4},{5,0},{9,12},{13,8},{2,7},{6,3},{1... | collective-permute-start | bytes 116744 | tf_op jit(solution)/shard_map/ppermute | solution.py:276
  32.2 1.9 %collective-permute-done.7 = bf16[152,128]{1,0:T(8,128)(2,1)S(1)} collective-permute-done((bf16[152,128]{1,0:T(8,128)(2,1)S(1)}, bf16[152,128]{1,0:T(8,128)(2,1)S(1)}, u32[]{:S(2)}, u32[]{:S(2)}) %collective-permute-start.7) | collective-permute-done | bytes 38944 | tf_op jit(solution)/shard_map/ppermute | solution.py:276
  34.1 1.5 %collective-permute-start.8 = (bf16[152,128]{1,0:T(8,128)(2,1)S(1)}, bf16[152,128]{1,0:T(8,128)(2,1)S(1)}, u32[]{:S(2)}, u32[]{:S(2)}) collective-permute-start(bf16[152,128]{1,0:T(8,128)(2,1)S(1)} %add_convert_fusion), channel_id=1, source_target_pairs={{0,6},{4,2},{8,14},{12,10},{1,7},{5,3},{9,15},{13,11},{2,4},{6,0},... | collective-permute-start | bytes 116744 | tf_op jit(solution)/shard_map/ppermute | solution.py:276
  35.6 2.9 %collective-permute-done.8 = bf16[152,128]{1,0:T(8,128)(2,1)S(1)} collective-permute-done((bf16[152,128]{1,0:T(8,128)(2,1)S(1)}, bf16[152,128]{1,0:T(8,128)(2,1)S(1)}, u32[]{:S(2)}, u32[]{:S(2)}) %collective-permute-start.8) | collective-permute-done | bytes 38944 | tf_op jit(solution)/shard_map/ppermute | solution.py:276
  38.5 0.4 %collective-permute-start.9 = (f32[152,128]{1,0:T(8,128)S(1)}, f32[152,128]{1,0:T(8,128)S(1)}, u32[]{:S(2)}, u32[]{:S(2)}) collective-permute-start(f32[152,128]{1,0:T(8,128)S(1)} %convert_add_fusion.a_ref), channel_id=1, source_target_pairs={{0,4},{4,0},{8,12},{12,8},{1,5},{5,1},{9,13},{13,9},{2,6},{6,2},{1... | collective-permute-start | bytes 233480 | tf_op jit(solution)/shard_map/ppermute | solution.py:413
  38.9 0.9 %collective-permute-done.9.b_ref = f32[152,128]{1,0:T(8,128)S(1)} collective-permute-done((f32[152,128]{1,0:T(8,128)S(1)}, f32[152,128]{1,0:T(8,128)S(1)}, u32[]{:S(2)}, u32[]{:S(2)}) %collective-permute-start.9) | collective-permute-done | bytes 77856 | tf_op jit(solution)/shard_map/ppermute | solution.py:413
  39.8 1.2 %last.1 = (f32[128,128]{1,0:T(8,128)}, f32[3,3,4,64]{3,2,1,0:T(4,128)}, f32[64,256]{1,0:T(8,128)}) custom-call(s32[6]{0:T(128)S(1)} %stack.58.pos, f32[152,128]{1,0:T(8,128)S(1)} %convert_add_fusion.a_ref, f32[152,128]{1,0:T(8,128)S(1)} %collective-permute-done.9.b_ref), custom_call_target="tpu_custom_call" | custom-call | tf_op jit(solution)/shard_map/last/pallas_call | solution.py:394
  (47 shorter events, 1.0 us)
Async XLA Ops:
  0.6 8.6 %copy-start.1 = (bf16[1,8,128,256]{3,2,1,0:T(8,128)(2,1)S(1)}, bf16[1,8,128,256]{3,2,1,0:T(8,128)(2,1)}, u32[]{:S(2)}) copy-start(bf16[1,8,128,256]{3,2,1,0:T(8,128)(2,1)} %param.21) | copy-start | bytes 1572868
  1.6 8.8 %collective-permute-start.1 = (bf16[16,2,256]{2,1,0:T(2,128)(2,1)S(1)}, bf16[16,2,256]{2,1,0:T(2,128)(2,1)S(1)}, u32[]{:S(2)}, u32[]{:S(2)}) collective-permute-start(bf16[16,2,256]{2,1,0:T(2,128)(2,1)S(1)} %pad_maximum_fusion.2), channel_id=1, source_target_pairs={{0,0},{1,2},{2,1},{3,3},{4,4},{5,6},{6,5},{7,7},{8,8},{9,10},{10,9... | collective-permute-start | bytes 49160 | tf_op jit(solution)/shard_map/ppermute | solution.py:32
  2.3 8.1 %collective-permute-start = (bf16[16,2,256]{2,1,0:T(2,128)(2,1)S(1)}, bf16[16,2,256]{2,1,0:T(2,128)(2,1)S(1)}, u32[]{:S(2)}, u32[]{:S(2)}) collective-permute-start(bf16[16,2,256]{2,1,0:T(2,128)(2,1)S(1)} %pad_maximum_fusion.1), channel_id=1, source_target_pairs={{0,1},{1,0},{2,3},{3,2},{4,5},{5,4},{6,7},{7,6},{8,9},{9,8},{10,11... | collective-permute-start | bytes 49160 | tf_op jit(solution)/shard_map/ppermute | solution.py:31
  9.2 0.7 %copy-start.4 = (bf16[3,3,4,128]{3,2,1,0:T(4,128)(2,1)S(1)}, bf16[3,3,4,128]{3,2,1,0:T(4,128)(2,1)}, u32[]{:S(2)}) copy-start(bf16[3,3,4,128]{3,2,1,0:T(4,128)(2,1)} %param.15) | copy-start | bytes 27652
  9.3 0.8 %copy-start.2 = (bf16[128,256]{1,0:T(8,128)(2,1)S(1)}, bf16[128,256]{1,0:T(8,128)(2,1)}, u32[]{:S(2)}) copy-start(bf16[128,256]{1,0:T(8,128)(2,1)} %w3_ref.5) | copy-start | bytes 196612
  10.5 2.4 %copy-start = (bf16[1,8,128,256]{3,2,1,0:T(8,128)(2,1)S(1)}, bf16[1,8,128,256]{3,2,1,0:T(8,128)(2,1)}, u32[]{:S(2)}) copy-start(bf16[1,8,128,256]{3,2,1,0:T(8,128)(2,1)} %param.11) | copy-start | bytes 1572868
  10.6 6.1 %collective-permute-start.2 = (bf16[3,144,256]{2,1,0:T(8,128)(2,1)S(1)}, bf16[3,144,256]{2,1,0:T(8,128)(2,1)S(1)}, u32[]{:S(2)}, u32[]{:S(2)}) collective-permute-start(bf16[3,144,256]{2,1,0:T(8,128)(2,1)S(1)} %maximum_maximum_fusion), channel_id=1, source_target_pairs={{0,4},{4,0},{8,12},{12,8},{1,5},{5,1},{9,13},{13,9},{2,6},{6,2},{1... | collective-permute-start | bytes 663560 | tf_op jit(solution)/shard_map/ppermute | solution.py:31
  10.6 0.9 %copy-start.10 = (f32[128]{0:T(128)S(1)}, f32[128]{0:T(128)}, u32[]{:S(2)}) copy-start(f32[128]{0:T(128)} %param.13) | copy-start | bytes 1540
  10.6 1.6 %copy-start.6 = (f32[256]{0:T(256)S(1)}, f32[256]{0:T(256)}, u32[]{:S(2)}) copy-start(f32[256]{0:T(256)} %param.19) | copy-start | bytes 3076
  10.7 2.3 %copy-start.3 = (bf16[256,128]{1,0:T(8,128)(2,1)S(1)}, bf16[256,128]{1,0:T(8,128)(2,1)}, u32[]{:S(2)}) copy-start(bf16[256,128]{1,0:T(8,128)(2,1)} %w1_ref.5) | copy-start | bytes 196612
  10.7 6.0 %collective-permute-start.3 = (bf16[3,144,256]{2,1,0:T(8,128)(2,1)S(1)}, bf16[3,144,256]{2,1,0:T(8,128)(2,1)S(1)}, u32[]{:S(2)}, u32[]{:S(2)}) collective-permute-start(bf16[3,144,256]{2,1,0:T(8,128)(2,1)S(1)} %maximum_maximum_fusion.1), channel_id=1, source_target_pairs={{0,0},{4,8},{8,4},{12,12},{1,1},{5,9},{9,5},{13,13},{2,2},{6,10},{... | collective-permute-start | bytes 663560 | tf_op jit(solution)/shard_map/ppermute | solution.py:32
  11.5 0.7 %copy-start.7 = (f32[128]{0:T(128)S(1)}, f32[128]{0:T(128)}, u32[]{:S(2)}) copy-start(f32[128]{0:T(128)} %param.17) | copy-start | bytes 1540
  11.5 0.7 %copy-start.8 = (f32[128]{0:T(128)S(1)}, f32[128]{0:T(128)}, u32[]{:S(2)}) copy-start(f32[128]{0:T(128)} %param.16) | copy-start | bytes 1540
  11.5 0.7 %copy-start.9 = (f32[128]{0:T(128)S(1)}, f32[128]{0:T(128)}, u32[]{:S(2)}) copy-start(f32[128]{0:T(128)} %param.14) | copy-start | bytes 1540
  12.2 0.7 %copy-start.5 = (f32[256]{0:T(256)S(1)}, f32[256]{0:T(256)}, u32[]{:S(2)}) copy-start(f32[256]{0:T(256)} %param.20) | copy-start | bytes 3076
  19.6 3.9 %collective-permute-start.4 = (f32[2,152,128]{2,1,0:T(8,128)S(1)}, f32[2,152,128]{2,1,0:T(8,128)S(1)}, u32[]{:S(2)}, u32[]{:S(2)}) collective-permute-start(f32[2,152,128]{2,1,0:T(8,128)S(1)} %dynamic-slice_bitcast_fusion), channel_id=1, source_target_pairs={{0,4},{4,0},{8,12},{12,8},{1,5},{5,1},{9,13},{13,9},{2,6},{6,2},{1... | collective-permute-start | bytes 466952 | tf_op jit(solution)/shard_map/ppermute | solution.py:366
  23.6 3.5 %collective-permute-start.5 = (bf16[1,152,128]{2,1,0:T(8,128)(2,1)S(1)}, bf16[1,152,128]{2,1,0:T(8,128)(2,1)S(1)}, u32[]{:S(2)}, u32[]{:S(2)}) collective-permute-start(bf16[1,152,128]{2,1,0:T(8,128)(2,1)S(1)} %constant_dynamic-slice_fusion), channel_id=1, source_target_pairs={{0,20},{4,16},{8,28},{12,24},{16,4},{20,0},{24,12},{28,8},{1,21},{... | collective-permute-start | bytes 116744 | tf_op jit(solution)/shard_map/ppermute | solution.py:275
  27.1 3.5 %collective-permute-start.6 = (bf16[152,128]{1,0:T(8,128)(2,1)S(1)}, bf16[152,128]{1,0:T(8,128)(2,1)S(1)}, u32[]{:S(2)}, u32[]{:S(2)}) collective-permute-start(bf16[152,128]{1,0:T(8,128)(2,1)S(1)} %fusion.1), channel_id=1, source_target_pairs={{0,12},{4,8},{8,4},{12,0},{1,13},{5,9},{9,5},{13,1},{2,14},{6,10},... | collective-permute-start | bytes 116744 | tf_op jit(solution)/shard_map/ppermute | solution.py:271
  30.6 3.5 %collective-permute-start.7 = (bf16[152,128]{1,0:T(8,128)(2,1)S(1)}, bf16[152,128]{1,0:T(8,128)(2,1)S(1)}, u32[]{:S(2)}, u32[]{:S(2)}) collective-permute-start(bf16[152,128]{1,0:T(8,128)(2,1)S(1)} %add_convert_fusion.1), channel_id=1, source_target_pairs={{0,5},{4,1},{8,13},{12,9},{1,4},{5,0},{9,12},{13,8},{2,7},{6,3},{1... | collective-permute-start | bytes 116744 | tf_op jit(solution)/shard_map/ppermute | solution.py:276
  34.1 4.4 %collective-permute-start.8 = (bf16[152,128]{1,0:T(8,128)(2,1)S(1)}, bf16[152,128]{1,0:T(8,128)(2,1)S(1)}, u32[]{:S(2)}, u32[]{:S(2)}) collective-permute-start(bf16[152,128]{1,0:T(8,128)(2,1)S(1)} %add_convert_fusion), channel_id=1, source_target_pairs={{0,6},{4,2},{8,14},{12,10},{1,7},{5,3},{9,15},{13,11},{2,4},{6,0},... | collective-permute-start | bytes 116744 | tf_op jit(solution)/shard_map/ppermute | solution.py:276
  38.5 1.3 %collective-permute-start.9 = (f32[152,128]{1,0:T(8,128)S(1)}, f32[152,128]{1,0:T(8,128)S(1)}, u32[]{:S(2)}, u32[]{:S(2)}) collective-permute-start(f32[152,128]{1,0:T(8,128)S(1)} %convert_add_fusion.a_ref), channel_id=1, source_target_pairs={{0,4},{4,0},{8,12},{12,8},{1,5},{5,1},{9,13},{13,9},{2,6},{6,2},{1... | collective-permute-start | bytes 233480 | tf_op jit(solution)/shard_map/ppermute | solution.py:413

commit v3 on v2

--- a/solution.py
+++ b/solution.py
@@ -1,4 +1,5 @@
 import functools
+import itertools
 
 import jax
 import jax.numpy as jnp
@@ -14,22 +15,21 @@
 GROUP_ROWS = 24
 
 
-def pairings(count):
-    out = []
-    for start in (0, 1):
-        perm = []
-        for i in range(count):
-            other = ((i - start) ^ 1) + start
-            perm.append((i, other if i >= start and other < count else i))
-        out.append(perm)
-    return out
-
-
-def swap_edges(pick, axis):
-    even, odd = pairings(lax.axis_size(axis))
-    is_odd = lax.axis_index(axis) % 2
-    got_even = lax.ppermute(pick(is_odd == 0), axis, even)
-    got_odd = lax.ppermute(pick(is_odd == 1), axis, odd)
+def swap_edges(to_even, to_odd, axis):
+    count, bands = lax.axis_size(axis), lax.axis_size("dp")
+    got_even = lax.ppermute(to_even, axis, [(i, i ^ 1) for i in range(count)])
+    names = ("dp", "row", "col")
+    sizes = [lax.axis_size(a) for a in names]
+    which = names.index(axis)
+    perm = []
+    for at in itertools.product(*(range(n) for n in sizes)):
+        to = list(at)
+        if 0 < at[which] < count - 1:
+            to[which] = ((at[which] - 1) ^ 1) + 1
+        elif bands > 1:
+            to[0] ^= 1
+        perm.append(tuple(functools.reduce(lambda v, k: v * sizes[k] + p[k], range(3), 0) for p in (at, to)))
+    got_odd = lax.ppermute(to_odd, names, perm)
     return got_even, got_odd
 
 
@@ -45,10 +45,6 @@
     spot = lax.broadcasted_iota(jnp.int32, (wide, inner), 0)
     has_low, has_high = pos[3].astype(F32), pos[4].astype(F32)
     return jnp.where(spot < cols, 1.0, jnp.where(spot < cols + STRIP // 2, has_high, has_low))
-
-
-def vectors(ref, inner):
-    return [ref[i : i + 1, 0:inner] for i in range(4)] + [ref[4:5, :], ref[5:6, :]]
 
 
 def spread(ref, r, v):
@@ -85,29 +81,57 @@
     return a2, grad3, back3, grad2
 
 
-def weights_kernel(gw_ref, w3_ref, w2, w2t, w3t, *, inner, group_ch):
+def load_kernel(*refs, inner, group_ch):
+    sources, targets, (w2, w2t, w3t, gw_ref, sems) = refs[:11], refs[11:21], refs[21:]
+    gw_hbm, sources = sources[0], sources[1:]
+    copies = [pltpu.make_async_copy(gw_hbm, gw_ref, sems.at[10])]
+    copies += [pltpu.make_async_copy(src, dst, sems.at[i]) for i, (src, dst) in enumerate(zip(sources, targets))]
+    for copy in copies:
+        copy.start()
+    copies[0].wait()
     sub = lax.broadcasted_iota(jnp.int32, (inner, inner), 0)
     lane = lax.broadcasted_iota(jnp.int32, (inner, inner), 1)
     diag = jnp.where(sub // group_ch == lane // group_ch, 1.0, 0.0).astype(F32)
     for t in range(9):
-        four = gw_ref[t * group_ch : (t + 1) * group_ch, :]
+        four = gw_ref[t // 3, t % 3].astype(F32)
         eight = jnp.concatenate([four, four], axis=0)
         tiled = jnp.broadcast_to(eight[None], (inner // 8, 8, inner)).reshape(inner, inner)
         dense = tiled * diag
         w2[t * inner : (t + 1) * inner, :] = dense.astype(BF)
         w2t[(8 - t) * inner : (9 - t) * inner, :] = dense.T.astype(BF)
-    w3t[...] = w3_ref[...].T
+    copies[1].wait()
+    w3t[...] = targets[0][...].T
+    for copy in copies[2:]:
+        copy.wait()
+
+
+def edges_kernel(pos, x_ref, c_ref, col_even, col_odd, strip, even_ref, odd_ref, *, rows, cols):
+    col_is_odd = pos[6] == 1
+    chans = x_ref.shape[2]
+    gap = jnp.zeros((STRIP - 2 * EDGE, chans), F32)
+    for r in range(2 * rows):
+        a, b = col_even[r].astype(F32), col_odd[r].astype(F32)
+        high, low = jnp.where(col_is_odd, b, a), jnp.where(col_is_odd, a, b)
+        strip[r] = jnp.concatenate([high, gap, low], axis=0).astype(BF)
+    for ref, sends_high in ((even_ref, pos[0] == 0), (odd_ref, pos[0] == 1)):
+        at = jnp.where(sends_high, rows - 2, 0)
+        cot_at = jnp.where(sends_high, rows - 1, 0)
+        for i in range(2):
+            ref[i, 0:cols, :] = x_ref[at + i]
+            ref[i, cols:, :] = strip[at + i]
+        ref[2, 0:cols, :] = c_ref[cot_at]
+        ref[2, cols:, :] = strip[rows + cot_at]
 
 
 def inner_kernel(
-    pos, x_ref, c_ref, strip_ref, w1_ref, vec_ref, w2, w2t, w3_ref, w3t_ref,
+    pos, x_ref, c_ref, strip_ref, w1_ref, s1_ref, b1_ref, s2_ref, b2_ref, s3_ref, b3_ref, w2, w2t, w3_ref, w3t_ref,
     acts, gcat, d1, back, g1, gw3_ref, full_ref, gw1t_ref, xs, cs,
     *, rows, cols, chans, inner,
 ):
     wide = cols + STRIP
     step = 2
     col_ok = column_mask(pos, wide, cols, inner)
-    s1, b1, s2, b2, s3, b3 = vectors(vec_ref, inner)
+    s1, b1, s2, b2, s3, b3 = (v[...] for v in (s1_ref, b1_ref, s2_ref, b2_ref, s3_ref, b3_ref))
     w1 = w1_ref[...]
     for r in range(rows):
         xs[r, 0:cols, :] = x_ref[r]
@@ -150,14 +174,14 @@
 
 
 def rim_kernel(
-    pos, x_ref, c_ref, strip_ref, row_even, row_odd, w1_ref, vec_ref, w2, w2t, w3_ref, w3t_ref,
+    pos, x_ref, c_ref, strip_ref, row_even, row_odd, w1_ref, s1_ref, b1_ref, s2_ref, b2_ref, s3_ref, b3_ref, w2, w2t, w3_ref, w3t_ref,
     acts, gcat, d1, gw3_ref, full_ref, gw1t_ref,
     share_ref, g1, back, hacts, hgrad,
     *, rows, cols, chans, inner, group_ch,
 ):
     wide = cols + STRIP
     col_ok = column_mask(pos, wide, cols, inner)
-    s1, b1, s2, b2, s3, b3 = vectors(vec_ref, inner)
+    s1, b1, s2, b2, s3, b3 = (v[...] for v in (s1_ref, b1_ref, s2_ref, b2_ref, s3_ref, b3_ref))
     row_is_odd = pos[0]
     has_low, has_high = pos[1].astype(F32), pos[2].astype(F32)
 
@@ -215,15 +239,17 @@
     gw1 = (gw1t_ref[...] + dot(g.T, jnp.concatenate([x_ref[p] for p in outs], axis=0))).T
     n_dp = share_ref.shape[1]
     one, three = chans // n_dp, inner // n_dp
+    at = (pos[5], 1 - pos[5])
     for h in range(n_dp):
-        share_ref[0, h, 0:one, :] = gw1[h * one : (h + 1) * one]
+        slot = h ^ pos[7]
+        share_ref[at[0], slot, 0:one, :] = gw1[h * one : (h + 1) * one]
         for k in range(chans // inner):
-            share_ref[1, h, k * three : (k + 1) * three, :] = gw3[
+            share_ref[at[1], slot, k * three : (k + 1) * three, :] = gw3[
                 h * three : (h + 1) * three, k * inner : (k + 1) * inner
             ]
         group = gw2 if h == 0 else pltpu.roll(gw2, inner - h * three, 1)
-        share_ref[0, h, one : one + GROUP_ROWS, :] = group[0:GROUP_ROWS]
-        share_ref[1, h, one : one + GROUP_ROWS, :] = group[GROUP_ROWS : 2 * GROUP_ROWS]
+        share_ref[at[0], slot, one : one + GROUP_ROWS, :] = group[0:GROUP_ROWS]
+        share_ref[at[1], slot, one : one + GROUP_ROWS, :] = group[GROUP_ROWS : 2 * GROUP_ROWS]
 
 
 def out_kernel(g1_in, g1_rim, back_in, back_rim, w1_ref, out_ref, *, rows, cols, chans):
@@ -287,27 +313,10 @@
     n_dp, n_row, n_col = (lax.axis_size(a) for a in ("dp", "row", "col"))
     dp, row, col = (lax.axis_index(a) for a in ("dp", "row", "col"))
 
-    def col_edge(high):
-        start = jnp.where(high, cols - EDGE, 0)
-        return jnp.concatenate([lax.dynamic_slice_in_dim(v, start, EDGE, axis=1) for v in (x, c)], axis=0)
-
-    col_even, col_odd = swap_edges(col_edge, "col")
-    from_high = jnp.where(col % 2 == 0, col_even, col_odd)
-    from_low = jnp.where(col % 2 == 0, col_odd, col_even)
-    gap = jnp.zeros((2 * rows, STRIP - 2 * EDGE, chans), BF)
-    strip = jnp.concatenate([from_high, gap, from_low], axis=1)
-
-    def row_edge(high):
-        def cut(v, at, n, base=0):
-            return lax.dynamic_slice_in_dim(v, base + jnp.where(high, rows - n, 0), n, axis=0)
-
-        main = jnp.concatenate([cut(x, 0, 2), cut(c, 0, 1)], axis=0)
-        side = jnp.concatenate([cut(strip, 0, 2), cut(strip, 0, 1, rows)], axis=0)
-        return jnp.concatenate([main, side], axis=1)
-
-    row_even, row_odd = swap_edges(row_edge, "row")
     parity = (dp ^ (dp >> 1) ^ (dp >> 2) ^ (dp >> 3) ^ row ^ (row >> 1) ^ (row >> 2) ^ col ^ (col >> 1) ^ (col >> 2)) & 1
-    pos = jnp.stack([row % 2, row > 0, row < n_row - 1, col > 0, col < n_col - 1, parity]).astype(jnp.int32)
+    pos = jnp.stack(
+        [row % 2, row > 0, row < n_row - 1, col > 0, col < n_col - 1, parity, col % 2, dp]
+    ).astype(jnp.int32)
     wide = cols + STRIP
     one, three = chans // n_dp, inner // n_dp
     half_rows = one + GROUP_ROWS
@@ -316,19 +325,39 @@
     params = pltpu.CompilerParams(vmem_limit_bytes=8 << 20)
     sizes = dict(rows=rows, cols=cols, chans=chans)
     shape = jax.ShapeDtypeStruct
-    w2, w2t, w3t = pl.pallas_call(
-        functools.partial(weights_kernel, inner=inner, group_ch=group_ch),
-        out_shape=(shape((9 * inner, inner), BF), shape((9 * inner, inner), BF), shape((chans, inner), BF)),
-        in_specs=[vmem] * 2,
+
+    def col_edge(high):
+        start = jnp.where(high, cols - EDGE, 0)
+        return jnp.concatenate([lax.dynamic_slice_in_dim(v, start, EDGE, axis=1) for v in (x, c)], axis=0)
+
+    to_even, to_odd = col_edge(col % 2 == 0), col_edge(col % 2 == 1)
+    to_even, to_odd, pos = lax.optimization_barrier((to_even, to_odd, pos))
+    col_even, col_odd = swap_edges(to_even, to_odd, "col")
+    sources = (
+        expand_weight, reduce_weight, x, c, scale_one[None], shift_one[None], scale_two[None], shift_two[None],
+        scale_three[None], shift_three[None],
+    )
+    w3, w1, x, c, *vecs, w2, w2t, w3t = pl.pallas_call(
+        functools.partial(load_kernel, inner=inner, group_ch=group_ch),
+        out_shape=tuple(shape(v.shape, v.dtype) for v in sources)
+        + (shape((9 * inner, inner), BF), shape((9 * inner, inner), BF), shape((chans, inner), BF)),
+        in_specs=[pl.BlockSpec(memory_space=pltpu.HBM)] * 11,
+        out_specs=(vmem,) * 13,
+        scratch_shapes=[pltpu.VMEM(group_weight.shape, BF), pltpu.SemaphoreType.DMA((11,))],
+        compiler_params=params,
+        name="load",
+    )(*(pltpu.with_memory_space_constraint(v, pltpu.HBM) for v in (group_weight, *sources)))
+    shared = (w1, *vecs, w2, w2t, w3, w3t)
+    col_even, col_odd, shared, x, c = lax.optimization_barrier((col_even, col_odd, shared, x, c))
+    strip, to_even, to_odd = pl.pallas_call(
+        functools.partial(edges_kernel, rows=rows, cols=cols),
+        out_shape=(shape((2 * rows, STRIP, chans), BF),) + (shape((3, wide, chans), BF),) * 2,
+        in_specs=[smem] + [vmem] * 4,
         out_specs=(vmem,) * 3,
         compiler_params=params,
-        name="weights",
-    )(group_weight.astype(F32).reshape(9 * group_ch, inner), expand_weight)
-    narrow = jnp.stack([scale_one, shift_one, scale_two, shift_two])
-    vecs = jnp.concatenate(
-        [jnp.pad(narrow, ((0, 0), (0, chans - inner))), scale_three[None], shift_three[None]], axis=0
-    )
-    shared = (reduce_weight, vecs, w2, w2t, expand_weight, w3t)
+        name="edges",
+    )(pos, x, c, col_even, col_odd)
+    row_even, row_odd = swap_edges(to_even, to_odd, "row")
     acts, gcat, d1, back_in, g1_in, gw3, full, gw1t = pl.pallas_call(
         functools.partial(inner_kernel, inner=inner, **sizes),
         out_shape=(
@@ -341,7 +370,7 @@
             shape((3, inner, 3 * inner), F32),
             shape((inner, chans), F32),
         ),
-        in_specs=[smem] + [vmem] * 9,
+        in_specs=[smem] + [vmem] * 14,
         out_specs=(vmem,) * 8,
         scratch_shapes=[pltpu.VMEM((rows, wide, chans), BF), pltpu.VMEM((rows, wide, chans), BF)],
         compiler_params=params,
@@ -354,16 +383,14 @@
             shape((4 * cols, inner), BF),
             shape((2 * cols, chans), F32),
         ),
-        in_specs=[smem] + [vmem] * 17,
+        in_specs=[smem] + [vmem] * 22,
         out_specs=(vmem,) * 3,
         scratch_shapes=[pltpu.VMEM((4, wide, 3 * inner), BF), pltpu.VMEM((4, wide, 3 * inner), BF)],
         compiler_params=params,
         name="rim",
     )(pos, x, c, strip, row_even, row_odd, *shared, acts, gcat, d1, gw3, full, gw1t)
-    mine = lax.dynamic_index_in_dim(shares, parity, axis=0, keepdims=False)
-    theirs = lax.dynamic_index_in_dim(shares, 1 - parity, axis=0, keepdims=False)
     near = [(i, i ^ 1) for i in range(n_row)]
-    shares = (mine + lax.ppermute(theirs, "row", near)).astype(BF)
+    shares = (shares[0] + lax.ppermute(shares[1], "row", near)).astype(BF)
     g1_rim, shares = lax.optimization_barrier((g1_rim, shares))
     input_grad = pl.pallas_call(
         functools.partial(out_kernel, **sizes),
@@ -372,15 +399,12 @@
         out_specs=vmem,
         compiler_params=params,
         name="out",
-    )(g1_in, g1_rim, back_in, back_rim, reduce_weight)
+    )(g1_in, g1_rim, back_in, back_rim, w1)
     held = n_dp
     while held > 1:
-        half = held // 2
-        bit = (dp // half) % 2
-        mine = lax.dynamic_slice_in_dim(shares, bit * half, half, axis=0)
-        theirs = lax.dynamic_slice_in_dim(shares, (1 - bit) * half, half, axis=0)
-        shares = (mine.astype(F32) + crossed(theirs, "dp", half).astype(F32)).astype(BF)
-        held = half
+        held //= 2
+        other = crossed(shares[held:], "dp", held)
+        shares = (shares[:held].astype(F32) + other.astype(F32)).astype(BF)
     total = shares[0]
     steps = [("row", 1 << k) for k in range(1, n_row.bit_length() - 1)]
     steps += [("col", 1 << k) for k in range(n_col.bit_length() - 1)]

time: 41.3 us -> 38.1 us (0.923)
  starting transfers between devices: 16.2 us -> 12.9 us
  local copies, waits for them, and re-layouts: 4.2 us -> 0.96 us
  waiting for transfers between devices: 10.3 us -> 12.2 us
  Pallas kernels: 9.15 us -> 11 us
    ppermute x5, starting transfers between devices: 10.4 us -> 6.38 us  [the longest x2 3.1 us: swap_edges(): got_odd = lax.ppermute(to_odd, names, perm)]
    unnamed x22 -> x0, local copies, waits for them, and re-layouts: 2.06 us -> none
    pallas_call x1 -> x2, Pallas kernels: 0.17 us -> 2 us  [the longest x1 1.4 us: body(): pl.pallas_call(functools.partial(load_kernel, inner=inner, group_ch=group...]
    ppermute x5, waiting for transfers between devices: 1.03 us -> 2.7 us  [the longest x2 1.43 us: swap_edges(): got_odd = lax.ppermute(to_odd, names, perm)]
    dynamic_slice x5 -> x0, local copies, waits for them, and re-layouts: 1.04 us -> none  [the longest x4 1.03 us: cut(): lax.dynamic_slice_in_dim(v, base + jnp.where(high, rows - n, 0), n, axis=0)]
    ppermute x1, starting transfers between devices: 0.42 us -> 1.06 us  [body(): lax.ppermute(summed, 'row', near)]
  transfers between devices with their start and end apart: 10 -> 10, of which waited for: 6 -> 8; matrix products, arithmetic and copies ran while one was open for 3% -> 0% of each run, Pallas kernels for 12% -> 17%
where the time goes in v3:
time: 38.1 us; the launch traced here: 37.9 us
  starting transfers between devices  12.9 us (34%)
  waiting for transfers between devices  12.2 us (32%)
  Pallas kernels  11 us (29%)
  local copies, waits for them, and re-layouts  0.96 us (3%)
  between operations  0.78 us (2%)
    ppermute x2, waiting for transfers between devices, crossed(): lax.ppermute(value, ('row', 'col'), [(j * count + i, m * count + k) for i...  4.61 us
    pallas_call x1, Pallas kernels, body(): pl.pallas_call(functools.partial(inner_kernel, inner=inner, **sizes), out...  3.77 us
    ppermute x2, starting transfers between devices, crossed(): lax.ppermute(value, ('row', 'col'), [(j * count + i, m * count + k) for i...  3.38 us
    ppermute x2, starting transfers between devices, swap_edges(): got_odd = lax.ppermute(to_odd, names, perm)  3.1 us
    ppermute x2, starting transfers between devices, swap_edges(): got_even = lax.ppermute(to_even, axis, [(i, i ^ 1) for i in range(count)])  3.1 us
    pallas_call x1, Pallas kernels, body(): pl.pallas_call(functools.partial(rim_kernel, inner=inner, group_ch=group_...  2.87 us
    ppermute x1, waiting for transfers between devices, crossed(): lax.ppermute(value, ('dp', 'row'), [(i * n_row + j, k * n_row + m) for i,...  2.22 us
    ppermute x1, waiting for transfers between devices, crossed(): return lax.ppermute(value, 'row', [(i, i ^ bit ^ 1) for i in range(n_row)])  1.72 us
  transfers between devices with their start and end apart: 10, of which 8 were waited for; matrix products, arithmetic and copies ran while one was open for 0% of the time, Pallas kernels for 17%

profile of v3, /device:TPU:0, one launch (start us, length us, event | category | flops | bytes accessed | tf_op | source)
XLA Modules:
  0.0 37.9 jit_solution(16690122501670280445)
XLA Ops:
  0.7 0.9 %dynamic-slice_bitcast_fusion = (bf16[8,2,256]{2,1,0:T(2,128)(2,1)S(1)}, bf16[8,2,256]{2,1,0:T(2,128)(2,1)S(1)}, bf16[8,2,256]{2,1,0:T(2,128)(2,1)S(1)}, bf16[8,2,256]{2,1,0:T(2,128)(2,1)S(1)}) fusion(bf16[1,8,128,256]{3,2,1,0:T(8,128)(2,1)} %param.21, s32[]{:T(128)S(6)} %select_n.28, s32[]{:T(128)S(6)} %select_n.27, bf16[1,8,128,256]{3,2,1,0:T(8,128)(2,1)} %param.11), kind=kLoop, calls=%fused_computation.10 | loop fusion | bytes 65544 | tf_op jit(solution)/shard_map/dynamic_slice | solution.py:331
  1.7 3.0 %collective-permute-start = (bf16[16,2,256]{2,1,0:T(2,128)(2,1)S(1)}, bf16[16,2,256]{2,1,0:T(2,128)(2,1)S(1)}, u32[]{:S(2)}, u32[]{:S(2)}) collective-permute-start(bf16[16,2,256]{2,1,0:T(2,128)(2,1)S(1)} %pad_maximum_fusion), channel_id=1, source_target_pairs={{0,1},{1,0},{2,3},{3,2},{4,5},{5,4},{6,7},{7,6},{8,9},{9,8},{10,11... | collective-permute-start | bytes 49160 | tf_op jit(solution)/shard_map/ppermute | solution.py:20
  4.7 1.5 %collective-permute-start.1 = (bf16[16,2,256]{2,1,0:T(2,128)(2,1)S(1)}, bf16[16,2,256]{2,1,0:T(2,128)(2,1)S(1)}, u32[]{:S(2)}, u32[]{:S(2)}) collective-permute-start(bf16[16,2,256]{2,1,0:T(2,128)(2,1)S(1)} %pad_maximum_fusion.1), channel_id=1, source_target_pairs={{0,16},{1,2},{2,1},{3,19},{4,20},{5,6},{6,5},{7,23},{8,24},{9,10},... | collective-permute-start | bytes 49160 | tf_op jit(solution)/shard_map/ppermute | solution.py:32
  6.2 1.4 %load.1 = (bf16[128,256]{1,0:T(8,128)(2,1)S(1)}, bf16[256,128]{1,0:T(8,128)(2,1)S(1)}, bf16[8,128,256]{2,1,0:T(8,128)(2,1)S(1)}, bf16[8,128,256]{2,1,0:T(8,128)(...) custom-call(bf16[3,3,4,128]{3,2,1,0:T(4,128)(2,1)} %refs_0_.1, ...), custom_call_target="tpu_custom_call" | custom-call | tf_op jit(solution)/shard_map/load/pallas_call | solution.py:340
  7.7 0.8 %collective-permute-done.1.col_odd = bf16[16,2,256]{2,1,0:T(2,128)(2,1)S(1)} collective-permute-done((bf16[16,2,256]{2,1,0:T(2,128)(2,1)S(1)}, bf16[16,2,256]{2,1,0:T(2,128)(2,1)S(1)}, u32[]{:S(2)}, u32[]{:S(2)}) %collective-permute-start.1) | collective-permute-done | bytes 16416 | tf_op jit(solution)/shard_map/ppermute | solution.py:32
  8.5 0.6 %edges.1 = (bf16[16,16,256]{2,1,0:T(8,128)(2,1)S(1)}, bf16[3,144,256]{2,1,0:T(8,128)(2,1)S(1)}, bf16[3,144,256]{2,1,0:T(8,128)(2,1)S(1)}) custom-call(s32[8]{0:T(128)S(1)} %stack.51.pos, bf16[8,128,256]{2,1,0:T(8,128)(2,1)S(1)} %get-tuple-element.72.x_ref, bf16[8,128,256]{2,1,0:T(8,128)(2,1)S(1)} %get-tuple-element.73.c_ref, ...), custom_call_target="tpu_custom_call" | custom-call | tf_op jit(solution)/shard_map/edges/pallas_call | solution.py:352
  9.1 1.6 %collective-permute-start.3 = (bf16[3,144,256]{2,1,0:T(8,128)(2,1)S(1)}, bf16[3,144,256]{2,1,0:T(8,128)(2,1)S(1)}, u32[]{:S(2)}, u32[]{:S(2)}) collective-permute-start(bf16[3,144,256]{2,1,0:T(8,128)(2,1)S(1)} %get-tuple-element.90), channel_id=1, source_target_pairs={{0,16},{1,17},{2,18},{3,19},{4,8},{5,9},{6,10},{7,11},{8,4},{9,5},... | collective-permute-start | bytes 663560 | tf_op jit(solution)/shard_map/ppermute | solution.py:32
  10.7 3.8 %inner.1 = (bf16[8,144,384]{2,1,0:T(8,128)(2,1)S(1)}, bf16[6,144,384]{2,1,0:T(8,128)(2,1)S(1)}, f32[1024,128]{1,0:T(8,128)S(1)}, f32[768,256]{1,0:T(8,128)S(1)},...) custom-call(s32[8]{0:T(128)S(1)} %stack.51.pos, ...), custom_call_target="tpu_custom_call" | custom-call | tf_op jit(solution)/shard_map/inner/pallas_call | solution.py:361
  14.5 0.6 %collective-permute-done.3.row_odd = bf16[3,144,256]{2,1,0:T(8,128)(2,1)S(1)} collective-permute-done((bf16[3,144,256]{2,1,0:T(8,128)(2,1)S(1)}, bf16[3,144,256]{2,1,0:T(8,128)(2,1)S(1)}, u32[]{:S(2)}, u32[]{:S(2)}) %collective-permute-start.3) | collective-permute-done | bytes 221216 | tf_op jit(solution)/shard_map/ppermute | solution.py:32
  15.1 2.9 %rim.1 = (f32[2,2,152,128]{3,2,1,0:T(8,128)S(1)}, bf16[512,128]{1,0:T(8,128)(2,1)S(1)}, f32[256,256]{1,0:T(8,128)S(1)}) custom-call(s32[8]{0:T(128)S(1)} %stack.51.pos, bf16[8,128,256]{2,1,0:T(8,128)(2,1)S(1)} %get-tuple-element.72.x_ref, bf16[8,128,256]{2,1,0:T(8,128)(2,1)S(1)} %get-tuple-element.73.c_ref, ...), custom_call_target="tpu_custom_call" | custom-call | tf_op jit(solution)/shard_map/rim/pallas_call | solution.py:379
  18.0 0.2 collective-permute-start.4
  18.2 1.3 %collective-permute-done.4 = f32[2,152,128]{2,1,0:T(8,128)S(1)} collective-permute-done((f32[2,152,128]{2,1,0:T(8,128)S(1)}, f32[2,152,128]{2,1,0:T(8,128)S(1)}, u32[]{:S(2)}, u32[]{:S(2)}) %collective-permute-start.4) | collective-permute-done | bytes 155680 | tf_op jit(solution)/shard_map/ppermute | solution.py:393
  19.5 1.3 %collective-permute-start.5 = (bf16[1,152,128]{2,1,0:T(8,128)(2,1)S(1)}, bf16[1,152,128]{2,1,0:T(8,128)(2,1)S(1)}, u32[]{:S(2)}, u32[]{:S(2)}) collective-permute-start(bf16[1,152,128]{2,1,0:T(8,128)(2,1)S(1)} %slice.15), channel_id=1, source_target_pairs={{0,20},{4,16},{8,28},{12,24},{16,4},{20,0},{24,12},{28,8},{1,21},{... | collective-permute-start | bytes 116744 | tf_op jit(solution)/shard_map/ppermute | solution.py:301
  20.9 2.2 %collective-permute-done.5 = bf16[1,152,128]{2,1,0:T(8,128)(2,1)S(1)} collective-permute-done((bf16[1,152,128]{2,1,0:T(8,128)(2,1)S(1)}, bf16[1,152,128]{2,1,0:T(8,128)(2,1)S(1)}, u32[]{:S(2)}, u32[]{:S(2)}) %collective-permute-start.5) | collective-permute-done | bytes 38944 | tf_op jit(solution)/shard_map/ppermute | solution.py:301
  23.1 0.7 %collective-permute-start.6 = (bf16[152,128]{1,0:T(8,128)(2,1)S(1)}, bf16[152,128]{1,0:T(8,128)(2,1)S(1)}, u32[]{:S(2)}, u32[]{:S(2)}) collective-permute-start(bf16[152,128]{1,0:T(8,128)(2,1)S(1)} %fusion.1), channel_id=1, source_target_pairs={{0,12},{4,8},{8,4},{12,0},{1,13},{5,9},{9,5},{13,1},{2,14},{6,10},... | collective-permute-start | bytes 116744 | tf_op jit(solution)/shard_map/ppermute | solution.py:297
  23.8 1.1 %out.1 = bf16[8,128,256]{2,1,0:T(8,128)(2,1)} custom-call(bf16[512,128]{1,0:T(8,128)(2,1)S(1)} %get-tuple-element.88.g1_in, bf16[512,128]{1,0:T(8,128)(2,1)S(1)} %get-tuple-element.99.g1_rim, f32[768,256]{1,0:T(8,128)S(1)} %get-tuple-element.100.back_in, f32[256,256]{1,0:T(8,128)S(1)} %get-tuple-element.101.back_rim, ...), custom_call_target="tpu_custom_call" | custom-call | tf_op jit(solution)/shard_map/out/pallas_call | solution.py:395
  24.9 1.7 %collective-permute-done.6 = bf16[152,128]{1,0:T(8,128)(2,1)S(1)} collective-permute-done((bf16[152,128]{1,0:T(8,128)(2,1)S(1)}, bf16[152,128]{1,0:T(8,128)(2,1)S(1)}, u32[]{:S(2)}, u32[]{:S(2)}) %collective-permute-start.6) | collective-permute-done | bytes 38944 | tf_op jit(solution)/shard_map/ppermute | solution.py:297
  26.7 1.0 %collective-permute-start.7 = (bf16[152,128]{1,0:T(8,128)(2,1)S(1)}, bf16[152,128]{1,0:T(8,128)(2,1)S(1)}, u32[]{:S(2)}, u32[]{:S(2)}) collective-permute-start(bf16[152,128]{1,0:T(8,128)(2,1)S(1)} %add_convert_fusion.1), channel_id=1, source_target_pairs={{0,5},{4,1},{8,13},{12,9},{1,4},{5,0},{9,12},{13,8},{2,7},{6,3},{1... | collective-permute-start | bytes 116744 | tf_op jit(solution)/shard_map/ppermute | solution.py:302
  27.6 2.6 %collective-permute-done.7 = bf16[152,128]{1,0:T(8,128)(2,1)S(1)} collective-permute-done((bf16[152,128]{1,0:T(8,128)(2,1)S(1)}, bf16[152,128]{1,0:T(8,128)(2,1)S(1)}, u32[]{:S(2)}, u32[]{:S(2)}) %collective-permute-start.7) | collective-permute-done | bytes 38944 | tf_op jit(solution)/shard_map/ppermute | solution.py:302
  30.2 2.4 %collective-permute-start.8 = (bf16[152,128]{1,0:T(8,128)(2,1)S(1)}, bf16[152,128]{1,0:T(8,128)(2,1)S(1)}, u32[]{:S(2)}, u32[]{:S(2)}) collective-permute-start(bf16[152,128]{1,0:T(8,128)(2,1)S(1)} %add_convert_fusion), channel_id=1, source_target_pairs={{0,6},{4,2},{8,14},{12,10},{1,7},{5,3},{9,15},{13,11},{2,4},{6,0},... | collective-permute-start | bytes 116744 | tf_op jit(solution)/shard_map/ppermute | solution.py:302
  32.7 2.0 %collective-permute-done.8 = bf16[152,128]{1,0:T(8,128)(2,1)S(1)} collective-permute-done((bf16[152,128]{1,0:T(8,128)(2,1)S(1)}, bf16[152,128]{1,0:T(8,128)(2,1)S(1)}, u32[]{:S(2)}, u32[]{:S(2)}) %collective-permute-start.8) | collective-permute-done | bytes 38944 | tf_op jit(solution)/shard_map/ppermute | solution.py:302
  34.7 1.1 %collective-permute-start.9 = (f32[152,128]{1,0:T(8,128)S(1)}, f32[152,128]{1,0:T(8,128)S(1)}, u32[]{:S(2)}, u32[]{:S(2)}) collective-permute-start(f32[152,128]{1,0:T(8,128)S(1)} %convert_add_fusion.a_ref), channel_id=1, source_target_pairs={{0,4},{4,0},{8,12},{12,8},{1,5},{5,1},{9,13},{13,9},{2,6},{6,2},{1... | collective-permute-start | bytes 233480 | tf_op jit(solution)/shard_map/ppermute | solution.py:437
  35.8 0.9 %collective-permute-done.9.b_ref = f32[152,128]{1,0:T(8,128)S(1)} collective-permute-done((f32[152,128]{1,0:T(8,128)S(1)}, f32[152,128]{1,0:T(8,128)S(1)}, u32[]{:S(2)}, u32[]{:S(2)}) %collective-permute-start.9) | collective-permute-done | bytes 77856 | tf_op jit(solution)/shard_map/ppermute | solution.py:437
  36.7 1.2 %last.1 = (f32[128,128]{1,0:T(8,128)}, f32[3,3,4,64]{3,2,1,0:T(4,128)}, f32[64,256]{1,0:T(8,128)}) custom-call(s32[8]{0:T(128)S(1)} %stack.51.pos, f32[152,128]{1,0:T(8,128)S(1)} %convert_add_fusion.a_ref, f32[152,128]{1,0:T(8,128)S(1)} %collective-permute-done.9.b_ref), custom_call_target="tpu_custom_call" | custom-call | tf_op jit(solution)/shard_map/last/pallas_call | solution.py:418
  (13 shorter events, 0.3 us)
Async XLA Ops:
  1.7 6.0 %collective-permute-start = (bf16[16,2,256]{2,1,0:T(2,128)(2,1)S(1)}, bf16[16,2,256]{2,1,0:T(2,128)(2,1)S(1)}, u32[]{:S(2)}, u32[]{:S(2)}) collective-permute-start(bf16[16,2,256]{2,1,0:T(2,128)(2,1)S(1)} %pad_maximum_fusion), channel_id=1, source_target_pairs={{0,1},{1,0},{2,3},{3,2},{4,5},{5,4},{6,7},{7,6},{8,9},{9,8},{10,11... | collective-permute-start | bytes 49160 | tf_op jit(solution)/shard_map/ppermute | solution.py:20
  4.7 3.7 %collective-permute-start.1 = (bf16[16,2,256]{2,1,0:T(2,128)(2,1)S(1)}, bf16[16,2,256]{2,1,0:T(2,128)(2,1)S(1)}, u32[]{:S(2)}, u32[]{:S(2)}) collective-permute-start(bf16[16,2,256]{2,1,0:T(2,128)(2,1)S(1)} %pad_maximum_fusion.1), channel_id=1, source_target_pairs={{0,16},{1,2},{2,1},{3,19},{4,20},{5,6},{6,5},{7,23},{8,24},{9,10},... | collective-permute-start | bytes 49160 | tf_op jit(solution)/shard_map/ppermute | solution.py:32
  9.1 5.4 %collective-permute-start.2 = (bf16[3,144,256]{2,1,0:T(8,128)(2,1)S(1)}, bf16[3,144,256]{2,1,0:T(8,128)(2,1)S(1)}, u32[]{:S(2)}, u32[]{:S(2)}) collective-permute-start(bf16[3,144,256]{2,1,0:T(8,128)(2,1)S(1)} %get-tuple-element.89), channel_id=1, source_target_pairs={{0,4},{4,0},{8,12},{12,8},{1,5},{5,1},{9,13},{13,9},{2,6},{6,2},{1... | collective-permute-start | bytes 663560 | tf_op jit(solution)/shard_map/ppermute | solution.py:20
  9.1 6.0 %collective-permute-start.3 = (bf16[3,144,256]{2,1,0:T(8,128)(2,1)S(1)}, bf16[3,144,256]{2,1,0:T(8,128)(2,1)S(1)}, u32[]{:S(2)}, u32[]{:S(2)}) collective-permute-start(bf16[3,144,256]{2,1,0:T(8,128)(2,1)S(1)} %get-tuple-element.90), channel_id=1, source_target_pairs={{0,16},{1,17},{2,18},{3,19},{4,8},{5,9},{6,10},{7,11},{8,4},{9,5},... | collective-permute-start | bytes 663560 | tf_op jit(solution)/shard_map/ppermute | solution.py:32
  18.0 1.4 %collective-permute-start.4 = (f32[2,152,128]{2,1,0:T(8,128)S(1)}, f32[2,152,128]{2,1,0:T(8,128)S(1)}, u32[]{:S(2)}, u32[]{:S(2)}) collective-permute-start(f32[2,152,128]{2,1,0:T(8,128)S(1)} %slice_bitcast_fusion), channel_id=1, source_target_pairs={{0,4},{4,0},{8,12},{12,8},{1,5},{5,1},{9,13},{13,9},{2,6},{6,2},{1... | collective-permute-start | bytes 466952 | tf_op jit(solution)/shard_map/ppermute | solution.py:393
  19.5 3.6 %collective-permute-start.5 = (bf16[1,152,128]{2,1,0:T(8,128)(2,1)S(1)}, bf16[1,152,128]{2,1,0:T(8,128)(2,1)S(1)}, u32[]{:S(2)}, u32[]{:S(2)}) collective-permute-start(bf16[1,152,128]{2,1,0:T(8,128)(2,1)S(1)} %slice.15), channel_id=1, source_target_pairs={{0,20},{4,16},{8,28},{12,24},{16,4},{20,0},{24,12},{28,8},{1,21},{... | collective-permute-start | bytes 116744 | tf_op jit(solution)/shard_map/ppermute | solution.py:301
  23.1 3.6 %collective-permute-start.6 = (bf16[152,128]{1,0:T(8,128)(2,1)S(1)}, bf16[152,128]{1,0:T(8,128)(2,1)S(1)}, u32[]{:S(2)}, u32[]{:S(2)}) collective-permute-start(bf16[152,128]{1,0:T(8,128)(2,1)S(1)} %fusion.1), channel_id=1, source_target_pairs={{0,12},{4,8},{8,4},{12,0},{1,13},{5,9},{9,5},{13,1},{2,14},{6,10},... | collective-permute-start | bytes 116744 | tf_op jit(solution)/shard_map/ppermute | solution.py:297
  26.7 3.5 %collective-permute-start.7 = (bf16[152,128]{1,0:T(8,128)(2,1)S(1)}, bf16[152,128]{1,0:T(8,128)(2,1)S(1)}, u32[]{:S(2)}, u32[]{:S(2)}) collective-permute-start(bf16[152,128]{1,0:T(8,128)(2,1)S(1)} %add_convert_fusion.1), channel_id=1, source_target_pairs={{0,5},{4,1},{8,13},{12,9},{1,4},{5,0},{9,12},{13,8},{2,7},{6,3},{1... | collective-permute-start | bytes 116744 | tf_op jit(solution)/shard_map/ppermute | solution.py:302
  30.2 4.4 %collective-permute-start.8 = (bf16[152,128]{1,0:T(8,128)(2,1)S(1)}, bf16[152,128]{1,0:T(8,128)(2,1)S(1)}, u32[]{:S(2)}, u32[]{:S(2)}) collective-permute-start(bf16[152,128]{1,0:T(8,128)(2,1)S(1)} %add_convert_fusion), channel_id=1, source_target_pairs={{0,6},{4,2},{8,14},{12,10},{1,7},{5,3},{9,15},{13,11},{2,4},{6,0},... | collective-permute-start | bytes 116744 | tf_op jit(solution)/shard_map/ppermute | solution.py:302
  34.7 2.0 %collective-permute-start.9 = (f32[152,128]{1,0:T(8,128)S(1)}, f32[152,128]{1,0:T(8,128)S(1)}, u32[]{:S(2)}, u32[]{:S(2)}) collective-permute-start(f32[152,128]{1,0:T(8,128)S(1)} %convert_add_fusion.a_ref), channel_id=1, source_target_pairs={{0,4},{4,0},{8,12},{12,8},{1,5},{5,1},{9,13},{13,9},{2,6},{6,2},{1... | collective-permute-start | bytes 233480 | tf_op jit(solution)/shard_map/ppermute | solution.py:437

commit v4 on v3

--- a/solution.py
+++ b/solution.py
@@ -41,9 +41,23 @@
     return 0.5 + 0.5 * jnp.tanh(0.5 * v)
 
 
-def column_mask(pos, wide, cols, inner):
+def parity_of_place():
+    bits = 0
+    for axis in ("dp", "row", "col"):
+        at = lax.axis_index(axis)
+        for k in range((lax.axis_size(axis) - 1).bit_length()):
+            bits = bits + (at >> k)
+    return bits % 2
+
+
+def has_neighbours(axis):
+    at = lax.axis_index(axis)
+    return jnp.where(at > 0, 1.0, 0.0).astype(F32), jnp.where(at < lax.axis_size(axis) - 1, 1.0, 0.0).astype(F32)
+
+
+def column_mask(wide, cols, inner):
     spot = lax.broadcasted_iota(jnp.int32, (wide, inner), 0)
-    has_low, has_high = pos[3].astype(F32), pos[4].astype(F32)
+    has_low, has_high = has_neighbours("col")
     return jnp.where(spot < cols, 1.0, jnp.where(spot < cols + STRIP // 2, has_high, has_low))
 
 
@@ -105,15 +119,16 @@
         copy.wait()
 
 
-def edges_kernel(pos, x_ref, c_ref, col_even, col_odd, strip, even_ref, odd_ref, *, rows, cols):
-    col_is_odd = pos[6] == 1
+def edges_kernel(x_ref, c_ref, col_even, col_odd, strip, even_ref, odd_ref, *, rows, cols):
+    col_is_odd = lax.axis_index("col") % 2 == 1
+    row_is_odd = lax.axis_index("row") % 2
     chans = x_ref.shape[2]
     gap = jnp.zeros((STRIP - 2 * EDGE, chans), F32)
     for r in range(2 * rows):
         a, b = col_even[r].astype(F32), col_odd[r].astype(F32)
         high, low = jnp.where(col_is_odd, b, a), jnp.where(col_is_odd, a, b)
         strip[r] = jnp.concatenate([high, gap, low], axis=0).astype(BF)
-    for ref, sends_high in ((even_ref, pos[0] == 0), (odd_ref, pos[0] == 1)):
+    for ref, sends_high in ((even_ref, row_is_odd == 0), (odd_ref, row_is_odd == 1)):
         at = jnp.where(sends_high, rows - 2, 0)
         cot_at = jnp.where(sends_high, rows - 1, 0)
         for i in range(2):
@@ -124,13 +139,13 @@
 
 
 def inner_kernel(
-    pos, x_ref, c_ref, strip_ref, w1_ref, s1_ref, b1_ref, s2_ref, b2_ref, s3_ref, b3_ref, w2, w2t, w3_ref, w3t_ref,
+    x_ref, c_ref, strip_ref, w1_ref, s1_ref, b1_ref, s2_ref, b2_ref, s3_ref, b3_ref, w2, w2t, w3_ref, w3t_ref,
     acts, gcat, d1, back, g1, gw3_ref, full_ref, gw1t_ref, xs, cs,
     *, rows, cols, chans, inner,
 ):
     wide = cols + STRIP
     step = 2
-    col_ok = column_mask(pos, wide, cols, inner)
+    col_ok = column_mask(wide, cols, inner)
     s1, b1, s2, b2, s3, b3 = (v[...] for v in (s1_ref, b1_ref, s2_ref, b2_ref, s3_ref, b3_ref))
     w1 = w1_ref[...]
     for r in range(rows):
@@ -174,16 +189,16 @@
 
 
 def rim_kernel(
-    pos, x_ref, c_ref, strip_ref, row_even, row_odd, w1_ref, s1_ref, b1_ref, s2_ref, b2_ref, s3_ref, b3_ref, w2, w2t, w3_ref, w3t_ref,
+    x_ref, c_ref, strip_ref, row_even, row_odd, w1_ref, s1_ref, b1_ref, s2_ref, b2_ref, s3_ref, b3_ref, w2, w2t, w3_ref, w3t_ref,
     acts, gcat, d1, gw3_ref, full_ref, gw1t_ref,
     share_ref, g1, back, hacts, hgrad,
     *, rows, cols, chans, inner, group_ch,
 ):
     wide = cols + STRIP
-    col_ok = column_mask(pos, wide, cols, inner)
+    col_ok = column_mask(wide, cols, inner)
     s1, b1, s2, b2, s3, b3 = (v[...] for v in (s1_ref, b1_ref, s2_ref, b2_ref, s3_ref, b3_ref))
-    row_is_odd = pos[0]
-    has_low, has_high = pos[1].astype(F32), pos[2].astype(F32)
+    row_is_odd = lax.axis_index("row") % 2
+    has_low, has_high = has_neighbours("row")
 
     def halo(i, low):
         a, b = row_even[i].astype(F32), row_odd[i].astype(F32)
@@ -239,9 +254,10 @@
     gw1 = (gw1t_ref[...] + dot(g.T, jnp.concatenate([x_ref[p] for p in outs], axis=0))).T
     n_dp = share_ref.shape[1]
     one, three = chans // n_dp, inner // n_dp
-    at = (pos[5], 1 - pos[5])
+    parity = parity_of_place()
+    at = (parity, 1 - parity)
     for h in range(n_dp):
-        slot = h ^ pos[7]
+        slot = h ^ lax.axis_index("dp")
         share_ref[at[0], slot, 0:one, :] = gw1[h * one : (h + 1) * one]
         for k in range(chans // inner):
             share_ref[at[1], slot, k * three : (k + 1) * three, :] = gw3[
@@ -268,9 +284,9 @@
 
 
 def last_kernel(
-    pos, a_ref, b_ref, r_out, g_out, e_out, r_ref, g_ref, e_ref, sems, *, scale, one, three, chans, inner, group_ch
+    a_ref, b_ref, r_out, g_out, e_out, r_ref, g_ref, e_ref, sems, *, scale, one, three, chans, inner, group_ch
 ):
-    other_first = pos[5] == 1
+    other_first = parity_of_place() == 1
     first = jnp.where(other_first, b_ref[...], a_ref[...]) * scale
     second = jnp.where(other_first, a_ref[...], b_ref[...]) * scale
     r_ref[...] = first[0:one]
@@ -311,17 +327,12 @@
     group_ch = group_weight.shape[2]
     x, c = features[0], cotangent[0]
     n_dp, n_row, n_col = (lax.axis_size(a) for a in ("dp", "row", "col"))
-    dp, row, col = (lax.axis_index(a) for a in ("dp", "row", "col"))
-
-    parity = (dp ^ (dp >> 1) ^ (dp >> 2) ^ (dp >> 3) ^ row ^ (row >> 1) ^ (row >> 2) ^ col ^ (col >> 1) ^ (col >> 2)) & 1
-    pos = jnp.stack(
-        [row % 2, row > 0, row < n_row - 1, col > 0, col < n_col - 1, parity, col % 2, dp]
-    ).astype(jnp.int32)
+    col = lax.axis_index("col")
+
     wide = cols + STRIP
     one, three = chans // n_dp, inner // n_dp
     half_rows = one + GROUP_ROWS
     vmem = pl.BlockSpec(memory_space=pltpu.VMEM)
-    smem = pl.BlockSpec(memory_space=pltpu.SMEM)
     params = pltpu.CompilerParams(vmem_limit_bytes=8 << 20)
     sizes = dict(rows=rows, cols=cols, chans=chans)
     shape = jax.ShapeDtypeStruct
@@ -331,7 +342,6 @@
         return jnp.concatenate([lax.dynamic_slice_in_dim(v, start, EDGE, axis=1) for v in (x, c)], axis=0)
 
     to_even, to_odd = col_edge(col % 2 == 0), col_edge(col % 2 == 1)
-    to_even, to_odd, pos = lax.optimization_barrier((to_even, to_odd, pos))
     col_even, col_odd = swap_edges(to_even, to_odd, "col")
     sources = (
         expand_weight, reduce_weight, x, c, scale_one[None], shift_one[None], scale_two[None], shift_two[None],
@@ -352,11 +362,11 @@
     strip, to_even, to_odd = pl.pallas_call(
         functools.partial(edges_kernel, rows=rows, cols=cols),
         out_shape=(shape((2 * rows, STRIP, chans), BF),) + (shape((3, wide, chans), BF),) * 2,
-        in_specs=[smem] + [vmem] * 4,
+        in_specs=[vmem] * 4,
         out_specs=(vmem,) * 3,
         compiler_params=params,
         name="edges",
-    )(pos, x, c, col_even, col_odd)
+    )(x, c, col_even, col_odd)
     row_even, row_odd = swap_edges(to_even, to_odd, "row")
     acts, gcat, d1, back_in, g1_in, gw3, full, gw1t = pl.pallas_call(
         functools.partial(inner_kernel, inner=inner, **sizes),
@@ -370,12 +380,12 @@
             shape((3, inner, 3 * inner), F32),
             shape((inner, chans), F32),
         ),
-        in_specs=[smem] + [vmem] * 14,
+        in_specs=[vmem] * 14,
         out_specs=(vmem,) * 8,
         scratch_shapes=[pltpu.VMEM((rows, wide, chans), BF), pltpu.VMEM((rows, wide, chans), BF)],
         compiler_params=params,
         name="inner",
-    )(pos, x, c, strip, *shared)
+    )(x, c, strip, *shared)
     shares, g1_rim, back_rim = pl.pallas_call(
         functools.partial(rim_kernel, inner=inner, group_ch=group_ch, **sizes),
         out_shape=(
@@ -383,12 +393,12 @@
             shape((4 * cols, inner), BF),
             shape((2 * cols, chans), F32),
         ),
-        in_specs=[smem] + [vmem] * 22,
+        in_specs=[vmem] * 22,
         out_specs=(vmem,) * 3,
         scratch_shapes=[pltpu.VMEM((4, wide, 3 * inner), BF), pltpu.VMEM((4, wide, 3 * inner), BF)],
         compiler_params=params,
         name="rim",
-    )(pos, x, c, strip, row_even, row_odd, *shared, acts, gcat, d1, gw3, full, gw1t)
+    )(x, c, strip, row_even, row_odd, *shared, acts, gcat, d1, gw3, full, gw1t)
     near = [(i, i ^ 1) for i in range(n_row)]
     shares = (shares[0] + lax.ppermute(shares[1], "row", near)).astype(BF)
     g1_rim, shares = lax.optimization_barrier((g1_rim, shares))
@@ -424,7 +434,7 @@
             jax.ShapeDtypeStruct((3, 3, group_ch, three), F32),
             jax.ShapeDtypeStruct((three, chans), F32),
         ),
-        in_specs=[smem, vmem, vmem],
+        in_specs=[vmem, vmem],
         out_specs=(pl.BlockSpec(memory_space=pl.ANY),) * 3,
         scratch_shapes=[
             pltpu.VMEM((one, inner), F32),
@@ -434,7 +444,7 @@
         ],
         compiler_params=pltpu.CompilerParams(vmem_limit_bytes=2 << 20),
         name="last",
-    )(pos, summed, lax.ppermute(summed, "row", near))
+    )(summed, lax.ppermute(summed, "row", near))
     return input_grad[None], reduce_grad, jnp.transpose(group_grad, (3, 0, 1, 2)), expand_grad
 
 

time: 38.1 us -> 36.5 us (0.958)
  Pallas kernels: 11 us -> 8.79 us
  waiting for transfers between devices: 12.2 us -> 12.7 us
    pallas_call x1, Pallas kernels: 2.87 us -> 2.31 us  [body(): pl.pallas_call(functools.partial(rim_kernel, inner=inner, group_ch=group_...]
    pallas_call x1, Pallas kernels: 1.23 us -> 0.69 us  [body(): pl.pallas_call(functools.partial(last_kernel, scale=pixels ** (-0.5), one...]
    pallas_call x1, Pallas kernels: 0.6 us -> 0.06 us  [body(): pl.pallas_call(functools.partial(edges_kernel, rows=rows, cols=cols), out...]
    ppermute x2, waiting for transfers between devices: 1.43 us -> 1.97 us  [swap_edges(): got_odd = lax.ppermute(to_odd, names, perm)]
    pallas_call x1, Pallas kernels: 3.77 us -> 3.23 us  [body(): pl.pallas_call(functools.partial(inner_kernel, inner=inner, **sizes), out...]
  transfers between devices with their start and end apart: 10 -> 10, of which waited for: 8 -> 8; matrix products, arithmetic and copies ran while one was open for 0% -> 0% of each run, Pallas kernels for 17% -> 16%
where the time goes in v4:
time: 36.5 us; the launch traced here: 36.3 us
  starting transfers between devices  13 us (36%)
  waiting for transfers between devices  12.7 us (35%)
  Pallas kernels  8.79 us (24%)
  local copies, waits for them, and re-layouts  0.87 us (2%)
  between operations  0.74 us (2%)
    ppermute x2, waiting for transfers between devices, crossed(): lax.ppermute(value, ('row', 'col'), [(j * count + i, m * count + k) for i...  4.62 us
    ppermute x2, starting transfers between devices, crossed(): lax.ppermute(value, ('row', 'col'), [(j * count + i, m * count + k) for i...  3.38 us
    pallas_call x1, Pallas kernels, body(): pl.pallas_call(functools.partial(inner_kernel, inner=inner, **sizes), out...  3.23 us
    ppermute x2, starting transfers between devices, swap_edges(): got_odd = lax.ppermute(to_odd, names, perm)  3.17 us
    ppermute x2, starting transfers between devices, swap_edges(): got_even = lax.ppermute(to_even, axis, [(i, i ^ 1) for i in range(count)])  3.16 us
    pallas_call x1, Pallas kernels, body(): pl.pallas_call(functools.partial(rim_kernel, inner=inner, group_ch=group_...  2.31 us
    ppermute x1, waiting for transfers between devices, crossed(): lax.ppermute(value, ('dp', 'row'), [(i * n_row + j, k * n_row + m) for i,...  2.22 us
    ppermute x2, waiting for transfers between devices, swap_edges(): got_odd = lax.ppermute(to_odd, names, perm)  1.97 us
  transfers between devices with their start and end apart: 10, of which 8 were waited for; matrix products, arithmetic and copies ran while one was open for 0% of the time, Pallas kernels for 16%

profile of v4, /device:TPU:0, one launch (start us, length us, event | category | flops | bytes accessed | tf_op | source)
XLA Modules:
  0.0 36.3 jit_solution(8735304074192087541)
XLA Ops:
  0.6 0.9 %dynamic-slice_bitcast_fusion = (bf16[8,2,256]{2,1,0:T(2,128)(2,1)S(1)}, bf16[8,2,256]{2,1,0:T(2,128)(2,1)S(1)}, bf16[8,2,256]{2,1,0:T(2,128)(2,1)S(1)}, bf16[8,2,256]{2,1,0:T(2,128)(2,1)S(1)}) fusion(bf16[1,8,128,256]{3,2,1,0:T(8,128)(2,1)} %param.21, s32[]{:T(128)S(6)} %select_n.22, s32[]{:T(128)S(6)} %select_n.21, bf16[1,8,128,256]{3,2,1,0:T(8,128)(2,1)} %param.11), kind=kLoop, calls=%fused_computation.10 | loop fusion | bytes 65544 | tf_op jit(solution)/shard_map/dynamic_slice | solution.py:342
  1.5 3.1 %collective-permute-start = (bf16[16,2,256]{2,1,0:T(2,128)(2,1)S(1)}, bf16[16,2,256]{2,1,0:T(2,128)(2,1)S(1)}, u32[]{:S(2)}, u32[]{:S(2)}) collective-permute-start(bf16[16,2,256]{2,1,0:T(2,128)(2,1)S(1)} %pad_maximum_fusion), channel_id=1, source_target_pairs={{0,1},{1,0},{2,3},{3,2},{4,5},{5,4},{6,7},{7,6},{8,9},{9,8},{10,11... | collective-permute-start | bytes 49160 | tf_op jit(solution)/shard_map/ppermute | solution.py:20
  4.7 1.6 %collective-permute-start.1 = (bf16[16,2,256]{2,1,0:T(2,128)(2,1)S(1)}, bf16[16,2,256]{2,1,0:T(2,128)(2,1)S(1)}, u32[]{:S(2)}, u32[]{:S(2)}) collective-permute-start(bf16[16,2,256]{2,1,0:T(2,128)(2,1)S(1)} %pad_maximum_fusion.1), channel_id=1, source_target_pairs={{0,16},{1,2},{2,1},{3,19},{4,20},{5,6},{6,5},{7,23},{8,24},{9,10},... | collective-permute-start | bytes 49160 | tf_op jit(solution)/shard_map/ppermute | solution.py:32
  6.2 1.4 %load.1 = (bf16[128,256]{1,0:T(8,128)(2,1)S(1)}, bf16[256,128]{1,0:T(8,128)(2,1)S(1)}, bf16[8,128,256]{2,1,0:T(8,128)(2,1)S(1)}, bf16[8,128,256]{2,1,0:T(8,128)(...) custom-call(bf16[3,3,4,128]{3,2,1,0:T(4,128)(2,1)} %refs_0_.1, ...), custom_call_target="tpu_custom_call" | custom-call | tf_op jit(solution)/shard_map/load/pallas_call | solution.py:350
  7.7 0.8 %collective-permute-done.1.col_odd = bf16[16,2,256]{2,1,0:T(2,128)(2,1)S(1)} collective-permute-done((bf16[16,2,256]{2,1,0:T(2,128)(2,1)S(1)}, bf16[16,2,256]{2,1,0:T(2,128)(2,1)S(1)}, u32[]{:S(2)}, u32[]{:S(2)}) %collective-permute-start.1) | collective-permute-done | bytes 16416 | tf_op jit(solution)/shard_map/ppermute | solution.py:32
  8.5 0.1 collective-permute-start.2
  8.6 1.6 %collective-permute-start.3 = (bf16[3,144,256]{2,1,0:T(8,128)(2,1)S(1)}, bf16[3,144,256]{2,1,0:T(8,128)(2,1)S(1)}, u32[]{:S(2)}, u32[]{:S(2)}) collective-permute-start(bf16[3,144,256]{2,1,0:T(8,128)(2,1)S(1)} %get-tuple-element.84), channel_id=1, source_target_pairs={{0,16},{1,17},{2,18},{3,19},{4,8},{5,9},{6,10},{7,11},{8,4},{9,5},... | collective-permute-start | bytes 663560 | tf_op jit(solution)/shard_map/ppermute | solution.py:32
  10.2 3.2 %inner.1 = (bf16[8,144,384]{2,1,0:T(8,128)(2,1)S(1)}, bf16[6,144,384]{2,1,0:T(8,128)(2,1)S(1)}, f32[1024,128]{1,0:T(8,128)S(1)}, f32[768,256]{1,0:T(8,128)S(1)},...) custom-call(bf16[8,128,256]{2,1,0:T(8,128)(2,1)S(1)} %get-tuple-elem, ...), custom_call_target="tpu_custom_call" | custom-call | tf_op jit(solution)/shard_map/inner/pallas_call | solution.py:371
  13.4 1.2 %collective-permute-done.3.row_odd = bf16[3,144,256]{2,1,0:T(8,128)(2,1)S(1)} collective-permute-done((bf16[3,144,256]{2,1,0:T(8,128)(2,1)S(1)}, bf16[3,144,256]{2,1,0:T(8,128)(2,1)S(1)}, u32[]{:S(2)}, u32[]{:S(2)}) %collective-permute-start.3) | collective-permute-done | bytes 221216 | tf_op jit(solution)/shard_map/ppermute | solution.py:32
  14.6 2.3 %rim.1 = (f32[2,2,152,128]{3,2,1,0:T(8,128)S(1)}, bf16[512,128]{1,0:T(8,128)(2,1)S(1)}, f32[256,256]{1,0:T(8,128)S(1)}) custom-call(bf16[8,128,256]{2,1,0:T(8,128)(2,1)S(1)} %get-tuple-element.66.x_ref, bf16[8,128,256]{2,1,0:T(8,128)(2,1)S(1)} %get-tuple-element.67.c_ref, bf16[16,16,256]{2,1,0:T(8,128)(2,1)S(1)} %get-tuple-element.70.strip_ref, ...), custom_call_target="tpu_custom_call" | custom-call | tf_op jit(solution)/shard_map/rim/pallas_call | solution.py:389
  16.9 0.2 collective-permute-start.4
  17.1 1.3 %collective-permute-done.4 = f32[2,152,128]{2,1,0:T(8,128)S(1)} collective-permute-done((f32[2,152,128]{2,1,0:T(8,128)S(1)}, f32[2,152,128]{2,1,0:T(8,128)S(1)}, u32[]{:S(2)}, u32[]{:S(2)}) %collective-permute-start.4) | collective-permute-done | bytes 155680 | tf_op jit(solution)/shard_map/ppermute | solution.py:403
  18.4 1.3 %collective-permute-start.5 = (bf16[1,152,128]{2,1,0:T(8,128)(2,1)S(1)}, bf16[1,152,128]{2,1,0:T(8,128)(2,1)S(1)}, u32[]{:S(2)}, u32[]{:S(2)}) collective-permute-start(bf16[1,152,128]{2,1,0:T(8,128)(2,1)S(1)} %slice.15), channel_id=1, source_target_pairs={{0,20},{4,16},{8,28},{12,24},{16,4},{20,0},{24,12},{28,8},{1,21},{... | collective-permute-start | bytes 116744 | tf_op jit(solution)/shard_map/ppermute | solution.py:317
  19.8 2.2 %collective-permute-done.5 = bf16[1,152,128]{2,1,0:T(8,128)(2,1)S(1)} collective-permute-done((bf16[1,152,128]{2,1,0:T(8,128)(2,1)S(1)}, bf16[1,152,128]{2,1,0:T(8,128)(2,1)S(1)}, u32[]{:S(2)}, u32[]{:S(2)}) %collective-permute-start.5) | collective-permute-done | bytes 38944 | tf_op jit(solution)/shard_map/ppermute | solution.py:317
  22.0 0.7 %collective-permute-start.6 = (bf16[152,128]{1,0:T(8,128)(2,1)S(1)}, bf16[152,128]{1,0:T(8,128)(2,1)S(1)}, u32[]{:S(2)}, u32[]{:S(2)}) collective-permute-start(bf16[152,128]{1,0:T(8,128)(2,1)S(1)} %fusion.1), channel_id=1, source_target_pairs={{0,12},{4,8},{8,4},{12,0},{1,13},{5,9},{9,5},{13,1},{2,14},{6,10},... | collective-permute-start | bytes 116744 | tf_op jit(solution)/shard_map/ppermute | solution.py:313
  22.7 1.1 %out.1 = bf16[8,128,256]{2,1,0:T(8,128)(2,1)} custom-call(bf16[512,128]{1,0:T(8,128)(2,1)S(1)} %get-tuple-element.82.g1_in, bf16[512,128]{1,0:T(8,128)(2,1)S(1)} %get-tuple-element.93.g1_rim, f32[768,256]{1,0:T(8,128)S(1)} %get-tuple-element.94.back_in, f32[256,256]{1,0:T(8,128)S(1)} %get-tuple-element.95.back_rim, bf16[256,128]{1,0:T(8,128)(2,1)S(1)} %get-tuple-element.71.w1_ref), custom_call_target="tpu_custom_call" | custom-call | tf_op jit(solution)/shard_map/out/pallas_call | solution.py:405
  23.8 1.7 %collective-permute-done.6 = bf16[152,128]{1,0:T(8,128)(2,1)S(1)} collective-permute-done((bf16[152,128]{1,0:T(8,128)(2,1)S(1)}, bf16[152,128]{1,0:T(8,128)(2,1)S(1)}, u32[]{:S(2)}, u32[]{:S(2)}) %collective-permute-start.6) | collective-permute-done | bytes 38944 | tf_op jit(solution)/shard_map/ppermute | solution.py:313
  25.6 1.0 %collective-permute-start.7 = (bf16[152,128]{1,0:T(8,128)(2,1)S(1)}, bf16[152,128]{1,0:T(8,128)(2,1)S(1)}, u32[]{:S(2)}, u32[]{:S(2)}) collective-permute-start(bf16[152,128]{1,0:T(8,128)(2,1)S(1)} %add_convert_fusion.1), channel_id=1, source_target_pairs={{0,5},{4,1},{8,13},{12,9},{1,4},{5,0},{9,12},{13,8},{2,7},{6,3},{1... | collective-permute-start | bytes 116744 | tf_op jit(solution)/shard_map/ppermute | solution.py:318
  26.5 2.6 %collective-permute-done.7 = bf16[152,128]{1,0:T(8,128)(2,1)S(1)} collective-permute-done((bf16[152,128]{1,0:T(8,128)(2,1)S(1)}, bf16[152,128]{1,0:T(8,128)(2,1)S(1)}, u32[]{:S(2)}, u32[]{:S(2)}) %collective-permute-start.7) | collective-permute-done | bytes 38944 | tf_op jit(solution)/shard_map/ppermute | solution.py:318
  29.1 2.4 %collective-permute-start.8 = (bf16[152,128]{1,0:T(8,128)(2,1)S(1)}, bf16[152,128]{1,0:T(8,128)(2,1)S(1)}, u32[]{:S(2)}, u32[]{:S(2)}) collective-permute-start(bf16[152,128]{1,0:T(8,128)(2,1)S(1)} %add_convert_fusion), channel_id=1, source_target_pairs={{0,6},{4,2},{8,14},{12,10},{1,7},{5,3},{9,15},{13,11},{2,4},{6,0},... | collective-permute-start | bytes 116744 | tf_op jit(solution)/shard_map/ppermute | solution.py:318
  31.6 2.0 %collective-permute-done.8 = bf16[152,128]{1,0:T(8,128)(2,1)S(1)} collective-permute-done((bf16[152,128]{1,0:T(8,128)(2,1)S(1)}, bf16[152,128]{1,0:T(8,128)(2,1)S(1)}, u32[]{:S(2)}, u32[]{:S(2)}) %collective-permute-start.8) | collective-permute-done | bytes 38944 | tf_op jit(solution)/shard_map/ppermute | solution.py:318
  33.6 1.1 %collective-permute-start.9 = (f32[152,128]{1,0:T(8,128)S(1)}, f32[152,128]{1,0:T(8,128)S(1)}, u32[]{:S(2)}, u32[]{:S(2)}) collective-permute-start(f32[152,128]{1,0:T(8,128)S(1)} %convert_add_fusion.a_ref), channel_id=1, source_target_pairs={{0,4},{4,0},{8,12},{12,8},{1,5},{5,1},{9,13},{13,9},{2,6},{6,2},{1... | collective-permute-start | bytes 233480 | tf_op jit(solution)/shard_map/ppermute | solution.py:447
  34.7 0.9 %collective-permute-done.9.b_ref = f32[152,128]{1,0:T(8,128)S(1)} collective-permute-done((f32[152,128]{1,0:T(8,128)S(1)}, f32[152,128]{1,0:T(8,128)S(1)}, u32[]{:S(2)}, u32[]{:S(2)}) %collective-permute-start.9) | collective-permute-done | bytes 77856 | tf_op jit(solution)/shard_map/ppermute | solution.py:447
  35.6 0.7 %last.1 = (f32[128,128]{1,0:T(8,128)}, f32[3,3,4,64]{3,2,1,0:T(4,128)}, f32[64,256]{1,0:T(8,128)}) custom-call(f32[152,128]{1,0:T(8,128)S(1)} %convert_add_fusion.a_ref, f32[152,128]{1,0:T(8,128)S(1)} %collective-permute-done.9.b_ref), custom_call_target="tpu_custom_call" | custom-call | tf_op jit(solution)/shard_map/last/pallas_call | solution.py:428
  (12 shorter events, 0.2 us)
Async XLA Ops:
  1.5 6.1 %collective-permute-start = (bf16[16,2,256]{2,1,0:T(2,128)(2,1)S(1)}, bf16[16,2,256]{2,1,0:T(2,128)(2,1)S(1)}, u32[]{:S(2)}, u32[]{:S(2)}) collective-permute-start(bf16[16,2,256]{2,1,0:T(2,128)(2,1)S(1)} %pad_maximum_fusion), channel_id=1, source_target_pairs={{0,1},{1,0},{2,3},{3,2},{4,5},{5,4},{6,7},{7,6},{8,9},{9,8},{10,11... | collective-permute-start | bytes 49160 | tf_op jit(solution)/shard_map/ppermute | solution.py:20
  4.7 3.8 %collective-permute-start.1 = (bf16[16,2,256]{2,1,0:T(2,128)(2,1)S(1)}, bf16[16,2,256]{2,1,0:T(2,128)(2,1)S(1)}, u32[]{:S(2)}, u32[]{:S(2)}) collective-permute-start(bf16[16,2,256]{2,1,0:T(2,128)(2,1)S(1)} %pad_maximum_fusion.1), channel_id=1, source_target_pairs={{0,16},{1,2},{2,1},{3,19},{4,20},{5,6},{6,5},{7,23},{8,24},{9,10},... | collective-permute-start | bytes 49160 | tf_op jit(solution)/shard_map/ppermute | solution.py:32
  8.5 4.9 %collective-permute-start.2 = (bf16[3,144,256]{2,1,0:T(8,128)(2,1)S(1)}, bf16[3,144,256]{2,1,0:T(8,128)(2,1)S(1)}, u32[]{:S(2)}, u32[]{:S(2)}) collective-permute-start(bf16[3,144,256]{2,1,0:T(8,128)(2,1)S(1)} %get-tuple-element.83), channel_id=1, source_target_pairs={{0,4},{4,0},{8,12},{12,8},{1,5},{5,1},{9,13},{13,9},{2,6},{6,2},{1... | collective-permute-start | bytes 663560 | tf_op jit(solution)/shard_map/ppermute | solution.py:20
  8.6 6.0 %collective-permute-start.3 = (bf16[3,144,256]{2,1,0:T(8,128)(2,1)S(1)}, bf16[3,144,256]{2,1,0:T(8,128)(2,1)S(1)}, u32[]{:S(2)}, u32[]{:S(2)}) collective-permute-start(bf16[3,144,256]{2,1,0:T(8,128)(2,1)S(1)} %get-tuple-element.84), channel_id=1, source_target_pairs={{0,16},{1,17},{2,18},{3,19},{4,8},{5,9},{6,10},{7,11},{8,4},{9,5},... | collective-permute-start | bytes 663560 | tf_op jit(solution)/shard_map/ppermute | solution.py:32
  16.9 1.4 %collective-permute-start.4 = (f32[2,152,128]{2,1,0:T(8,128)S(1)}, f32[2,152,128]{2,1,0:T(8,128)S(1)}, u32[]{:S(2)}, u32[]{:S(2)}) collective-permute-start(f32[2,152,128]{2,1,0:T(8,128)S(1)} %slice_bitcast_fusion), channel_id=1, source_target_pairs={{0,4},{4,0},{8,12},{12,8},{1,5},{5,1},{9,13},{13,9},{2,6},{6,2},{1... | collective-permute-start | bytes 466952 | tf_op jit(solution)/shard_map/ppermute | solution.py:403
  18.4 3.6 %collective-permute-start.5 = (bf16[1,152,128]{2,1,0:T(8,128)(2,1)S(1)}, bf16[1,152,128]{2,1,0:T(8,128)(2,1)S(1)}, u32[]{:S(2)}, u32[]{:S(2)}) collective-permute-start(bf16[1,152,128]{2,1,0:T(8,128)(2,1)S(1)} %slice.15), channel_id=1, source_target_pairs={{0,20},{4,16},{8,28},{12,24},{16,4},{20,0},{24,12},{28,8},{1,21},{... | collective-permute-start | bytes 116744 | tf_op jit(solution)/shard_map/ppermute | solution.py:317
  22.0 3.6 %collective-permute-start.6 = (bf16[152,128]{1,0:T(8,128)(2,1)S(1)}, bf16[152,128]{1,0:T(8,128)(2,1)S(1)}, u32[]{:S(2)}, u32[]{:S(2)}) collective-permute-start(bf16[152,128]{1,0:T(8,128)(2,1)S(1)} %fusion.1), channel_id=1, source_target_pairs={{0,12},{4,8},{8,4},{12,0},{1,13},{5,9},{9,5},{13,1},{2,14},{6,10},... | collective-permute-start | bytes 116744 | tf_op jit(solution)/shard_map/ppermute | solution.py:313
  25.6 3.5 %collective-permute-start.7 = (bf16[152,128]{1,0:T(8,128)(2,1)S(1)}, bf16[152,128]{1,0:T(8,128)(2,1)S(1)}, u32[]{:S(2)}, u32[]{:S(2)}) collective-permute-start(bf16[152,128]{1,0:T(8,128)(2,1)S(1)} %add_convert_fusion.1), channel_id=1, source_target_pairs={{0,5},{4,1},{8,13},{12,9},{1,4},{5,0},{9,12},{13,8},{2,7},{6,3},{1... | collective-permute-start | bytes 116744 | tf_op jit(solution)/shard_map/ppermute | solution.py:318
  29.1 4.4 %collective-permute-start.8 = (bf16[152,128]{1,0:T(8,128)(2,1)S(1)}, bf16[152,128]{1,0:T(8,128)(2,1)S(1)}, u32[]{:S(2)}, u32[]{:S(2)}) collective-permute-start(bf16[152,128]{1,0:T(8,128)(2,1)S(1)} %add_convert_fusion), channel_id=1, source_target_pairs={{0,6},{4,2},{8,14},{12,10},{1,7},{5,3},{9,15},{13,11},{2,4},{6,0},... | collective-permute-start | bytes 116744 | tf_op jit(solution)/shard_map/ppermute | solution.py:318
  33.6 2.0 %collective-permute-start.9 = (f32[152,128]{1,0:T(8,128)S(1)}, f32[152,128]{1,0:T(8,128)S(1)}, u32[]{:S(2)}, u32[]{:S(2)}) collective-permute-start(f32[152,128]{1,0:T(8,128)S(1)} %convert_add_fusion.a_ref), channel_id=1, source_target_pairs={{0,4},{4,0},{8,12},{12,8},{1,5},{5,1},{9,13},{13,9},{2,6},{6,2},{1... | collective-permute-start | bytes 233480 | tf_op jit(solution)/shard_map/ppermute | solution.py:447

commit v5 on v4

--- a/solution.py
+++ b/solution.py
@@ -26,6 +26,8 @@
         to = list(at)
         if 0 < at[which] < count - 1:
             to[which] = ((at[which] - 1) ^ 1) + 1
+        elif axis == "col":
+            to[1] ^= 1
         elif bands > 1:
             to[0] ^= 1
         perm.append(tuple(functools.reduce(lambda v, k: v * sizes[k] + p[k], range(3), 0) for p in (at, to)))
@@ -68,12 +70,11 @@
     ref[r, :, 2 * inner :] = pltpu.roll(v, wide - 1, 0).astype(BF)
 
 
-def conv3(windows, w_ref):
-    n = w_ref.shape[0] // 3
-    out = dot(windows(0), w_ref[0:n, :])
-    for dh in (1, 2):
-        out = out + dot(windows(dh), w_ref[dh * n : (dh + 1) * n, :])
-    return out
+def conv_pairs(row, starts, w_ref):
+    left = [jnp.concatenate([row(i + j) for j in range(4)], axis=1) for i in starts]
+    out = dot(jnp.concatenate(left, axis=0), w_ref[...])
+    n, inner = left[0].shape[0], w_ref.shape[1] // 2
+    return [out[i * n : (i + 1) * n, k * inner : (k + 1) * inner] for i in range(len(starts)) for k in range(2)]
 
 
 def reduce_act(x, w1, s1, b1):
@@ -95,8 +96,26 @@
     return a2, grad3, back3, grad2
 
 
+def cut_kernel(x_hbm, c_hbm, odd_ref, even_ref, low_ref, high_ref, sems, *, rows, cols):
+    copies = []
+    for i, src in enumerate((x_hbm, c_hbm)):
+        at = slice(i * rows, (i + 1) * rows)
+        copies.append(pltpu.make_async_copy(src.at[:, 0:8, :], low_ref.at[at], sems.at[2 * i]))
+        copies.append(pltpu.make_async_copy(src.at[:, cols - 8 : cols, :], high_ref.at[at], sems.at[2 * i + 1]))
+    for copy in copies:
+        copy.start()
+    is_odd = lax.axis_index("col") % 2 == 1
+    for copy in copies:
+        copy.wait()
+    for r in range(2 * rows):
+        low = low_ref[r].astype(F32)[0:EDGE]
+        high = high_ref[r].astype(F32)[8 - EDGE : 8]
+        even_ref[r] = jnp.where(is_odd, low, high).astype(BF)
+        odd_ref[r] = jnp.where(is_odd, high, low).astype(BF)
+
+
 def load_kernel(*refs, inner, group_ch):
-    sources, targets, (w2, w2t, w3t, gw_ref, sems) = refs[:11], refs[11:21], refs[21:]
+    sources, targets, (w2, w2t, w3t, same, pick, gw_ref, sems) = refs[:11], refs[11:21], refs[21:]
     gw_hbm, sources = sources[0], sources[1:]
     copies = [pltpu.make_async_copy(gw_hbm, gw_ref, sems.at[10])]
     copies += [pltpu.make_async_copy(src, dst, sems.at[i]) for i, (src, dst) in enumerate(zip(sources, targets))]
@@ -111,15 +130,24 @@
         eight = jnp.concatenate([four, four], axis=0)
         tiled = jnp.broadcast_to(eight[None], (inner // 8, 8, inner)).reshape(inner, inner)
         dense = tiled * diag
-        w2[t * inner : (t + 1) * inner, :] = dense.astype(BF)
-        w2t[(8 - t) * inner : (9 - t) * inner, :] = dense.T.astype(BF)
+        for ref, tap, block in ((w2, t, dense.astype(BF)), (w2t, 8 - t, dense.T.astype(BF))):
+            ref[tap * inner : (tap + 1) * inner, 0:inner] = block
+            ref[(tap + 3) * inner : (tap + 4) * inner, inner:] = block
+    for ref in (w2, w2t):
+        ref[9 * inner :, 0:inner] = jnp.zeros((3 * inner, inner), BF)
+        ref[0 : 3 * inner, inner:] = jnp.zeros((3 * inner, inner), BF)
+    for k in range(3):
+        same[:, k * inner : (k + 1) * inner] = diag
+    for t in range(9):
+        place = t * group_ch + sub % group_ch
+        pick[t * inner : (t + 1) * inner, :] = jnp.where(lane == place, 1.0, 0.0).astype(BF)
     copies[1].wait()
     w3t[...] = targets[0][...].T
     for copy in copies[2:]:
         copy.wait()
 
 
-def edges_kernel(x_ref, c_ref, col_even, col_odd, strip, even_ref, odd_ref, *, rows, cols):
+def edges_kernel(x_ref, c_ref, col_odd, col_even, strip, even_ref, odd_ref, *, rows, cols):
     col_is_odd = lax.axis_index("col") % 2 == 1
     row_is_odd = lax.axis_index("row") % 2
     chans = x_ref.shape[2]
@@ -140,7 +168,7 @@
 
 def inner_kernel(
     x_ref, c_ref, strip_ref, w1_ref, s1_ref, b1_ref, s2_ref, b2_ref, s3_ref, b3_ref, w2, w2t, w3_ref, w3t_ref,
-    acts, gcat, d1, back, g1, gw3_ref, full_ref, gw1t_ref, xs, cs,
+    acts, gcat, d1, back, g1, gw3_ref, full_ref, gw1_ref, xt, xs, cs,
     *, rows, cols, chans, inner,
 ):
     wide = cols + STRIP
@@ -162,8 +190,9 @@
             d1[r * cols : (r + 1) * cols, :] = slope[k * wide : k * wide + cols]
     rest = (s2, b2, w3_ref[...], w3t_ref[...], s3, b3)
     gw3 = jnp.zeros((inner, chans), F32)
+    convs = conv_pairs(lambda r: acts[r], range(0, rows - 2, step), w2)
     for p0 in range(1, rows - 1, step):
-        conv = conv3(lambda dh: acts[p0 - 1 + dh : p0 - 1 + dh + step].reshape(step * wide, 3 * inner), w2)
+        conv = jnp.concatenate(convs[p0 - 1 : p0 - 1 + step], axis=0)
         skip = xs[p0 : p0 + step].reshape(step * wide, chans)
         ct = cs[p0 : p0 + step].reshape(step * wide, chans)
         a2, grad3, back3, grad2 = through(conv, skip, ct, *rest)
@@ -180,18 +209,21 @@
     for dh in range(3):
         full_ref[dh] = dot(own_gt, acts[dh : dh + rows - 2, 0:cols, :].reshape(n, 3 * inner))
     gw1t = jnp.zeros((inner, chans), F32)
+    convs = conv_pairs(lambda r: gcat[r, 0:cols, :], range(0, rows - 4, step), w2t)
     for p0 in range(2, rows - 2, step):
-        conv = conv3(lambda dh: gcat[p0 - 2 + dh : p0 - 2 + dh + step, 0:cols, :].reshape(step * cols, 3 * inner), w2t)
+        conv = jnp.concatenate(convs[p0 - 2 : p0 - 2 + step], axis=0)
         g = (conv * d1[p0 * cols : (p0 + step) * cols, :]).astype(BF)
         g1[(p0 - 2) * cols : (p0 - 2 + step) * cols, :] = g
         gw1t = gw1t + dot(g.T, x_ref[p0 : p0 + step].reshape(step * cols, chans))
-    gw1t_ref[...] = gw1t
+    gw1_ref[...] = gw1t.T
+    for k, p in enumerate((0, 1, rows - 2, rows - 1)):
+        xt[:, k * cols : (k + 1) * cols] = x_ref[p].T
 
 
 def rim_kernel(
     x_ref, c_ref, strip_ref, row_even, row_odd, w1_ref, s1_ref, b1_ref, s2_ref, b2_ref, s3_ref, b3_ref, w2, w2t, w3_ref, w3t_ref,
-    acts, gcat, d1, gw3_ref, full_ref, gw1t_ref,
-    share_ref, g1, back, hacts, hgrad,
+    acts, gcat, d1, gw3_ref, full_ref, gw1_ref, xt, same, pick,
+    share_ref, g1, back, hacts, hgrad, far_ref,
     *, rows, cols, chans, inner, group_ch,
 ):
     wide = cols + STRIP
@@ -200,25 +232,29 @@
     row_is_odd = lax.axis_index("row") % 2
     has_low, has_high = has_neighbours("row")
 
-    def halo(i, low):
-        a, b = row_even[i].astype(F32), row_odd[i].astype(F32)
-        take_odd = (row_is_odd == 0) if low else (row_is_odd == 1)
-        return jnp.where(take_odd, b, a).astype(BF)
+    @pl.when(row_is_odd == 0)
+    def _():
+        far_ref[0:3] = row_odd[...]
+        far_ref[3:6] = row_even[...]
+
+    @pl.when(row_is_odd == 1)
+    def _():
+        far_ref[0:3] = row_even[...]
+        far_ref[3:6] = row_odd[...]
 
     def wider(ref, r, base):
         return jnp.concatenate([ref[r], strip_ref[base + r]], axis=0)
 
-    far = [halo(0, True), halo(1, True), halo(0, False), halo(1, False)]
+    far = [far_ref[i] for i in (0, 1, 3, 4)]
     act, _ = reduce_act(jnp.concatenate(far, axis=0), w1_ref[...], s1, b1)
     for k in range(4):
         spread(hacts, k, act[k * wide : (k + 1) * wide] * (col_ok * (has_low if k < 2 else has_high)))
     def act_row(r):
         return hacts[r] if r < 2 else acts[r - 2] if r < rows + 2 else hacts[r - rows]
 
-    mids = (0, 1, rows, rows + 1)
-    conv = conv3(lambda dh: jnp.concatenate([act_row(q + dh) for q in mids], axis=0), w2)
+    conv = jnp.concatenate(conv_pairs(act_row, (0, rows), w2), axis=0)
     skip = jnp.concatenate([far[1], wider(x_ref, 0, 0), wider(x_ref, rows - 1, 0), far[2]], axis=0)
-    ct = jnp.concatenate([halo(2, True), wider(c_ref, 0, rows), wider(c_ref, rows - 1, rows), halo(2, False)], axis=0)
+    ct = jnp.concatenate([far_ref[2], wider(c_ref, 0, rows), wider(c_ref, rows - 1, rows), far_ref[5]], axis=0)
     a2, grad3, back3, grad2 = through(conv, skip, ct, s2, b2, w3_ref[...], w3t_ref[...], s3, b3)
     for k in range(4):
         g = grad2[k * wide : (k + 1) * wide] * col_ok
@@ -229,29 +265,23 @@
     gw3 = gw3_ref[...] + dot(
         jnp.concatenate([a2[at] for at in own], axis=0).T, jnp.concatenate([grad3[at] for at in own], axis=0)
     )
+    def grad_row(q):
+        return (hgrad[q] if q < 2 else gcat[q - 2] if q < rows else hgrad[q - rows + 2])[0:cols]
+
+    outs = (0, 1, rows - 2, rows - 1)
+    conv = jnp.concatenate(conv_pairs(grad_row, (0, rows - 2), w2t), axis=0)
+    slope = jnp.concatenate([d1[0 : 2 * cols, :], d1[(rows - 2) * cols :, :]], axis=0)
+    g = (conv * slope).astype(BF)
+    g1[...] = g
     own_gt = jnp.concatenate([hgrad[k, 0:cols, inner : 2 * inner] for k in (1, 2)], axis=0).T
-    sub = lax.broadcasted_iota(jnp.int32, (inner, 3 * inner), 0)
-    lane = lax.broadcasted_iota(jnp.int32, (inner, 3 * inner), 1)
-    same = jnp.where(sub // group_ch == (lane % inner) // group_ch, 1.0, 0.0).astype(F32)
-    pick_sub = lax.broadcasted_iota(jnp.int32, (3 * inner, inner), 0)
-    pick_lane = lax.broadcasted_iota(jnp.int32, (3 * inner, inner), 1)
     compact = jnp.zeros((inner, inner), F32)
     for dh in range(3):
         near = jnp.concatenate([act_row(q + dh)[0:cols] for q in (1, rows)], axis=0)
-        full = ((full_ref[dh] + dot(own_gt, near)) * same).astype(BF)
-        place = (dh * 3 + pick_sub // inner) * group_ch + pick_sub % group_ch
-        compact = compact + dot(full, jnp.where(pick_lane == place, 1.0, 0.0).astype(BF))
+        full = ((full_ref[dh] + dot(own_gt, near)) * same[...]).astype(BF)
+        compact = compact + dot(full, pick[dh * 3 * inner : (dh + 1) * 3 * inner, :])
     gw2 = compact.T
 
-    def grad_row(q):
-        return (hgrad[q] if q < 2 else gcat[q - 2] if q < rows else hgrad[q - rows + 2])[0:cols]
-
-    outs = (0, 1, rows - 2, rows - 1)
-    conv = conv3(lambda dh: jnp.concatenate([grad_row(p + dh) for p in outs], axis=0), w2t)
-    slope = jnp.concatenate([d1[0 : 2 * cols, :], d1[(rows - 2) * cols :, :]], axis=0)
-    g = (conv * slope).astype(BF)
-    g1[...] = g
-    gw1 = (gw1t_ref[...] + dot(g.T, jnp.concatenate([x_ref[p] for p in outs], axis=0))).T
+    gw1 = gw1_ref[...] + dot(xt[...], g)
     n_dp = share_ref.shape[1]
     one, three = chans // n_dp, inner // n_dp
     parity = parity_of_place()
@@ -327,7 +357,6 @@
     group_ch = group_weight.shape[2]
     x, c = features[0], cotangent[0]
     n_dp, n_row, n_col = (lax.axis_size(a) for a in ("dp", "row", "col"))
-    col = lax.axis_index("col")
 
     wide = cols + STRIP
     one, three = chans // n_dp, inner // n_dp
@@ -337,28 +366,34 @@
     sizes = dict(rows=rows, cols=cols, chans=chans)
     shape = jax.ShapeDtypeStruct
 
-    def col_edge(high):
-        start = jnp.where(high, cols - EDGE, 0)
-        return jnp.concatenate([lax.dynamic_slice_in_dim(v, start, EDGE, axis=1) for v in (x, c)], axis=0)
-
-    to_even, to_odd = col_edge(col % 2 == 0), col_edge(col % 2 == 1)
+    x, c = (pltpu.with_memory_space_constraint(v, pltpu.HBM) for v in (x, c))
+    to_odd, to_even = pl.pallas_call(
+        functools.partial(cut_kernel, rows=rows, cols=cols),
+        out_shape=(shape((2 * rows, EDGE, chans), BF),) * 2,
+        in_specs=[pl.BlockSpec(memory_space=pltpu.HBM)] * 2,
+        out_specs=(vmem,) * 2,
+        scratch_shapes=[pltpu.VMEM((2 * rows, 8, chans), BF)] * 2 + [pltpu.SemaphoreType.DMA((4,))],
+        compiler_params=params,
+        name="cut",
+    )(x, c)
     col_even, col_odd = swap_edges(to_even, to_odd, "col")
     sources = (
         expand_weight, reduce_weight, x, c, scale_one[None], shift_one[None], scale_two[None], shift_two[None],
         scale_three[None], shift_three[None],
     )
-    w3, w1, x, c, *vecs, w2, w2t, w3t = pl.pallas_call(
+    w3, w1, x, c, *vecs, w2, w2t, w3t, same, pick = pl.pallas_call(
         functools.partial(load_kernel, inner=inner, group_ch=group_ch),
         out_shape=tuple(shape(v.shape, v.dtype) for v in sources)
-        + (shape((9 * inner, inner), BF), shape((9 * inner, inner), BF), shape((chans, inner), BF)),
+        + (shape((12 * inner, 2 * inner), BF), shape((12 * inner, 2 * inner), BF), shape((chans, inner), BF))
+        + (shape((inner, 3 * inner), F32), shape((9 * inner, inner), BF)),
         in_specs=[pl.BlockSpec(memory_space=pltpu.HBM)] * 11,
-        out_specs=(vmem,) * 13,
+        out_specs=(vmem,) * 15,
         scratch_shapes=[pltpu.VMEM(group_weight.shape, BF), pltpu.SemaphoreType.DMA((11,))],
         compiler_params=params,
         name="load",
     )(*(pltpu.with_memory_space_constraint(v, pltpu.HBM) for v in (group_weight, *sources)))
     shared = (w1, *vecs, w2, w2t, w3, w3t)
-    col_even, col_odd, shared, x, c = lax.optimization_barrier((col_even, col_odd, shared, x, c))
+    col_odd, col_even, shared, x, c = lax.optimization_barrier((col_odd, col_even, shared, x, c))
     strip, to_even, to_odd = pl.pallas_call(
         functools.partial(edges_kernel, rows=rows, cols=cols),
         out_shape=(shape((2 * rows, STRIP, chans), BF),) + (shape((3, wide, chans), BF),) * 2,
@@ -366,9 +401,9 @@
         out_specs=(vmem,) * 3,
         compiler_params=params,
         name="edges",
-    )(x, c, col_even, col_odd)
+    )(x, c, col_odd, col_even)
     row_even, row_odd = swap_edges(to_even, to_odd, "row")
-    acts, gcat, d1, back_in, g1_in, gw3, full, gw1t = pl.pallas_call(
+    acts, gcat, d1, back_in, g1_in, gw3, full, gw1, xt = pl.pallas_call(
         functools.partial(inner_kernel, inner=inner, **sizes),
         out_shape=(
             shape((rows, wide, 3 * inner), BF),
@@ -378,10 +413,11 @@
             shape(((rows - 4) * cols, inner), BF),
             shape((inner, chans), F32),
             shape((3, inner, 3 * inner), F32),
-            shape((inner, chans), F32),
+            shape((chans, inner), F32),
+            shape((chans, 4 * cols), BF),
         ),
         in_specs=[vmem] * 14,
-        out_specs=(vmem,) * 8,
+        out_specs=(vmem,) * 9,
         scratch_shapes=[pltpu.VMEM((rows, wide, chans), BF), pltpu.VMEM((rows, wide, chans), BF)],
         compiler_params=params,
         name="inner",
@@ -393,12 +429,12 @@
             shape((4 * cols, inner), BF),
             shape((2 * cols, chans), F32),
         ),
-        in_specs=[vmem] * 22,
+        in_specs=[vmem] * 25,
         out_specs=(vmem,) * 3,
-        scratch_shapes=[pltpu.VMEM((4, wide, 3 * inner), BF), pltpu.VMEM((4, wide, 3 * inner), BF)],
+        scratch_shapes=[pltpu.VMEM((4, wide, 3 * inner), BF)] * 2 + [pltpu.VMEM((6, wide, chans), BF)],
         compiler_params=params,
         name="rim",
-    )(x, c, strip, row_even, row_odd, *shared, acts, gcat, d1, gw3, full, gw1t)
+    )(x, c, strip, row_even, row_odd, *shared, acts, gcat, d1, gw3, full, gw1, xt, same, pick)
     near = [(i, i ^ 1) for i in range(n_row)]
     shares = (shares[0] + lax.ppermute(shares[1], "row", near)).astype(BF)
     g1_rim, shares = lax.optimization_barrier((g1_rim, shares))

time: 36.5 us -> 35 us (0.959)
  local copies, waits for them, and re-layouts: 0.87 us -> 0.02 us
  waiting for transfers between devices: 12.7 us -> 12 us
  Pallas kernels: 8.79 us -> 9.28 us
  starting transfers between devices: 13 us -> 12.6 us
    ppermute x2, starting transfers between devices: 3.17 us -> 2.1 us  [swap_edges(): got_odd = lax.ppermute(to_odd, names, perm)]
    ppermute x2, starting transfers between devices: 3.16 us -> 4.22 us  [swap_edges(): got_even = lax.ppermute(to_even, axis, [(i, i ^ 1) for i in range(count)])]
    pallas_call x0 -> x1, Pallas kernels: none -> 0.89 us  [body(): pl.pallas_call(functools.partial(cut_kernel, rows=rows, cols=cols), out_s...]
    dynamic_slice x1 -> x0, local copies, waits for them, and re-layouts: 0.85 us -> none  [col_edge(): lax.dynamic_slice_in_dim(v, start, EDGE, axis=1)]
    ppermute x1, starting transfers between devices: 1.06 us -> 0.42 us  [body(): lax.ppermute(summed, 'row', near)]
    ppermute x2, waiting for transfers between devices: 1.97 us -> 1.35 us  [swap_edges(): got_odd = lax.ppermute(to_odd, names, perm)]
where the time goes in v5:
time: 35 us; the launch traced here: 34.8 us
  starting transfers between devices  12.6 us (36%)
  waiting for transfers between devices  12 us (34%)
  Pallas kernels  9.28 us (27%)
  between operations  0.72 us (2%)
    ppermute x2, waiting for transfers between devices, crossed(): lax.ppermute(value, ('row', 'col'), [(j * count + i, m * count + k) for i...  4.26 us
    ppermute x2, starting transfers between devices, swap_edges(): got_even = lax.ppermute(to_even, axis, [(i, i ^ 1) for i in range(count)])  4.22 us
    ppermute x2, starting transfers between devices, crossed(): lax.ppermute(value, ('row', 'col'), [(j * count + i, m * count + k) for i...  3.62 us
    pallas_call x1, Pallas kernels, body(): pl.pallas_call(functools.partial(inner_kernel, inner=inner, **sizes), out...  3.04 us
    ppermute x1, waiting for transfers between devices, crossed(): lax.ppermute(value, ('dp', 'row'), [(i * n_row + j, k * n_row + m) for i,...  2.22 us
    ppermute x2, starting transfers between devices, swap_edges(): got_odd = lax.ppermute(to_odd, names, perm)  2.1 us
    pallas_call x1, Pallas kernels, body(): pl.pallas_call(functools.partial(rim_kernel, inner=inner, group_ch=group_...  2.1 us
    ppermute x1, waiting for transfers between devices, crossed(): return lax.ppermute(value, 'row', [(i, i ^ bit ^ 1) for i in range(n_row)])  1.72 us
  transfers between devices with their start and end apart: 10, of which 8 were waited for; matrix products, arithmetic and copies ran while one was open for 0% of the time, Pallas kernels for 16%

profile of v5, /device:TPU:0, one launch (start us, length us, event | category | flops | bytes accessed | tf_op | source)
XLA Modules:
  0.0 34.8 jit_solution(14097239488614267680)
XLA Ops:
  0.6 0.9 %cut.1 = (bf16[16,2,256]{2,1,0:T(2,128)(2,1)S(1)}, bf16[16,2,256]{2,1,0:T(2,128)(2,1)S(1)}) custom-call(bf16[8,128,256]{2,1,0:T(8,128)(2,1)} %bitcast.18, bf16[8,128,256]{2,1,0:T(8,128)(2,1)} %bitcast.20), custom_call_target="tpu_custom_call" | custom-call | tf_op jit(solution)/shard_map/cut/pallas_call | solution.py:370
  1.5 0.5 %collective-permute-start = (bf16[16,2,256]{2,1,0:T(2,128)(2,1)S(1)}, bf16[16,2,256]{2,1,0:T(2,128)(2,1)S(1)}, u32[]{:S(2)}, u32[]{:S(2)}) collective-permute-start(bf16[16,2,256]{2,1,0:T(2,128)(2,1)S(1)} %get-tuple-element.58), channel_id=1, source_target_pairs={{0,4},{1,2},{2,1},{3,7},{4,0},{5,6},{6,5},{7,3},{8,12},{9,10},{10,... | collective-permute-start | bytes 49160 | tf_op jit(solution)/shard_map/ppermute | solution.py:34
  2.0 4.1 %collective-permute-start.1 = (bf16[16,2,256]{2,1,0:T(2,128)(2,1)S(1)}, bf16[16,2,256]{2,1,0:T(2,128)(2,1)S(1)}, u32[]{:S(2)}, u32[]{:S(2)}) collective-permute-start(bf16[16,2,256]{2,1,0:T(2,128)(2,1)S(1)} %get-tuple-element.59), channel_id=1, source_target_pairs={{0,1},{1,0},{2,3},{3,2},{4,5},{5,4},{6,7},{7,6},{8,9},{9,8},{10,11... | collective-permute-start | bytes 49160 | tf_op jit(solution)/shard_map/ppermute | solution.py:20
  6.2 1.4 %load.1 = (bf16[128,256]{1,0:T(8,128)(2,1)S(1)}, bf16[256,128]{1,0:T(8,128)(2,1)S(1)}, bf16[8,128,256]{2,1,0:T(8,128)(2,1)S(1)}, bf16[8,128,256]{2,1,0:T(8,128)(...) custom-call(bf16[3,3,4,128]{3,2,1,0:T(4,128)(2,1)} %refs_0_.1, ...), custom_call_target="tpu_custom_call" | custom-call | tf_op jit(solution)/shard_map/load/pallas_call | solution.py:384
  7.6 0.3 collective-permute-done.1.col_even
  8.0 0.1 collective-permute-start.2
  8.1 1.6 %collective-permute-start.3 = (bf16[3,144,256]{2,1,0:T(8,128)(2,1)S(1)}, bf16[3,144,256]{2,1,0:T(8,128)(2,1)S(1)}, u32[]{:S(2)}, u32[]{:S(2)}) collective-permute-start(bf16[3,144,256]{2,1,0:T(8,128)(2,1)S(1)} %get-tuple-element.91), channel_id=1, source_target_pairs={{0,16},{1,17},{2,18},{3,19},{4,8},{5,9},{6,10},{7,11},{8,4},{9,5},... | collective-permute-start | bytes 663560 | tf_op jit(solution)/shard_map/ppermute | solution.py:34
  9.6 3.0 %inner.1 = (bf16[8,144,384]{2,1,0:T(8,128)(2,1)S(1)}, bf16[6,144,384]{2,1,0:T(8,128)(2,1)S(1)}, f32[1024,128]{1,0:T(8,128)S(1)}, f32[768,256]{1,0:T(8,128)S(1)},...) custom-call(bf16[8,128,256]{2,1,0:T(8,128)(2,1)S(1)} %get-tuple-elem, ...), custom_call_target="tpu_custom_call" | custom-call | tf_op jit(solution)/shard_map/inner/pallas_call | solution.py:406
  12.7 1.4 %collective-permute-done.3.row_odd = bf16[3,144,256]{2,1,0:T(8,128)(2,1)S(1)} collective-permute-done((bf16[3,144,256]{2,1,0:T(8,128)(2,1)S(1)}, bf16[3,144,256]{2,1,0:T(8,128)(2,1)S(1)}, u32[]{:S(2)}, u32[]{:S(2)}) %collective-permute-start.3) | collective-permute-done | bytes 221216 | tf_op jit(solution)/shard_map/ppermute | solution.py:34
  14.1 2.1 %rim.1 = (f32[2,2,152,128]{3,2,1,0:T(8,128)S(1)}, bf16[512,128]{1,0:T(8,128)(2,1)S(1)}, f32[256,256]{1,0:T(8,128)S(1)}) custom-call(bf16[8,128,256]{2,1,0:T(8,128)(2,1)S(1)} %get-tuple-element.73.x_ref, bf16[8,128,256]{2,1,0:T(8,128)(2,1)S(1)} %get-tuple-element.74.c_ref, bf16[16,16,256]{2,1,0:T(8,128)(2,1)S(1)} %get-tuple-element.77.strip_ref, ...), custom_call_target="tpu_custom_call" | custom-call | tf_op jit(solution)/shard_map/rim/pallas_call | solution.py:425
  16.2 0.2 collective-permute-start.4
  16.4 1.3 %collective-permute-done.4 = f32[2,152,128]{2,1,0:T(8,128)S(1)} collective-permute-done((f32[2,152,128]{2,1,0:T(8,128)S(1)}, f32[2,152,128]{2,1,0:T(8,128)S(1)}, u32[]{:S(2)}, u32[]{:S(2)}) %collective-permute-start.4) | collective-permute-done | bytes 155680 | tf_op jit(solution)/shard_map/ppermute | solution.py:439
  17.7 1.3 %collective-permute-start.5 = (bf16[1,152,128]{2,1,0:T(8,128)(2,1)S(1)}, bf16[1,152,128]{2,1,0:T(8,128)(2,1)S(1)}, u32[]{:S(2)}, u32[]{:S(2)}) collective-permute-start(bf16[1,152,128]{2,1,0:T(8,128)(2,1)S(1)} %slice.15), channel_id=1, source_target_pairs={{0,20},{4,16},{8,28},{12,24},{16,4},{20,0},{24,12},{28,8},{1,21},{... | collective-permute-start | bytes 116744 | tf_op jit(solution)/shard_map/ppermute | solution.py:347
  19.0 2.2 %collective-permute-done.5 = bf16[1,152,128]{2,1,0:T(8,128)(2,1)S(1)} collective-permute-done((bf16[1,152,128]{2,1,0:T(8,128)(2,1)S(1)}, bf16[1,152,128]{2,1,0:T(8,128)(2,1)S(1)}, u32[]{:S(2)}, u32[]{:S(2)}) %collective-permute-start.5) | collective-permute-done | bytes 38944 | tf_op jit(solution)/shard_map/ppermute | solution.py:347
  21.2 0.7 %collective-permute-start.6 = (bf16[152,128]{1,0:T(8,128)(2,1)S(1)}, bf16[152,128]{1,0:T(8,128)(2,1)S(1)}, u32[]{:S(2)}, u32[]{:S(2)}) collective-permute-start(bf16[152,128]{1,0:T(8,128)(2,1)S(1)} %fusion.1), channel_id=1, source_target_pairs={{0,12},{4,8},{8,4},{12,0},{1,13},{5,9},{9,5},{13,1},{2,14},{6,10},... | collective-permute-start | bytes 116744 | tf_op jit(solution)/shard_map/ppermute | solution.py:343
  22.0 1.1 %out.1 = bf16[8,128,256]{2,1,0:T(8,128)(2,1)} custom-call(bf16[512,128]{1,0:T(8,128)(2,1)S(1)} %get-tuple-element.89.g1_in, bf16[512,128]{1,0:T(8,128)(2,1)S(1)} %get-tuple-element.103.g1_rim, f32[768,256]{1,0:T(8,128)S(1)} %get-tuple-element.104.back_in, f32[256,256]{1,0:T(8,128)S(1)} %get-tuple-element.105.back_rim, ...), custom_call_target="tpu_custom_call" | custom-call | tf_op jit(solution)/shard_map/out/pallas_call | solution.py:441
  23.1 1.7 %collective-permute-done.6 = bf16[152,128]{1,0:T(8,128)(2,1)S(1)} collective-permute-done((bf16[152,128]{1,0:T(8,128)(2,1)S(1)}, bf16[152,128]{1,0:T(8,128)(2,1)S(1)}, u32[]{:S(2)}, u32[]{:S(2)}) %collective-permute-start.6) | collective-permute-done | bytes 38944 | tf_op jit(solution)/shard_map/ppermute | solution.py:343
  24.8 1.8 %collective-permute-start.7 = (bf16[152,128]{1,0:T(8,128)(2,1)S(1)}, bf16[152,128]{1,0:T(8,128)(2,1)S(1)}, u32[]{:S(2)}, u32[]{:S(2)}) collective-permute-start(bf16[152,128]{1,0:T(8,128)(2,1)S(1)} %add_convert_fusion.1), channel_id=1, source_target_pairs={{0,5},{4,1},{8,13},{12,9},{1,4},{5,0},{9,12},{13,8},{2,7},{6,3},{1... | collective-permute-start | bytes 116744 | tf_op jit(solution)/shard_map/ppermute | solution.py:348
  26.7 1.7 %collective-permute-done.7 = bf16[152,128]{1,0:T(8,128)(2,1)S(1)} collective-permute-done((bf16[152,128]{1,0:T(8,128)(2,1)S(1)}, bf16[152,128]{1,0:T(8,128)(2,1)S(1)}, u32[]{:S(2)}, u32[]{:S(2)}) %collective-permute-start.7) | collective-permute-done | bytes 38944 | tf_op jit(solution)/shard_map/ppermute | solution.py:348
  28.3 1.8 %collective-permute-start.8 = (bf16[152,128]{1,0:T(8,128)(2,1)S(1)}, bf16[152,128]{1,0:T(8,128)(2,1)S(1)}, u32[]{:S(2)}, u32[]{:S(2)}) collective-permute-start(bf16[152,128]{1,0:T(8,128)(2,1)S(1)} %add_convert_fusion), channel_id=1, source_target_pairs={{0,6},{4,2},{8,14},{12,10},{1,7},{5,3},{9,15},{13,11},{2,4},{6,0},... | collective-permute-start | bytes 116744 | tf_op jit(solution)/shard_map/ppermute | solution.py:348
  30.1 2.6 %collective-permute-done.8 = bf16[152,128]{1,0:T(8,128)(2,1)S(1)} collective-permute-done((bf16[152,128]{1,0:T(8,128)(2,1)S(1)}, bf16[152,128]{1,0:T(8,128)(2,1)S(1)}, u32[]{:S(2)}, u32[]{:S(2)}) %collective-permute-start.8) | collective-permute-done | bytes 38944 | tf_op jit(solution)/shard_map/ppermute | solution.py:348
  32.7 0.4 %collective-permute-start.9 = (f32[152,128]{1,0:T(8,128)S(1)}, f32[152,128]{1,0:T(8,128)S(1)}, u32[]{:S(2)}, u32[]{:S(2)}) collective-permute-start(f32[152,128]{1,0:T(8,128)S(1)} %convert_add_fusion.a_ref), channel_id=1, source_target_pairs={{0,4},{4,0},{8,12},{12,8},{1,5},{5,1},{9,13},{13,9},{2,6},{6,2},{1... | collective-permute-start | bytes 233480 | tf_op jit(solution)/shard_map/ppermute | solution.py:483
  33.1 0.9 %collective-permute-done.9.b_ref = f32[152,128]{1,0:T(8,128)S(1)} collective-permute-done((f32[152,128]{1,0:T(8,128)S(1)}, f32[152,128]{1,0:T(8,128)S(1)}, u32[]{:S(2)}, u32[]{:S(2)}) %collective-permute-start.9) | collective-permute-done | bytes 77856 | tf_op jit(solution)/shard_map/ppermute | solution.py:483
  34.1 0.7 %last.1 = (f32[128,128]{1,0:T(8,128)}, f32[3,3,4,64]{3,2,1,0:T(4,128)}, f32[64,256]{1,0:T(8,128)}) custom-call(f32[152,128]{1,0:T(8,128)S(1)} %convert_add_fusion.a_ref, f32[152,128]{1,0:T(8,128)S(1)} %collective-permute-done.9.b_ref), custom_call_target="tpu_custom_call" | custom-call | tf_op jit(solution)/shard_map/last/pallas_call | solution.py:464
  (10 shorter events, 0.2 us)
Async XLA Ops:
  1.5 6.1 %collective-permute-start = (bf16[16,2,256]{2,1,0:T(2,128)(2,1)S(1)}, bf16[16,2,256]{2,1,0:T(2,128)(2,1)S(1)}, u32[]{:S(2)}, u32[]{:S(2)}) collective-permute-start(bf16[16,2,256]{2,1,0:T(2,128)(2,1)S(1)} %get-tuple-element.58), channel_id=1, source_target_pairs={{0,4},{1,2},{2,1},{3,7},{4,0},{5,6},{6,5},{7,3},{8,12},{9,10},{10,... | collective-permute-start | bytes 49160 | tf_op jit(solution)/shard_map/ppermute | solution.py:34
  2.0 5.9 %collective-permute-start.1 = (bf16[16,2,256]{2,1,0:T(2,128)(2,1)S(1)}, bf16[16,2,256]{2,1,0:T(2,128)(2,1)S(1)}, u32[]{:S(2)}, u32[]{:S(2)}) collective-permute-start(bf16[16,2,256]{2,1,0:T(2,128)(2,1)S(1)} %get-tuple-element.59), channel_id=1, source_target_pairs={{0,1},{1,0},{2,3},{3,2},{4,5},{5,4},{6,7},{7,6},{8,9},{9,8},{10,11... | collective-permute-start | bytes 49160 | tf_op jit(solution)/shard_map/ppermute | solution.py:20
  8.0 4.7 %collective-permute-start.2 = (bf16[3,144,256]{2,1,0:T(8,128)(2,1)S(1)}, bf16[3,144,256]{2,1,0:T(8,128)(2,1)S(1)}, u32[]{:S(2)}, u32[]{:S(2)}) collective-permute-start(bf16[3,144,256]{2,1,0:T(8,128)(2,1)S(1)} %get-tuple-element.90), channel_id=1, source_target_pairs={{0,4},{4,0},{8,12},{12,8},{1,5},{5,1},{9,13},{13,9},{2,6},{6,2},{1... | collective-permute-start | bytes 663560 | tf_op jit(solution)/shard_map/ppermute | solution.py:20
  8.1 6.0 %collective-permute-start.3 = (bf16[3,144,256]{2,1,0:T(8,128)(2,1)S(1)}, bf16[3,144,256]{2,1,0:T(8,128)(2,1)S(1)}, u32[]{:S(2)}, u32[]{:S(2)}) collective-permute-start(bf16[3,144,256]{2,1,0:T(8,128)(2,1)S(1)} %get-tuple-element.91), channel_id=1, source_target_pairs={{0,16},{1,17},{2,18},{3,19},{4,8},{5,9},{6,10},{7,11},{8,4},{9,5},... | collective-permute-start | bytes 663560 | tf_op jit(solution)/shard_map/ppermute | solution.py:34
  16.2 1.4 %collective-permute-start.4 = (f32[2,152,128]{2,1,0:T(8,128)S(1)}, f32[2,152,128]{2,1,0:T(8,128)S(1)}, u32[]{:S(2)}, u32[]{:S(2)}) collective-permute-start(f32[2,152,128]{2,1,0:T(8,128)S(1)} %slice_bitcast_fusion), channel_id=1, source_target_pairs={{0,4},{4,0},{8,12},{12,8},{1,5},{5,1},{9,13},{13,9},{2,6},{6,2},{1... | collective-permute-start | bytes 466952 | tf_op jit(solution)/shard_map/ppermute | solution.py:439
  17.7 3.6 %collective-permute-start.5 = (bf16[1,152,128]{2,1,0:T(8,128)(2,1)S(1)}, bf16[1,152,128]{2,1,0:T(8,128)(2,1)S(1)}, u32[]{:S(2)}, u32[]{:S(2)}) collective-permute-start(bf16[1,152,128]{2,1,0:T(8,128)(2,1)S(1)} %slice.15), channel_id=1, source_target_pairs={{0,20},{4,16},{8,28},{12,24},{16,4},{20,0},{24,12},{28,8},{1,21},{... | collective-permute-start | bytes 116744 | tf_op jit(solution)/shard_map/ppermute | solution.py:347
  21.2 3.6 %collective-permute-start.6 = (bf16[152,128]{1,0:T(8,128)(2,1)S(1)}, bf16[152,128]{1,0:T(8,128)(2,1)S(1)}, u32[]{:S(2)}, u32[]{:S(2)}) collective-permute-start(bf16[152,128]{1,0:T(8,128)(2,1)S(1)} %fusion.1), channel_id=1, source_target_pairs={{0,12},{4,8},{8,4},{12,0},{1,13},{5,9},{9,5},{13,1},{2,14},{6,10},... | collective-permute-start | bytes 116744 | tf_op jit(solution)/shard_map/ppermute | solution.py:343
  24.8 3.5 %collective-permute-start.7 = (bf16[152,128]{1,0:T(8,128)(2,1)S(1)}, bf16[152,128]{1,0:T(8,128)(2,1)S(1)}, u32[]{:S(2)}, u32[]{:S(2)}) collective-permute-start(bf16[152,128]{1,0:T(8,128)(2,1)S(1)} %add_convert_fusion.1), channel_id=1, source_target_pairs={{0,5},{4,1},{8,13},{12,9},{1,4},{5,0},{9,12},{13,8},{2,7},{6,3},{1... | collective-permute-start | bytes 116744 | tf_op jit(solution)/shard_map/ppermute | solution.py:348
  28.3 4.4 %collective-permute-start.8 = (bf16[152,128]{1,0:T(8,128)(2,1)S(1)}, bf16[152,128]{1,0:T(8,128)(2,1)S(1)}, u32[]{:S(2)}, u32[]{:S(2)}) collective-permute-start(bf16[152,128]{1,0:T(8,128)(2,1)S(1)} %add_convert_fusion), channel_id=1, source_target_pairs={{0,6},{4,2},{8,14},{12,10},{1,7},{5,3},{9,15},{13,11},{2,4},{6,0},... | collective-permute-start | bytes 116744 | tf_op jit(solution)/shard_map/ppermute | solution.py:348
  32.7 1.3 %collective-permute-start.9 = (f32[152,128]{1,0:T(8,128)S(1)}, f32[152,128]{1,0:T(8,128)S(1)}, u32[]{:S(2)}, u32[]{:S(2)}) collective-permute-start(f32[152,128]{1,0:T(8,128)S(1)} %convert_add_fusion.a_ref), channel_id=1, source_target_pairs={{0,4},{4,0},{8,12},{12,8},{1,5},{5,1},{9,13},{13,9},{2,6},{6,2},{1... | collective-permute-start | bytes 233480 | tf_op jit(solution)/shard_map/ppermute | solution.py:483

commit v6 on v5

--- a/solution.py
+++ b/solution.py
@@ -147,23 +147,31 @@
         copy.wait()
 
 
-def edges_kernel(x_ref, c_ref, col_odd, col_even, strip, even_ref, odd_ref, *, rows, cols):
+def edges_kernel(
+    x_ref, c_ref, col_odd, col_even, w1_ref, s1_ref, b1_ref, strip, odd_ref, even_ref, *, rows, cols
+):
     col_is_odd = lax.axis_index("col") % 2 == 1
     row_is_odd = lax.axis_index("row") % 2
-    chans = x_ref.shape[2]
+    chans, inner = w1_ref.shape
+    wide = cols + STRIP
     gap = jnp.zeros((STRIP - 2 * EDGE, chans), F32)
     for r in range(2 * rows):
         a, b = col_even[r].astype(F32), col_odd[r].astype(F32)
         high, low = jnp.where(col_is_odd, b, a), jnp.where(col_is_odd, a, b)
         strip[r] = jnp.concatenate([high, gap, low], axis=0).astype(BF)
+    behind = [v for r in (1, rows - 2) for v in (x_ref[r], strip[r])]
+    act, _ = reduce_act(jnp.concatenate(behind, axis=0), w1_ref[...], s1_ref[...], b1_ref[...])
+    col_ok = column_mask(wide, cols, inner)
+    act_low, act_high = act[0:wide] * col_ok, act[wide:] * col_ok
     for ref, sends_high in ((even_ref, row_is_odd == 0), (odd_ref, row_is_odd == 1)):
-        at = jnp.where(sends_high, rows - 2, 0)
-        cot_at = jnp.where(sends_high, rows - 1, 0)
-        for i in range(2):
-            ref[i, 0:cols, :] = x_ref[at + i]
-            ref[i, cols:, :] = strip[at + i]
-        ref[2, 0:cols, :] = c_ref[cot_at]
-        ref[2, cols:, :] = strip[rows + cot_at]
+        at = jnp.where(sends_high, rows - 1, 0)
+        ref[0:cols, :] = x_ref[at]
+        ref[cols:wide, :] = strip[at]
+        ref[wide : wide + cols, :] = c_ref[at]
+        ref[wide + cols : 2 * wide, :] = strip[rows + at]
+        sent = jnp.where(sends_high, act_high, act_low)
+        ref[2 * wide :, 0:inner] = sent[0 : wide // 2].astype(BF)
+        ref[2 * wide :, inner:] = sent[wide // 2 :].astype(BF)
 
 
 def inner_kernel(
@@ -234,27 +242,30 @@
 
     @pl.when(row_is_odd == 0)
     def _():
-        far_ref[0:3] = row_odd[...]
-        far_ref[3:6] = row_even[...]
+        far_ref[0] = row_odd[...]
+        far_ref[1] = row_even[...]
 
     @pl.when(row_is_odd == 1)
     def _():
-        far_ref[0:3] = row_even[...]
-        far_ref[3:6] = row_odd[...]
+        far_ref[0] = row_even[...]
+        far_ref[1] = row_odd[...]
 
     def wider(ref, r, base):
         return jnp.concatenate([ref[r], strip_ref[base + r]], axis=0)
 
-    far = [far_ref[i] for i in (0, 1, 3, 4)]
-    act, _ = reduce_act(jnp.concatenate(far, axis=0), w1_ref[...], s1, b1)
-    for k in range(4):
-        spread(hacts, k, act[k * wide : (k + 1) * wide] * (col_ok * (has_low if k < 2 else has_high)))
+    near = [far_ref[i, 0:wide, :] for i in range(2)]
+    near_cot = [far_ref[i, wide : 2 * wide, :] for i in range(2)]
+    act, _ = reduce_act(jnp.concatenate(near, axis=0), w1_ref[...], s1, b1)
+    for k, has in ((0, has_low), (1, has_high)):
+        sent = far_ref[k, 2 * wide :, :].astype(F32)
+        spread(hacts, 3 * k, jnp.concatenate([sent[:, 0:inner], sent[:, inner:]], axis=0) * has)
+        spread(hacts, 1 + k, act[k * wide : (k + 1) * wide] * (col_ok * has))
     def act_row(r):
         return hacts[r] if r < 2 else acts[r - 2] if r < rows + 2 else hacts[r - rows]
 
     conv = jnp.concatenate(conv_pairs(act_row, (0, rows), w2), axis=0)
-    skip = jnp.concatenate([far[1], wider(x_ref, 0, 0), wider(x_ref, rows - 1, 0), far[2]], axis=0)
-    ct = jnp.concatenate([far_ref[2], wider(c_ref, 0, rows), wider(c_ref, rows - 1, rows), far_ref[5]], axis=0)
+    skip = jnp.concatenate([near[0], wider(x_ref, 0, 0), wider(x_ref, rows - 1, 0), near[1]], axis=0)
+    ct = jnp.concatenate([near_cot[0], wider(c_ref, 0, rows), wider(c_ref, rows - 1, rows), near_cot[1]], axis=0)
     a2, grad3, back3, grad2 = through(conv, skip, ct, s2, b2, w3_ref[...], w3t_ref[...], s3, b3)
     for k in range(4):
         g = grad2[k * wide : (k + 1) * wide] * col_ok
@@ -276,8 +287,8 @@
     own_gt = jnp.concatenate([hgrad[k, 0:cols, inner : 2 * inner] for k in (1, 2)], axis=0).T
     compact = jnp.zeros((inner, inner), F32)
     for dh in range(3):
-        near = jnp.concatenate([act_row(q + dh)[0:cols] for q in (1, rows)], axis=0)
-        full = ((full_ref[dh] + dot(own_gt, near)) * same[...]).astype(BF)
+        around = jnp.concatenate([act_row(q + dh)[0:cols] for q in (1, rows)], axis=0)
+        full = ((full_ref[dh] + dot(own_gt, around)) * same[...]).astype(BF)
         compact = compact + dot(full, pick[dh * 3 * inner : (dh + 1) * 3 * inner, :])
     gw2 = compact.T
 
@@ -337,15 +348,17 @@
         copy.wait()
 
 
-def crossed(value, axis, bit):
-    n_row = lax.axis_size("row")
-    if axis == "row":
-        return lax.ppermute(value, "row", [(i, i ^ bit ^ 1) for i in range(n_row)])
-    count = lax.axis_size(axis)
-    pairs = [(i, j, i ^ bit, j ^ 1) for i in range(count) for j in range(n_row)]
-    if axis == "dp":
-        return lax.ppermute(value, ("dp", "row"), [(i * n_row + j, k * n_row + m) for i, j, k, m in pairs])
-    return lax.ppermute(value, ("row", "col"), [(j * count + i, m * count + k) for i, j, k, m in pairs])
+def crossed(value, move, other_move):
+    names = ("dp", "row", "col")
+    sizes = [lax.axis_size(a) for a in names]
+    perm = []
+    for at in itertools.product(*(range(n) for n in sizes)):
+        axis, bit = other_move if sum(i.bit_count() for i in at) % 2 else move
+        to = list(at)
+        to[names.index(axis)] ^= bit
+        to[1] ^= 1
+        perm.append(tuple(functools.reduce(lambda v, k: v * sizes[k] + p[k], range(3), 0) for p in (at, to)))
+    return lax.ppermute(value, names, perm)
 
 
 def body(
@@ -394,14 +407,16 @@
     )(*(pltpu.with_memory_space_constraint(v, pltpu.HBM) for v in (group_weight, *sources)))
     shared = (w1, *vecs, w2, w2t, w3, w3t)
     col_odd, col_even, shared, x, c = lax.optimization_barrier((col_odd, col_even, shared, x, c))
-    strip, to_even, to_odd = pl.pallas_call(
+    w1, *vecs = shared[:7]
+    message = 2 * wide + wide * inner // chans
+    strip, to_odd, to_even = pl.pallas_call(
         functools.partial(edges_kernel, rows=rows, cols=cols),
-        out_shape=(shape((2 * rows, STRIP, chans), BF),) + (shape((3, wide, chans), BF),) * 2,
-        in_specs=[vmem] * 4,
+        out_shape=(shape((2 * rows, STRIP, chans), BF),) + (shape((message, chans), BF),) * 2,
+        in_specs=[vmem] * 7,
         out_specs=(vmem,) * 3,
         compiler_params=params,
         name="edges",
-    )(x, c, col_odd, col_even)
+    )(x, c, col_odd, col_even, w1, *vecs[:2])
     row_even, row_odd = swap_edges(to_even, to_odd, "row")
     acts, gcat, d1, back_in, g1_in, gw3, full, gw1, xt = pl.pallas_call(
         functools.partial(inner_kernel, inner=inner, **sizes),
@@ -431,7 +446,7 @@
         ),
         in_specs=[vmem] * 25,
         out_specs=(vmem,) * 3,
-        scratch_shapes=[pltpu.VMEM((4, wide, 3 * inner), BF)] * 2 + [pltpu.VMEM((6, wide, chans), BF)],
+        scratch_shapes=[pltpu.VMEM((4, wide, 3 * inner), BF)] * 2 + [pltpu.VMEM((2, message, chans), BF)],
         compiler_params=params,
         name="rim",
     )(x, c, strip, row_even, row_odd, *shared, acts, gcat, d1, gw3, full, gw1, xt, same, pick)
@@ -449,14 +464,14 @@
     held = n_dp
     while held > 1:
         held //= 2
-        other = crossed(shares[held:], "dp", held)
+        other = crossed(shares[held:], ("dp", held), ("dp", held))
         shares = (shares[:held].astype(F32) + other.astype(F32)).astype(BF)
     total = shares[0]
     steps = [("row", 1 << k) for k in range(1, n_row.bit_length() - 1)]
-    steps += [("col", 1 << k) for k in range(n_col.bit_length() - 1)]
-    for axis, bit in steps:
-        other = crossed(total, axis, bit)
-        if (axis, bit) == steps[0]:
+    steps += [("col", 1 << k) for k in reversed(range(n_col.bit_length() - 1))]
+    for i, step in enumerate(steps):
+        other = crossed(total, step, steps[(i + 1) % len(steps)])
+        if i == 0:
             input_grad, other = lax.optimization_barrier((input_grad, other))
         summed = total.astype(F32) + other.astype(F32)
         total = summed.astype(BF)

time: 35 us -> 34.6 us (0.989)
  waiting for transfers between devices: 12 us -> 11.6 us
    ppermute x2, waiting for transfers between devices: 1.35 us -> 0.96 us  [swap_edges(): got_odd = lax.ppermute(to_odd, names, perm)]
where the time goes in v6:
time: 34.6 us; the launch traced here: 34.4 us
  starting transfers between devices  12.6 us (36%)
  waiting for transfers between devices  11.6 us (34%)
  Pallas kernels  9.37 us (27%)
  between operations  0.73 us (2%)
    ppermute x4, waiting for transfers between devices, crossed(): return lax.ppermute(value, names, perm)  8.17 us
    ppermute x4, starting transfers between devices, crossed(): return lax.ppermute(value, names, perm)  5.65 us
    ppermute x2, starting transfers between devices, swap_edges(): got_even = lax.ppermute(to_even, axis, [(i, i ^ 1) for i in range(count)])  4.22 us
    pallas_call x1, Pallas kernels, body(): pl.pallas_call(functools.partial(inner_kernel, inner=inner, **sizes), out...  3.04 us
    ppermute x2, starting transfers between devices, swap_edges(): got_odd = lax.ppermute(to_odd, names, perm)  2.1 us
    pallas_call x1, Pallas kernels, body(): pl.pallas_call(functools.partial(rim_kernel, inner=inner, group_ch=group_...  2.04 us
    pallas_call x1, Pallas kernels, body(): pl.pallas_call(functools.partial(load_kernel, inner=inner, group_ch=group...  1.4 us
    ppermute x1, waiting for transfers between devices, body(): shares = (shares[0] + lax.ppermute(shares[1], 'row', near)).astype(BF)  1.27 us
  transfers between devices with their start and end apart: 10, of which 8 were waited for; matrix products, arithmetic and copies ran while one was open for 0% of the time, Pallas kernels for 16%

profile of v6, /device:TPU:0, one launch (start us, length us, event | category | flops | bytes accessed | tf_op | source)
XLA Modules:
  0.0 34.4 jit_solution(16310603761372845025)
XLA Ops:
  0.6 0.9 %cut.1 = (bf16[16,2,256]{2,1,0:T(2,128)(2,1)S(1)}, bf16[16,2,256]{2,1,0:T(2,128)(2,1)S(1)}) custom-call(bf16[8,128,256]{2,1,0:T(8,128)(2,1)} %bitcast.18, bf16[8,128,256]{2,1,0:T(8,128)(2,1)} %bitcast.20), custom_call_target="tpu_custom_call" | custom-call | tf_op jit(solution)/shard_map/cut/pallas_call | solution.py:383
  1.5 0.5 %collective-permute-start = (bf16[16,2,256]{2,1,0:T(2,128)(2,1)S(1)}, bf16[16,2,256]{2,1,0:T(2,128)(2,1)S(1)}, u32[]{:S(2)}, u32[]{:S(2)}) collective-permute-start(bf16[16,2,256]{2,1,0:T(2,128)(2,1)S(1)} %get-tuple-element.58), channel_id=1, source_target_pairs={{0,4},{1,2},{2,1},{3,7},{4,0},{5,6},{6,5},{7,3},{8,12},{9,10},{10,... | collective-permute-start | bytes 49160 | tf_op jit(solution)/shard_map/ppermute | solution.py:34
  2.0 4.1 %collective-permute-start.1 = (bf16[16,2,256]{2,1,0:T(2,128)(2,1)S(1)}, bf16[16,2,256]{2,1,0:T(2,128)(2,1)S(1)}, u32[]{:S(2)}, u32[]{:S(2)}) collective-permute-start(bf16[16,2,256]{2,1,0:T(2,128)(2,1)S(1)} %get-tuple-element.59), channel_id=1, source_target_pairs={{0,1},{1,0},{2,3},{3,2},{4,5},{5,4},{6,7},{7,6},{8,9},{9,8},{10,11... | collective-permute-start | bytes 49160 | tf_op jit(solution)/shard_map/ppermute | solution.py:20
  6.2 1.4 %load.1 = (bf16[128,256]{1,0:T(8,128)(2,1)S(1)}, bf16[256,128]{1,0:T(8,128)(2,1)S(1)}, bf16[8,128,256]{2,1,0:T(8,128)(2,1)S(1)}, bf16[8,128,256]{2,1,0:T(8,128)(...) custom-call(bf16[3,3,4,128]{3,2,1,0:T(4,128)(2,1)} %refs_0_.1, ...), custom_call_target="tpu_custom_call" | custom-call | tf_op jit(solution)/shard_map/load/pallas_call | solution.py:397
  7.6 0.3 collective-permute-done.1.col_even
  7.9 0.2 edges.1
  8.2 1.6 %collective-permute-start.3 = (bf16[360,256]{1,0:T(8,128)(2,1)S(1)}, bf16[360,256]{1,0:T(8,128)(2,1)S(1)}, u32[]{:S(2)}, u32[]{:S(2)}) collective-permute-start(bf16[360,256]{1,0:T(8,128)(2,1)S(1)} %get-tuple-element.91), channel_id=1, source_target_pairs={{0,16},{1,17},{2,18},{3,19},{4,8},{5,9},{6,10},{7,11},{8,4},{9,5},... | collective-permute-start | bytes 552968 | tf_op jit(solution)/shard_map/ppermute | solution.py:34
  9.8 3.0 %inner.1 = (bf16[8,144,384]{2,1,0:T(8,128)(2,1)S(1)}, bf16[6,144,384]{2,1,0:T(8,128)(2,1)S(1)}, f32[1024,128]{1,0:T(8,128)S(1)}, f32[768,256]{1,0:T(8,128)S(1)},...) custom-call(bf16[8,128,256]{2,1,0:T(8,128)(2,1)S(1)} %get-tuple-elem, ...), custom_call_target="tpu_custom_call" | custom-call | tf_op jit(solution)/shard_map/inner/pallas_call | solution.py:421
  12.9 1.0 %collective-permute-done.3.row_odd = bf16[360,256]{1,0:T(8,128)(2,1)S(1)} collective-permute-done((bf16[360,256]{1,0:T(8,128)(2,1)S(1)}, bf16[360,256]{1,0:T(8,128)(2,1)S(1)}, u32[]{:S(2)}, u32[]{:S(2)}) %collective-permute-start.3) | collective-permute-done | bytes 184352 | tf_op jit(solution)/shard_map/ppermute | solution.py:34
  13.8 2.0 %rim.1 = (f32[2,2,152,128]{3,2,1,0:T(8,128)S(1)}, bf16[512,128]{1,0:T(8,128)(2,1)S(1)}, f32[256,256]{1,0:T(8,128)S(1)}) custom-call(bf16[8,128,256]{2,1,0:T(8,128)(2,1)S(1)} %get-tuple-element.73.x_ref, bf16[8,128,256]{2,1,0:T(8,128)(2,1)S(1)} %get-tuple-element.74.c_ref, bf16[16,16,256]{2,1,0:T(8,128)(2,1)S(1)} %get-tuple-element.80.strip_ref, ...), custom_call_target="tpu_custom_call" | custom-call | tf_op jit(solution)/shard_map/rim/pallas_call | solution.py:440
  15.9 0.2 collective-permute-start.4
  16.1 1.3 %collective-permute-done.4 = f32[2,152,128]{2,1,0:T(8,128)S(1)} collective-permute-done((f32[2,152,128]{2,1,0:T(8,128)S(1)}, f32[2,152,128]{2,1,0:T(8,128)S(1)}, u32[]{:S(2)}, u32[]{:S(2)}) %collective-permute-start.4) | collective-permute-done | bytes 155680 | tf_op jit(solution)/shard_map/ppermute | solution.py:454
  17.4 1.3 %collective-permute-start.5 = (bf16[1,152,128]{2,1,0:T(8,128)(2,1)S(1)}, bf16[1,152,128]{2,1,0:T(8,128)(2,1)S(1)}, u32[]{:S(2)}, u32[]{:S(2)}) collective-permute-start(bf16[1,152,128]{2,1,0:T(8,128)(2,1)S(1)} %slice.15), channel_id=1, source_target_pairs={{0,20},{1,21},{2,22},{3,23},{4,16},{5,17},{6,18},{7,19},{8,28},{9,... | collective-permute-start | bytes 116744 | tf_op jit(solution)/shard_map/ppermute | solution.py:361
  18.7 2.2 %collective-permute-done.5 = bf16[1,152,128]{2,1,0:T(8,128)(2,1)S(1)} collective-permute-done((bf16[1,152,128]{2,1,0:T(8,128)(2,1)S(1)}, bf16[1,152,128]{2,1,0:T(8,128)(2,1)S(1)}, u32[]{:S(2)}, u32[]{:S(2)}) %collective-permute-start.5) | collective-permute-done | bytes 38944 | tf_op jit(solution)/shard_map/ppermute | solution.py:361
  20.9 0.7 %collective-permute-start.6 = (bf16[152,128]{1,0:T(8,128)(2,1)S(1)}, bf16[152,128]{1,0:T(8,128)(2,1)S(1)}, u32[]{:S(2)}, u32[]{:S(2)}) collective-permute-start(bf16[152,128]{1,0:T(8,128)(2,1)S(1)} %fusion.1), channel_id=1, source_target_pairs={{0,12},{1,7},{2,4},{3,15},{4,2},{5,9},{6,10},{7,1},{8,14},{9,5},{1... | collective-permute-start | bytes 116744 | tf_op jit(solution)/shard_map/ppermute | solution.py:361
  21.7 1.1 %out.1 = bf16[8,128,256]{2,1,0:T(8,128)(2,1)} custom-call(bf16[512,128]{1,0:T(8,128)(2,1)S(1)} %get-tuple-element.89.g1_in, bf16[512,128]{1,0:T(8,128)(2,1)S(1)} %get-tuple-element.103.g1_rim, f32[768,256]{1,0:T(8,128)S(1)} %get-tuple-element.104.back_in, f32[256,256]{1,0:T(8,128)S(1)} %get-tuple-element.105.back_rim, ...), custom_call_target="tpu_custom_call" | custom-call | tf_op jit(solution)/shard_map/out/pallas_call | solution.py:456
  22.8 1.6 %collective-permute-done.6 = bf16[152,128]{1,0:T(8,128)(2,1)S(1)} collective-permute-done((bf16[152,128]{1,0:T(8,128)(2,1)S(1)}, bf16[152,128]{1,0:T(8,128)(2,1)S(1)}, u32[]{:S(2)}, u32[]{:S(2)}) %collective-permute-start.6) | collective-permute-done | bytes 38944 | tf_op jit(solution)/shard_map/ppermute | solution.py:361
  24.4 1.7 %collective-permute-start.7 = (bf16[152,128]{1,0:T(8,128)(2,1)S(1)}, bf16[152,128]{1,0:T(8,128)(2,1)S(1)}, u32[]{:S(2)}, u32[]{:S(2)}) collective-permute-start(bf16[152,128]{1,0:T(8,128)(2,1)S(1)} %add_convert_fusion.1), channel_id=1, source_target_pairs={{0,6},{1,4},{2,7},{3,5},{4,1},{5,3},{6,0},{7,2},{8,13},{9,15},{10,... | collective-permute-start | bytes 116744 | tf_op jit(solution)/shard_map/ppermute | solution.py:361
  26.2 2.6 %collective-permute-done.7 = bf16[152,128]{1,0:T(8,128)(2,1)S(1)} collective-permute-done((bf16[152,128]{1,0:T(8,128)(2,1)S(1)}, bf16[152,128]{1,0:T(8,128)(2,1)S(1)}, u32[]{:S(2)}, u32[]{:S(2)}) %collective-permute-start.7) | collective-permute-done | bytes 38944 | tf_op jit(solution)/shard_map/ppermute | solution.py:361
  28.8 1.8 %collective-permute-start.8 = (bf16[152,128]{1,0:T(8,128)(2,1)S(1)}, bf16[152,128]{1,0:T(8,128)(2,1)S(1)}, u32[]{:S(2)}, u32[]{:S(2)}) collective-permute-start(bf16[152,128]{1,0:T(8,128)(2,1)S(1)} %add_convert_fusion), channel_id=1, source_target_pairs={{0,5},{1,13},{2,14},{3,6},{4,8},{5,0},{6,3},{7,11},{8,4},{9,12},{1... | collective-permute-start | bytes 116744 | tf_op jit(solution)/shard_map/ppermute | solution.py:361
  30.7 1.7 %collective-permute-done.8 = bf16[152,128]{1,0:T(8,128)(2,1)S(1)} collective-permute-done((bf16[152,128]{1,0:T(8,128)(2,1)S(1)}, bf16[152,128]{1,0:T(8,128)(2,1)S(1)}, u32[]{:S(2)}, u32[]{:S(2)}) %collective-permute-start.8) | collective-permute-done | bytes 38944 | tf_op jit(solution)/shard_map/ppermute | solution.py:361
  32.3 0.4 %collective-permute-start.9 = (f32[152,128]{1,0:T(8,128)S(1)}, f32[152,128]{1,0:T(8,128)S(1)}, u32[]{:S(2)}, u32[]{:S(2)}) collective-permute-start(f32[152,128]{1,0:T(8,128)S(1)} %convert_add_fusion.a_ref), channel_id=1, source_target_pairs={{0,4},{4,0},{8,12},{12,8},{1,5},{5,1},{9,13},{13,9},{2,6},{6,2},{1... | collective-permute-start | bytes 233480 | tf_op jit(solution)/shard_map/ppermute | solution.py:498
  32.8 0.9 %collective-permute-done.9.b_ref = f32[152,128]{1,0:T(8,128)S(1)} collective-permute-done((f32[152,128]{1,0:T(8,128)S(1)}, f32[152,128]{1,0:T(8,128)S(1)}, u32[]{:S(2)}, u32[]{:S(2)}) %collective-permute-start.9) | collective-permute-done | bytes 77856 | tf_op jit(solution)/shard_map/ppermute | solution.py:498
  33.7 0.7 %last.1 = (f32[128,128]{1,0:T(8,128)}, f32[3,3,4,64]{3,2,1,0:T(4,128)}, f32[64,256]{1,0:T(8,128)}) custom-call(f32[152,128]{1,0:T(8,128)S(1)} %convert_add_fusion.a_ref, f32[152,128]{1,0:T(8,128)S(1)} %collective-permute-done.9.b_ref), custom_call_target="tpu_custom_call" | custom-call | tf_op jit(solution)/shard_map/last/pallas_call | solution.py:479
  (10 shorter events, 0.2 us)
Async XLA Ops:
  1.5 6.1 %collective-permute-start = (bf16[16,2,256]{2,1,0:T(2,128)(2,1)S(1)}, bf16[16,2,256]{2,1,0:T(2,128)(2,1)S(1)}, u32[]{:S(2)}, u32[]{:S(2)}) collective-permute-start(bf16[16,2,256]{2,1,0:T(2,128)(2,1)S(1)} %get-tuple-element.58), channel_id=1, source_target_pairs={{0,4},{1,2},{2,1},{3,7},{4,0},{5,6},{6,5},{7,3},{8,12},{9,10},{10,... | collective-permute-start | bytes 49160 | tf_op jit(solution)/shard_map/ppermute | solution.py:34
  2.0 5.9 %collective-permute-start.1 = (bf16[16,2,256]{2,1,0:T(2,128)(2,1)S(1)}, bf16[16,2,256]{2,1,0:T(2,128)(2,1)S(1)}, u32[]{:S(2)}, u32[]{:S(2)}) collective-permute-start(bf16[16,2,256]{2,1,0:T(2,128)(2,1)S(1)} %get-tuple-element.59), channel_id=1, source_target_pairs={{0,1},{1,0},{2,3},{3,2},{4,5},{5,4},{6,7},{7,6},{8,9},{9,8},{10,11... | collective-permute-start | bytes 49160 | tf_op jit(solution)/shard_map/ppermute | solution.py:20
  8.1 4.7 %collective-permute-start.2 = (bf16[360,256]{1,0:T(8,128)(2,1)S(1)}, bf16[360,256]{1,0:T(8,128)(2,1)S(1)}, u32[]{:S(2)}, u32[]{:S(2)}) collective-permute-start(bf16[360,256]{1,0:T(8,128)(2,1)S(1)} %get-tuple-element.90), channel_id=1, source_target_pairs={{0,4},{4,0},{8,12},{12,8},{1,5},{5,1},{9,13},{13,9},{2,6},{6,2},{1... | collective-permute-start | bytes 552968 | tf_op jit(solution)/shard_map/ppermute | solution.py:20
  8.2 5.6 %collective-permute-start.3 = (bf16[360,256]{1,0:T(8,128)(2,1)S(1)}, bf16[360,256]{1,0:T(8,128)(2,1)S(1)}, u32[]{:S(2)}, u32[]{:S(2)}) collective-permute-start(bf16[360,256]{1,0:T(8,128)(2,1)S(1)} %get-tuple-element.91), channel_id=1, source_target_pairs={{0,16},{1,17},{2,18},{3,19},{4,8},{5,9},{6,10},{7,11},{8,4},{9,5},... | collective-permute-start | bytes 552968 | tf_op jit(solution)/shard_map/ppermute | solution.py:34
  15.9 1.4 %collective-permute-start.4 = (f32[2,152,128]{2,1,0:T(8,128)S(1)}, f32[2,152,128]{2,1,0:T(8,128)S(1)}, u32[]{:S(2)}, u32[]{:S(2)}) collective-permute-start(f32[2,152,128]{2,1,0:T(8,128)S(1)} %slice_bitcast_fusion), channel_id=1, source_target_pairs={{0,4},{4,0},{8,12},{12,8},{1,5},{5,1},{9,13},{13,9},{2,6},{6,2},{1... | collective-permute-start | bytes 466952 | tf_op jit(solution)/shard_map/ppermute | solution.py:454
  17.4 3.6 %collective-permute-start.5 = (bf16[1,152,128]{2,1,0:T(8,128)(2,1)S(1)}, bf16[1,152,128]{2,1,0:T(8,128)(2,1)S(1)}, u32[]{:S(2)}, u32[]{:S(2)}) collective-permute-start(bf16[1,152,128]{2,1,0:T(8,128)(2,1)S(1)} %slice.15), channel_id=1, source_target_pairs={{0,20},{1,21},{2,22},{3,23},{4,16},{5,17},{6,18},{7,19},{8,28},{9,... | collective-permute-start | bytes 116744 | tf_op jit(solution)/shard_map/ppermute | solution.py:361
  20.9 3.5 %collective-permute-start.6 = (bf16[152,128]{1,0:T(8,128)(2,1)S(1)}, bf16[152,128]{1,0:T(8,128)(2,1)S(1)}, u32[]{:S(2)}, u32[]{:S(2)}) collective-permute-start(bf16[152,128]{1,0:T(8,128)(2,1)S(1)} %fusion.1), channel_id=1, source_target_pairs={{0,12},{1,7},{2,4},{3,15},{4,2},{5,9},{6,10},{7,1},{8,14},{9,5},{1... | collective-permute-start | bytes 116744 | tf_op jit(solution)/shard_map/ppermute | solution.py:361
  24.4 4.4 %collective-permute-start.7 = (bf16[152,128]{1,0:T(8,128)(2,1)S(1)}, bf16[152,128]{1,0:T(8,128)(2,1)S(1)}, u32[]{:S(2)}, u32[]{:S(2)}) collective-permute-start(bf16[152,128]{1,0:T(8,128)(2,1)S(1)} %add_convert_fusion.1), channel_id=1, source_target_pairs={{0,6},{1,4},{2,7},{3,5},{4,1},{5,3},{6,0},{7,2},{8,13},{9,15},{10,... | collective-permute-start | bytes 116744 | tf_op jit(solution)/shard_map/ppermute | solution.py:361
  28.8 3.5 %collective-permute-start.8 = (bf16[152,128]{1,0:T(8,128)(2,1)S(1)}, bf16[152,128]{1,0:T(8,128)(2,1)S(1)}, u32[]{:S(2)}, u32[]{:S(2)}) collective-permute-start(bf16[152,128]{1,0:T(8,128)(2,1)S(1)} %add_convert_fusion), channel_id=1, source_target_pairs={{0,5},{1,13},{2,14},{3,6},{4,8},{5,0},{6,3},{7,11},{8,4},{9,12},{1... | collective-permute-start | bytes 116744 | tf_op jit(solution)/shard_map/ppermute | solution.py:361
  32.3 1.3 %collective-permute-start.9 = (f32[152,128]{1,0:T(8,128)S(1)}, f32[152,128]{1,0:T(8,128)S(1)}, u32[]{:S(2)}, u32[]{:S(2)}) collective-permute-start(f32[152,128]{1,0:T(8,128)S(1)} %convert_add_fusion.a_ref), channel_id=1, source_target_pairs={{0,4},{4,0},{8,12},{12,8},{1,5},{5,1},{9,13},{13,9},{2,6},{6,2},{1... | collective-permute-start | bytes 233480 | tf_op jit(solution)/shard_map/ppermute | solution.py:498

commit v7 on v6

--- a/solution.py
+++ b/solution.py
@@ -273,9 +273,6 @@
     own = [slice(k * wide, k * wide + cols) for k in (1, 2)]
     for k in range(2):
         back[k * cols : (k + 1) * cols, :] = back3[own[k]]
-    gw3 = gw3_ref[...] + dot(
-        jnp.concatenate([a2[at] for at in own], axis=0).T, jnp.concatenate([grad3[at] for at in own], axis=0)
-    )
     def grad_row(q):
         return (hgrad[q] if q < 2 else gcat[q - 2] if q < rows else hgrad[q - rows + 2])[0:cols]
 
@@ -285,14 +282,20 @@
     g = (conv * slope).astype(BF)
     g1[...] = g
     own_gt = jnp.concatenate([hgrad[k, 0:cols, inner : 2 * inner] for k in (1, 2)], axis=0).T
-    compact = jnp.zeros((inner, inner), F32)
-    for dh in range(3):
-        around = jnp.concatenate([act_row(q + dh)[0:cols] for q in (1, rows)], axis=0)
-        full = ((full_ref[dh] + dot(own_gt, around)) * same[...]).astype(BF)
-        compact = compact + dot(full, pick[dh * 3 * inner : (dh + 1) * 3 * inner, :])
+    around = jnp.concatenate(
+        [jnp.concatenate([act_row(q + dh)[0:cols] for q in (1, rows)], axis=0) for dh in range(3)], axis=1
+    )
+    full = dot(own_gt, around)
+    full = jnp.concatenate(
+        [(full_ref[dh] + full[:, dh * 3 * inner : (dh + 1) * 3 * inner]) * same[...] for dh in range(3)], axis=1
+    )
+    compact = dot(full.astype(BF), pick[...])
     gw2 = compact.T
 
     gw1 = gw1_ref[...] + dot(xt[...], g)
+    gw3 = gw3_ref[...] + dot(
+        jnp.concatenate([a2[at] for at in own], axis=0).T, jnp.concatenate([grad3[at] for at in own], axis=0)
+    )
     n_dp = share_ref.shape[1]
     one, three = chans // n_dp, inner // n_dp
     parity = parity_of_place()

time: 34.6 us -> 34.5 us (level)
  no operation moved by 1% of the time
where the time goes in v7:
time: 34.5 us; the launch traced here: 34.3 us
  starting transfers between devices  12.6 us (37%)
  waiting for transfers between devices  11.6 us (34%)
  Pallas kernels  9.28 us (27%)
  between operations  0.73 us (2%)
    ppermute x4, waiting for transfers between devices, crossed(): return lax.ppermute(value, names, perm)  8.17 us
    ppermute x4, starting transfers between devices, crossed(): return lax.ppermute(value, names, perm)  5.65 us
    ppermute x2, starting transfers between devices, swap_edges(): got_even = lax.ppermute(to_even, axis, [(i, i ^ 1) for i in range(count)])  4.22 us
    pallas_call x1, Pallas kernels, body(): pl.pallas_call(functools.partial(inner_kernel, inner=inner, **sizes), out...  3.04 us
    ppermute x2, starting transfers between devices, swap_edges(): got_odd = lax.ppermute(to_odd, names, perm)  2.1 us
    pallas_call x1, Pallas kernels, body(): pl.pallas_call(functools.partial(rim_kernel, inner=inner, group_ch=group_...  1.94 us
    pallas_call x1, Pallas kernels, body(): pl.pallas_call(functools.partial(load_kernel, inner=inner, group_ch=group...  1.4 us
    ppermute x1, waiting for transfers between devices, body(): shares = (shares[0] + lax.ppermute(shares[1], 'row', near)).astype(BF)  1.27 us
  transfers between devices with their start and end apart: 10, of which 8 were waited for; matrix products, arithmetic and copies ran while one was open for 0% of the time, Pallas kernels for 16%

profile of v7, /device:TPU:0, one launch (start us, length us, event | category | flops | bytes accessed | tf_op | source)
XLA Modules:
  0.0 34.3 jit_solution(15225303616043374796)
XLA Ops:
  0.6 0.9 %cut.1 = (bf16[16,2,256]{2,1,0:T(2,128)(2,1)S(1)}, bf16[16,2,256]{2,1,0:T(2,128)(2,1)S(1)}) custom-call(bf16[8,128,256]{2,1,0:T(8,128)(2,1)} %bitcast.18, bf16[8,128,256]{2,1,0:T(8,128)(2,1)} %bitcast.20), custom_call_target="tpu_custom_call" | custom-call | tf_op jit(solution)/shard_map/cut/pallas_call | solution.py:386
  1.5 0.5 %collective-permute-start = (bf16[16,2,256]{2,1,0:T(2,128)(2,1)S(1)}, bf16[16,2,256]{2,1,0:T(2,128)(2,1)S(1)}, u32[]{:S(2)}, u32[]{:S(2)}) collective-permute-start(bf16[16,2,256]{2,1,0:T(2,128)(2,1)S(1)} %get-tuple-element.58), channel_id=1, source_target_pairs={{0,4},{1,2},{2,1},{3,7},{4,0},{5,6},{6,5},{7,3},{8,12},{9,10},{10,... | collective-permute-start | bytes 49160 | tf_op jit(solution)/shard_map/ppermute | solution.py:34
  2.0 4.1 %collective-permute-start.1 = (bf16[16,2,256]{2,1,0:T(2,128)(2,1)S(1)}, bf16[16,2,256]{2,1,0:T(2,128)(2,1)S(1)}, u32[]{:S(2)}, u32[]{:S(2)}) collective-permute-start(bf16[16,2,256]{2,1,0:T(2,128)(2,1)S(1)} %get-tuple-element.59), channel_id=1, source_target_pairs={{0,1},{1,0},{2,3},{3,2},{4,5},{5,4},{6,7},{7,6},{8,9},{9,8},{10,11... | collective-permute-start | bytes 49160 | tf_op jit(solution)/shard_map/ppermute | solution.py:20
  6.2 1.4 %load.1 = (bf16[128,256]{1,0:T(8,128)(2,1)S(1)}, bf16[256,128]{1,0:T(8,128)(2,1)S(1)}, bf16[8,128,256]{2,1,0:T(8,128)(2,1)S(1)}, bf16[8,128,256]{2,1,0:T(8,128)(...) custom-call(bf16[3,3,4,128]{3,2,1,0:T(4,128)(2,1)} %refs_0_.1, ...), custom_call_target="tpu_custom_call" | custom-call | tf_op jit(solution)/shard_map/load/pallas_call | solution.py:400
  7.6 0.3 collective-permute-done.1.col_even
  7.9 0.2 edges.1
  8.2 1.6 %collective-permute-start.3 = (bf16[360,256]{1,0:T(8,128)(2,1)S(1)}, bf16[360,256]{1,0:T(8,128)(2,1)S(1)}, u32[]{:S(2)}, u32[]{:S(2)}) collective-permute-start(bf16[360,256]{1,0:T(8,128)(2,1)S(1)} %get-tuple-element.91), channel_id=1, source_target_pairs={{0,16},{1,17},{2,18},{3,19},{4,8},{5,9},{6,10},{7,11},{8,4},{9,5},... | collective-permute-start | bytes 552968 | tf_op jit(solution)/shard_map/ppermute | solution.py:34
  9.8 3.0 %inner.1 = (bf16[8,144,384]{2,1,0:T(8,128)(2,1)S(1)}, bf16[6,144,384]{2,1,0:T(8,128)(2,1)S(1)}, f32[1024,128]{1,0:T(8,128)S(1)}, f32[768,256]{1,0:T(8,128)S(1)},...) custom-call(bf16[8,128,256]{2,1,0:T(8,128)(2,1)S(1)} %get-tuple-elem, ...), custom_call_target="tpu_custom_call" | custom-call | tf_op jit(solution)/shard_map/inner/pallas_call | solution.py:424
  12.9 1.0 %collective-permute-done.3.row_odd = bf16[360,256]{1,0:T(8,128)(2,1)S(1)} collective-permute-done((bf16[360,256]{1,0:T(8,128)(2,1)S(1)}, bf16[360,256]{1,0:T(8,128)(2,1)S(1)}, u32[]{:S(2)}, u32[]{:S(2)}) %collective-permute-start.3) | collective-permute-done | bytes 184352 | tf_op jit(solution)/shard_map/ppermute | solution.py:34
  13.8 1.9 %rim.1 = (f32[2,2,152,128]{3,2,1,0:T(8,128)S(1)}, bf16[512,128]{1,0:T(8,128)(2,1)S(1)}, f32[256,256]{1,0:T(8,128)S(1)}) custom-call(bf16[8,128,256]{2,1,0:T(8,128)(2,1)S(1)} %get-tuple-element.73.x_ref, bf16[8,128,256]{2,1,0:T(8,128)(2,1)S(1)} %get-tuple-element.74.c_ref, bf16[16,16,256]{2,1,0:T(8,128)(2,1)S(1)} %get-tuple-element.80.strip_ref, ...), custom_call_target="tpu_custom_call" | custom-call | tf_op jit(solution)/shard_map/rim/pallas_call | solution.py:443
  15.8 0.2 collective-permute-start.4
  16.0 1.3 %collective-permute-done.4 = f32[2,152,128]{2,1,0:T(8,128)S(1)} collective-permute-done((f32[2,152,128]{2,1,0:T(8,128)S(1)}, f32[2,152,128]{2,1,0:T(8,128)S(1)}, u32[]{:S(2)}, u32[]{:S(2)}) %collective-permute-start.4) | collective-permute-done | bytes 155680 | tf_op jit(solution)/shard_map/ppermute | solution.py:457
  17.3 1.3 %collective-permute-start.5 = (bf16[1,152,128]{2,1,0:T(8,128)(2,1)S(1)}, bf16[1,152,128]{2,1,0:T(8,128)(2,1)S(1)}, u32[]{:S(2)}, u32[]{:S(2)}) collective-permute-start(bf16[1,152,128]{2,1,0:T(8,128)(2,1)S(1)} %slice.15), channel_id=1, source_target_pairs={{0,20},{1,21},{2,22},{3,23},{4,16},{5,17},{6,18},{7,19},{8,28},{9,... | collective-permute-start | bytes 116744 | tf_op jit(solution)/shard_map/ppermute | solution.py:364
  18.6 2.2 %collective-permute-done.5 = bf16[1,152,128]{2,1,0:T(8,128)(2,1)S(1)} collective-permute-done((bf16[1,152,128]{2,1,0:T(8,128)(2,1)S(1)}, bf16[1,152,128]{2,1,0:T(8,128)(2,1)S(1)}, u32[]{:S(2)}, u32[]{:S(2)}) %collective-permute-start.5) | collective-permute-done | bytes 38944 | tf_op jit(solution)/shard_map/ppermute | solution.py:364
  20.9 0.7 %collective-permute-start.6 = (bf16[152,128]{1,0:T(8,128)(2,1)S(1)}, bf16[152,128]{1,0:T(8,128)(2,1)S(1)}, u32[]{:S(2)}, u32[]{:S(2)}) collective-permute-start(bf16[152,128]{1,0:T(8,128)(2,1)S(1)} %fusion.1), channel_id=1, source_target_pairs={{0,12},{1,7},{2,4},{3,15},{4,2},{5,9},{6,10},{7,1},{8,14},{9,5},{1... | collective-permute-start | bytes 116744 | tf_op jit(solution)/shard_map/ppermute | solution.py:364
  21.6 1.1 %out.1 = bf16[8,128,256]{2,1,0:T(8,128)(2,1)} custom-call(bf16[512,128]{1,0:T(8,128)(2,1)S(1)} %get-tuple-element.89.g1_in, bf16[512,128]{1,0:T(8,128)(2,1)S(1)} %get-tuple-element.103.g1_rim, f32[768,256]{1,0:T(8,128)S(1)} %get-tuple-element.104.back_in, f32[256,256]{1,0:T(8,128)S(1)} %get-tuple-element.105.back_rim, ...), custom_call_target="tpu_custom_call" | custom-call | tf_op jit(solution)/shard_map/out/pallas_call | solution.py:459
  22.7 1.6 %collective-permute-done.6 = bf16[152,128]{1,0:T(8,128)(2,1)S(1)} collective-permute-done((bf16[152,128]{1,0:T(8,128)(2,1)S(1)}, bf16[152,128]{1,0:T(8,128)(2,1)S(1)}, u32[]{:S(2)}, u32[]{:S(2)}) %collective-permute-start.6) | collective-permute-done | bytes 38944 | tf_op jit(solution)/shard_map/ppermute | solution.py:364
  24.3 1.7 %collective-permute-start.7 = (bf16[152,128]{1,0:T(8,128)(2,1)S(1)}, bf16[152,128]{1,0:T(8,128)(2,1)S(1)}, u32[]{:S(2)}, u32[]{:S(2)}) collective-permute-start(bf16[152,128]{1,0:T(8,128)(2,1)S(1)} %add_convert_fusion.1), channel_id=1, source_target_pairs={{0,6},{1,4},{2,7},{3,5},{4,1},{5,3},{6,0},{7,2},{8,13},{9,15},{10,... | collective-permute-start | bytes 116744 | tf_op jit(solution)/shard_map/ppermute | solution.py:364
  26.1 2.6 %collective-permute-done.7 = bf16[152,128]{1,0:T(8,128)(2,1)S(1)} collective-permute-done((bf16[152,128]{1,0:T(8,128)(2,1)S(1)}, bf16[152,128]{1,0:T(8,128)(2,1)S(1)}, u32[]{:S(2)}, u32[]{:S(2)}) %collective-permute-start.7) | collective-permute-done | bytes 38944 | tf_op jit(solution)/shard_map/ppermute | solution.py:364
  28.7 1.8 %collective-permute-start.8 = (bf16[152,128]{1,0:T(8,128)(2,1)S(1)}, bf16[152,128]{1,0:T(8,128)(2,1)S(1)}, u32[]{:S(2)}, u32[]{:S(2)}) collective-permute-start(bf16[152,128]{1,0:T(8,128)(2,1)S(1)} %add_convert_fusion), channel_id=1, source_target_pairs={{0,5},{1,13},{2,14},{3,6},{4,8},{5,0},{6,3},{7,11},{8,4},{9,12},{1... | collective-permute-start | bytes 116744 | tf_op jit(solution)/shard_map/ppermute | solution.py:364
  30.6 1.7 %collective-permute-done.8 = bf16[152,128]{1,0:T(8,128)(2,1)S(1)} collective-permute-done((bf16[152,128]{1,0:T(8,128)(2,1)S(1)}, bf16[152,128]{1,0:T(8,128)(2,1)S(1)}, u32[]{:S(2)}, u32[]{:S(2)}) %collective-permute-start.8) | collective-permute-done | bytes 38944 | tf_op jit(solution)/shard_map/ppermute | solution.py:364
  32.3 0.4 %collective-permute-start.9 = (f32[152,128]{1,0:T(8,128)S(1)}, f32[152,128]{1,0:T(8,128)S(1)}, u32[]{:S(2)}, u32[]{:S(2)}) collective-permute-start(f32[152,128]{1,0:T(8,128)S(1)} %convert_add_fusion.a_ref), channel_id=1, source_target_pairs={{0,4},{4,0},{8,12},{12,8},{1,5},{5,1},{9,13},{13,9},{2,6},{6,2},{1... | collective-permute-start | bytes 233480 | tf_op jit(solution)/shard_map/ppermute | solution.py:501
  32.7 0.9 %collective-permute-done.9.b_ref = f32[152,128]{1,0:T(8,128)S(1)} collective-permute-done((f32[152,128]{1,0:T(8,128)S(1)}, f32[152,128]{1,0:T(8,128)S(1)}, u32[]{:S(2)}, u32[]{:S(2)}) %collective-permute-start.9) | collective-permute-done | bytes 77856 | tf_op jit(solution)/shard_map/ppermute | solution.py:501
  33.6 0.7 %last.1 = (f32[128,128]{1,0:T(8,128)}, f32[3,3,4,64]{3,2,1,0:T(4,128)}, f32[64,256]{1,0:T(8,128)}) custom-call(f32[152,128]{1,0:T(8,128)S(1)} %convert_add_fusion.a_ref, f32[152,128]{1,0:T(8,128)S(1)} %collective-permute-done.9.b_ref), custom_call_target="tpu_custom_call" | custom-call | tf_op jit(solution)/shard_map/last/pallas_call | solution.py:482
  (10 shorter events, 0.2 us)
Async XLA Ops:
  1.5 6.1 %collective-permute-start = (bf16[16,2,256]{2,1,0:T(2,128)(2,1)S(1)}, bf16[16,2,256]{2,1,0:T(2,128)(2,1)S(1)}, u32[]{:S(2)}, u32[]{:S(2)}) collective-permute-start(bf16[16,2,256]{2,1,0:T(2,128)(2,1)S(1)} %get-tuple-element.58), channel_id=1, source_target_pairs={{0,4},{1,2},{2,1},{3,7},{4,0},{5,6},{6,5},{7,3},{8,12},{9,10},{10,... | collective-permute-start | bytes 49160 | tf_op jit(solution)/shard_map/ppermute | solution.py:34
  2.0 5.9 %collective-permute-start.1 = (bf16[16,2,256]{2,1,0:T(2,128)(2,1)S(1)}, bf16[16,2,256]{2,1,0:T(2,128)(2,1)S(1)}, u32[]{:S(2)}, u32[]{:S(2)}) collective-permute-start(bf16[16,2,256]{2,1,0:T(2,128)(2,1)S(1)} %get-tuple-element.59), channel_id=1, source_target_pairs={{0,1},{1,0},{2,3},{3,2},{4,5},{5,4},{6,7},{7,6},{8,9},{9,8},{10,11... | collective-permute-start | bytes 49160 | tf_op jit(solution)/shard_map/ppermute | solution.py:20
  8.1 4.7 %collective-permute-start.2 = (bf16[360,256]{1,0:T(8,128)(2,1)S(1)}, bf16[360,256]{1,0:T(8,128)(2,1)S(1)}, u32[]{:S(2)}, u32[]{:S(2)}) collective-permute-start(bf16[360,256]{1,0:T(8,128)(2,1)S(1)} %get-tuple-element.90), channel_id=1, source_target_pairs={{0,4},{4,0},{8,12},{12,8},{1,5},{5,1},{9,13},{13,9},{2,6},{6,2},{1... | collective-permute-start | bytes 552968 | tf_op jit(solution)/shard_map/ppermute | solution.py:20
  8.2 5.6 %collective-permute-start.3 = (bf16[360,256]{1,0:T(8,128)(2,1)S(1)}, bf16[360,256]{1,0:T(8,128)(2,1)S(1)}, u32[]{:S(2)}, u32[]{:S(2)}) collective-permute-start(bf16[360,256]{1,0:T(8,128)(2,1)S(1)} %get-tuple-element.91), channel_id=1, source_target_pairs={{0,16},{1,17},{2,18},{3,19},{4,8},{5,9},{6,10},{7,11},{8,4},{9,5},... | collective-permute-start | bytes 552968 | tf_op jit(solution)/shard_map/ppermute | solution.py:34
  15.8 1.4 %collective-permute-start.4 = (f32[2,152,128]{2,1,0:T(8,128)S(1)}, f32[2,152,128]{2,1,0:T(8,128)S(1)}, u32[]{:S(2)}, u32[]{:S(2)}) collective-permute-start(f32[2,152,128]{2,1,0:T(8,128)S(1)} %slice_bitcast_fusion), channel_id=1, source_target_pairs={{0,4},{4,0},{8,12},{12,8},{1,5},{5,1},{9,13},{13,9},{2,6},{6,2},{1... | collective-permute-start | bytes 466952 | tf_op jit(solution)/shard_map/ppermute | solution.py:457
  17.3 3.6 %collective-permute-start.5 = (bf16[1,152,128]{2,1,0:T(8,128)(2,1)S(1)}, bf16[1,152,128]{2,1,0:T(8,128)(2,1)S(1)}, u32[]{:S(2)}, u32[]{:S(2)}) collective-permute-start(bf16[1,152,128]{2,1,0:T(8,128)(2,1)S(1)} %slice.15), channel_id=1, source_target_pairs={{0,20},{1,21},{2,22},{3,23},{4,16},{5,17},{6,18},{7,19},{8,28},{9,... | collective-permute-start | bytes 116744 | tf_op jit(solution)/shard_map/ppermute | solution.py:364
  20.9 3.5 %collective-permute-start.6 = (bf16[152,128]{1,0:T(8,128)(2,1)S(1)}, bf16[152,128]{1,0:T(8,128)(2,1)S(1)}, u32[]{:S(2)}, u32[]{:S(2)}) collective-permute-start(bf16[152,128]{1,0:T(8,128)(2,1)S(1)} %fusion.1), channel_id=1, source_target_pairs={{0,12},{1,7},{2,4},{3,15},{4,2},{5,9},{6,10},{7,1},{8,14},{9,5},{1... | collective-permute-start | bytes 116744 | tf_op jit(solution)/shard_map/ppermute | solution.py:364
  24.3 4.4 %collective-permute-start.7 = (bf16[152,128]{1,0:T(8,128)(2,1)S(1)}, bf16[152,128]{1,0:T(8,128)(2,1)S(1)}, u32[]{:S(2)}, u32[]{:S(2)}) collective-permute-start(bf16[152,128]{1,0:T(8,128)(2,1)S(1)} %add_convert_fusion.1), channel_id=1, source_target_pairs={{0,6},{1,4},{2,7},{3,5},{4,1},{5,3},{6,0},{7,2},{8,13},{9,15},{10,... | collective-permute-start | bytes 116744 | tf_op jit(solution)/shard_map/ppermute | solution.py:364
  28.7 3.5 %collective-permute-start.8 = (bf16[152,128]{1,0:T(8,128)(2,1)S(1)}, bf16[152,128]{1,0:T(8,128)(2,1)S(1)}, u32[]{:S(2)}, u32[]{:S(2)}) collective-permute-start(bf16[152,128]{1,0:T(8,128)(2,1)S(1)} %add_convert_fusion), channel_id=1, source_target_pairs={{0,5},{1,13},{2,14},{3,6},{4,8},{5,0},{6,3},{7,11},{8,4},{9,12},{1... | collective-permute-start | bytes 116744 | tf_op jit(solution)/shard_map/ppermute | solution.py:364
  32.3 1.3 %collective-permute-start.9 = (f32[152,128]{1,0:T(8,128)S(1)}, f32[152,128]{1,0:T(8,128)S(1)}, u32[]{:S(2)}, u32[]{:S(2)}) collective-permute-start(f32[152,128]{1,0:T(8,128)S(1)} %convert_add_fusion.a_ref), channel_id=1, source_target_pairs={{0,4},{4,0},{8,12},{12,8},{1,5},{5,1},{9,13},{13,9},{2,6},{6,2},{1... | collective-permute-start | bytes 233480 | tf_op jit(solution)/shard_map/ppermute | solution.py:501

commit v8 on v7

--- a/solution.py
+++ b/solution.py
@@ -331,22 +331,23 @@
     a_ref, b_ref, r_out, g_out, e_out, r_ref, g_ref, e_ref, sems, *, scale, one, three, chans, inner, group_ch
 ):
     other_first = parity_of_place() == 1
+    copies = [
+        pltpu.make_async_copy(src, dst, sems.at[i])
+        for i, (src, dst) in enumerate(((r_ref, r_out), (e_ref, e_out), (g_ref, g_out)))
+    ]
     first = jnp.where(other_first, b_ref[...], a_ref[...]) * scale
+    r_ref[...] = first[0:one]
+    copies[0].start()
     second = jnp.where(other_first, a_ref[...], b_ref[...]) * scale
-    r_ref[...] = first[0:one]
     for k in range(chans // inner):
         e_ref[:, k * inner : (k + 1) * inner] = second[k * three : (k + 1) * three]
+    copies[1].start()
     for t in range(9):
         at = t * group_ch
         part = first[one + at : one + at + group_ch] if at < GROUP_ROWS else second[
             one + at - GROUP_ROWS : one + at - GROUP_ROWS + group_ch]
         g_ref[t // 3, t % 3] = part[:, 0:three]
-    copies = [
-        pltpu.make_async_copy(src, dst, sems.at[i])
-        for i, (src, dst) in enumerate(((r_ref, r_out), (e_ref, e_out), (g_ref, g_out)))
-    ]
-    for copy in copies:
-        copy.start()
+    copies[2].start()
     for copy in copies:
         copy.wait()
 

time: 34.5 us -> 34.5 us (level)
  no operation moved by 1% of the time
where the time goes in v8:
time: 34.5 us; the launch traced here: 34.3 us
  starting transfers between devices  12.6 us (37%)
  waiting for transfers between devices  11.6 us (34%)
  Pallas kernels  9.28 us (27%)
  between operations  0.73 us (2%)
    ppermute x4, waiting for transfers between devices, crossed(): return lax.ppermute(value, names, perm)  8.17 us
    ppermute x4, starting transfers between devices, crossed(): return lax.ppermute(value, names, perm)  5.65 us
    ppermute x2, starting transfers between devices, swap_edges(): got_even = lax.ppermute(to_even, axis, [(i, i ^ 1) for i in range(count)])  4.22 us
    pallas_call x1, Pallas kernels, body(): pl.pallas_call(functools.partial(inner_kernel, inner=inner, **sizes), out...  3.04 us
    ppermute x2, starting transfers between devices, swap_edges(): got_odd = lax.ppermute(to_odd, names, perm)  2.1 us
    pallas_call x1, Pallas kernels, body(): pl.pallas_call(functools.partial(rim_kernel, inner=inner, group_ch=group_...  1.94 us
    pallas_call x1, Pallas kernels, body(): pl.pallas_call(functools.partial(load_kernel, inner=inner, group_ch=group...  1.4 us
    ppermute x1, waiting for transfers between devices, body(): shares = (shares[0] + lax.ppermute(shares[1], 'row', near)).astype(BF)  1.27 us
  transfers between devices with their start and end apart: 10, of which 8 were waited for; matrix products, arithmetic and copies ran while one was open for 0% of the time, Pallas kernels for 16%

profile of v8, /device:TPU:0, one launch (start us, length us, event | category | flops | bytes accessed | tf_op | source)
XLA Modules:
  0.0 34.3 jit_solution(10802247653736936726)
XLA Ops:
  0.6 0.9 %cut.1 = (bf16[16,2,256]{2,1,0:T(2,128)(2,1)S(1)}, bf16[16,2,256]{2,1,0:T(2,128)(2,1)S(1)}) custom-call(bf16[8,128,256]{2,1,0:T(8,128)(2,1)} %bitcast.18, bf16[8,128,256]{2,1,0:T(8,128)(2,1)} %bitcast.20), custom_call_target="tpu_custom_call" | custom-call | tf_op jit(solution)/shard_map/cut/pallas_call | solution.py:387
  1.5 0.5 %collective-permute-start = (bf16[16,2,256]{2,1,0:T(2,128)(2,1)S(1)}, bf16[16,2,256]{2,1,0:T(2,128)(2,1)S(1)}, u32[]{:S(2)}, u32[]{:S(2)}) collective-permute-start(bf16[16,2,256]{2,1,0:T(2,128)(2,1)S(1)} %get-tuple-element.58), channel_id=1, source_target_pairs={{0,4},{1,2},{2,1},{3,7},{4,0},{5,6},{6,5},{7,3},{8,12},{9,10},{10,... | collective-permute-start | bytes 49160 | tf_op jit(solution)/shard_map/ppermute | solution.py:34
  2.0 4.1 %collective-permute-start.1 = (bf16[16,2,256]{2,1,0:T(2,128)(2,1)S(1)}, bf16[16,2,256]{2,1,0:T(2,128)(2,1)S(1)}, u32[]{:S(2)}, u32[]{:S(2)}) collective-permute-start(bf16[16,2,256]{2,1,0:T(2,128)(2,1)S(1)} %get-tuple-element.59), channel_id=1, source_target_pairs={{0,1},{1,0},{2,3},{3,2},{4,5},{5,4},{6,7},{7,6},{8,9},{9,8},{10,11... | collective-permute-start | bytes 49160 | tf_op jit(solution)/shard_map/ppermute | solution.py:20
  6.2 1.4 %load.1 = (bf16[128,256]{1,0:T(8,128)(2,1)S(1)}, bf16[256,128]{1,0:T(8,128)(2,1)S(1)}, bf16[8,128,256]{2,1,0:T(8,128)(2,1)S(1)}, bf16[8,128,256]{2,1,0:T(8,128)(...) custom-call(bf16[3,3,4,128]{3,2,1,0:T(4,128)(2,1)} %refs_0_.1, ...), custom_call_target="tpu_custom_call" | custom-call | tf_op jit(solution)/shard_map/load/pallas_call | solution.py:401
  7.6 0.3 collective-permute-done.1.col_even
  7.9 0.2 edges.1
  8.2 1.6 %collective-permute-start.3 = (bf16[360,256]{1,0:T(8,128)(2,1)S(1)}, bf16[360,256]{1,0:T(8,128)(2,1)S(1)}, u32[]{:S(2)}, u32[]{:S(2)}) collective-permute-start(bf16[360,256]{1,0:T(8,128)(2,1)S(1)} %get-tuple-element.91), channel_id=1, source_target_pairs={{0,16},{1,17},{2,18},{3,19},{4,8},{5,9},{6,10},{7,11},{8,4},{9,5},... | collective-permute-start | bytes 552968 | tf_op jit(solution)/shard_map/ppermute | solution.py:34
  9.8 3.0 %inner.1 = (bf16[8,144,384]{2,1,0:T(8,128)(2,1)S(1)}, bf16[6,144,384]{2,1,0:T(8,128)(2,1)S(1)}, f32[1024,128]{1,0:T(8,128)S(1)}, f32[768,256]{1,0:T(8,128)S(1)},...) custom-call(bf16[8,128,256]{2,1,0:T(8,128)(2,1)S(1)} %get-tuple-elem, ...), custom_call_target="tpu_custom_call" | custom-call | tf_op jit(solution)/shard_map/inner/pallas_call | solution.py:425
  12.9 1.0 %collective-permute-done.3.row_odd = bf16[360,256]{1,0:T(8,128)(2,1)S(1)} collective-permute-done((bf16[360,256]{1,0:T(8,128)(2,1)S(1)}, bf16[360,256]{1,0:T(8,128)(2,1)S(1)}, u32[]{:S(2)}, u32[]{:S(2)}) %collective-permute-start.3) | collective-permute-done | bytes 184352 | tf_op jit(solution)/shard_map/ppermute | solution.py:34
  13.8 1.9 %rim.1 = (f32[2,2,152,128]{3,2,1,0:T(8,128)S(1)}, bf16[512,128]{1,0:T(8,128)(2,1)S(1)}, f32[256,256]{1,0:T(8,128)S(1)}) custom-call(bf16[8,128,256]{2,1,0:T(8,128)(2,1)S(1)} %get-tuple-element.73.x_ref, bf16[8,128,256]{2,1,0:T(8,128)(2,1)S(1)} %get-tuple-element.74.c_ref, bf16[16,16,256]{2,1,0:T(8,128)(2,1)S(1)} %get-tuple-element.80.strip_ref, ...), custom_call_target="tpu_custom_call" | custom-call | tf_op jit(solution)/shard_map/rim/pallas_call | solution.py:444
  15.8 0.2 collective-permute-start.4
  16.0 1.3 %collective-permute-done.4 = f32[2,152,128]{2,1,0:T(8,128)S(1)} collective-permute-done((f32[2,152,128]{2,1,0:T(8,128)S(1)}, f32[2,152,128]{2,1,0:T(8,128)S(1)}, u32[]{:S(2)}, u32[]{:S(2)}) %collective-permute-start.4) | collective-permute-done | bytes 155680 | tf_op jit(solution)/shard_map/ppermute | solution.py:458
  17.3 1.3 %collective-permute-start.5 = (bf16[1,152,128]{2,1,0:T(8,128)(2,1)S(1)}, bf16[1,152,128]{2,1,0:T(8,128)(2,1)S(1)}, u32[]{:S(2)}, u32[]{:S(2)}) collective-permute-start(bf16[1,152,128]{2,1,0:T(8,128)(2,1)S(1)} %slice.15), channel_id=1, source_target_pairs={{0,20},{1,21},{2,22},{3,23},{4,16},{5,17},{6,18},{7,19},{8,28},{9,... | collective-permute-start | bytes 116744 | tf_op jit(solution)/shard_map/ppermute | solution.py:365
  18.6 2.2 %collective-permute-done.5 = bf16[1,152,128]{2,1,0:T(8,128)(2,1)S(1)} collective-permute-done((bf16[1,152,128]{2,1,0:T(8,128)(2,1)S(1)}, bf16[1,152,128]{2,1,0:T(8,128)(2,1)S(1)}, u32[]{:S(2)}, u32[]{:S(2)}) %collective-permute-start.5) | collective-permute-done | bytes 38944 | tf_op jit(solution)/shard_map/ppermute | solution.py:365
  20.9 0.7 %collective-permute-start.6 = (bf16[152,128]{1,0:T(8,128)(2,1)S(1)}, bf16[152,128]{1,0:T(8,128)(2,1)S(1)}, u32[]{:S(2)}, u32[]{:S(2)}) collective-permute-start(bf16[152,128]{1,0:T(8,128)(2,1)S(1)} %fusion.1), channel_id=1, source_target_pairs={{0,12},{1,7},{2,4},{3,15},{4,2},{5,9},{6,10},{7,1},{8,14},{9,5},{1... | collective-permute-start | bytes 116744 | tf_op jit(solution)/shard_map/ppermute | solution.py:365
  21.6 1.1 %out.1 = bf16[8,128,256]{2,1,0:T(8,128)(2,1)} custom-call(bf16[512,128]{1,0:T(8,128)(2,1)S(1)} %get-tuple-element.89.g1_in, bf16[512,128]{1,0:T(8,128)(2,1)S(1)} %get-tuple-element.103.g1_rim, f32[768,256]{1,0:T(8,128)S(1)} %get-tuple-element.104.back_in, f32[256,256]{1,0:T(8,128)S(1)} %get-tuple-element.105.back_rim, ...), custom_call_target="tpu_custom_call" | custom-call | tf_op jit(solution)/shard_map/out/pallas_call | solution.py:460
  22.7 1.6 %collective-permute-done.6 = bf16[152,128]{1,0:T(8,128)(2,1)S(1)} collective-permute-done((bf16[152,128]{1,0:T(8,128)(2,1)S(1)}, bf16[152,128]{1,0:T(8,128)(2,1)S(1)}, u32[]{:S(2)}, u32[]{:S(2)}) %collective-permute-start.6) | collective-permute-done | bytes 38944 | tf_op jit(solution)/shard_map/ppermute | solution.py:365
  24.3 1.7 %collective-permute-start.7 = (bf16[152,128]{1,0:T(8,128)(2,1)S(1)}, bf16[152,128]{1,0:T(8,128)(2,1)S(1)}, u32[]{:S(2)}, u32[]{:S(2)}) collective-permute-start(bf16[152,128]{1,0:T(8,128)(2,1)S(1)} %add_convert_fusion.1), channel_id=1, source_target_pairs={{0,6},{1,4},{2,7},{3,5},{4,1},{5,3},{6,0},{7,2},{8,13},{9,15},{10,... | collective-permute-start | bytes 116744 | tf_op jit(solution)/shard_map/ppermute | solution.py:365
  26.1 2.6 %collective-permute-done.7 = bf16[152,128]{1,0:T(8,128)(2,1)S(1)} collective-permute-done((bf16[152,128]{1,0:T(8,128)(2,1)S(1)}, bf16[152,128]{1,0:T(8,128)(2,1)S(1)}, u32[]{:S(2)}, u32[]{:S(2)}) %collective-permute-start.7) | collective-permute-done | bytes 38944 | tf_op jit(solution)/shard_map/ppermute | solution.py:365
  28.7 1.8 %collective-permute-start.8 = (bf16[152,128]{1,0:T(8,128)(2,1)S(1)}, bf16[152,128]{1,0:T(8,128)(2,1)S(1)}, u32[]{:S(2)}, u32[]{:S(2)}) collective-permute-start(bf16[152,128]{1,0:T(8,128)(2,1)S(1)} %add_convert_fusion), channel_id=1, source_target_pairs={{0,5},{1,13},{2,14},{3,6},{4,8},{5,0},{6,3},{7,11},{8,4},{9,12},{1... | collective-permute-start | bytes 116744 | tf_op jit(solution)/shard_map/ppermute | solution.py:365
  30.6 1.7 %collective-permute-done.8 = bf16[152,128]{1,0:T(8,128)(2,1)S(1)} collective-permute-done((bf16[152,128]{1,0:T(8,128)(2,1)S(1)}, bf16[152,128]{1,0:T(8,128)(2,1)S(1)}, u32[]{:S(2)}, u32[]{:S(2)}) %collective-permute-start.8) | collective-permute-done | bytes 38944 | tf_op jit(solution)/shard_map/ppermute | solution.py:365
  32.3 0.4 %collective-permute-start.9 = (f32[152,128]{1,0:T(8,128)S(1)}, f32[152,128]{1,0:T(8,128)S(1)}, u32[]{:S(2)}, u32[]{:S(2)}) collective-permute-start(f32[152,128]{1,0:T(8,128)S(1)} %convert_add_fusion.a_ref), channel_id=1, source_target_pairs={{0,4},{4,0},{8,12},{12,8},{1,5},{5,1},{9,13},{13,9},{2,6},{6,2},{1... | collective-permute-start | bytes 233480 | tf_op jit(solution)/shard_map/ppermute | solution.py:502
  32.7 0.9 %collective-permute-done.9.b_ref = f32[152,128]{1,0:T(8,128)S(1)} collective-permute-done((f32[152,128]{1,0:T(8,128)S(1)}, f32[152,128]{1,0:T(8,128)S(1)}, u32[]{:S(2)}, u32[]{:S(2)}) %collective-permute-start.9) | collective-permute-done | bytes 77856 | tf_op jit(solution)/shard_map/ppermute | solution.py:502
  33.6 0.7 %last.1 = (f32[128,128]{1,0:T(8,128)}, f32[3,3,4,64]{3,2,1,0:T(4,128)}, f32[64,256]{1,0:T(8,128)}) custom-call(f32[152,128]{1,0:T(8,128)S(1)} %convert_add_fusion.a_ref, f32[152,128]{1,0:T(8,128)S(1)} %collective-permute-done.9.b_ref), custom_call_target="tpu_custom_call" | custom-call | tf_op jit(solution)/shard_map/last/pallas_call | solution.py:483
  (10 shorter events, 0.2 us)
Async XLA Ops:
  1.5 6.1 %collective-permute-start = (bf16[16,2,256]{2,1,0:T(2,128)(2,1)S(1)}, bf16[16,2,256]{2,1,0:T(2,128)(2,1)S(1)}, u32[]{:S(2)}, u32[]{:S(2)}) collective-permute-start(bf16[16,2,256]{2,1,0:T(2,128)(2,1)S(1)} %get-tuple-element.58), channel_id=1, source_target_pairs={{0,4},{1,2},{2,1},{3,7},{4,0},{5,6},{6,5},{7,3},{8,12},{9,10},{10,... | collective-permute-start | bytes 49160 | tf_op jit(solution)/shard_map/ppermute | solution.py:34
  2.0 5.9 %collective-permute-start.1 = (bf16[16,2,256]{2,1,0:T(2,128)(2,1)S(1)}, bf16[16,2,256]{2,1,0:T(2,128)(2,1)S(1)}, u32[]{:S(2)}, u32[]{:S(2)}) collective-permute-start(bf16[16,2,256]{2,1,0:T(2,128)(2,1)S(1)} %get-tuple-element.59), channel_id=1, source_target_pairs={{0,1},{1,0},{2,3},{3,2},{4,5},{5,4},{6,7},{7,6},{8,9},{9,8},{10,11... | collective-permute-start | bytes 49160 | tf_op jit(solution)/shard_map/ppermute | solution.py:20
  8.1 4.7 %collective-permute-start.2 = (bf16[360,256]{1,0:T(8,128)(2,1)S(1)}, bf16[360,256]{1,0:T(8,128)(2,1)S(1)}, u32[]{:S(2)}, u32[]{:S(2)}) collective-permute-start(bf16[360,256]{1,0:T(8,128)(2,1)S(1)} %get-tuple-element.90), channel_id=1, source_target_pairs={{0,4},{4,0},{8,12},{12,8},{1,5},{5,1},{9,13},{13,9},{2,6},{6,2},{1... | collective-permute-start | bytes 552968 | tf_op jit(solution)/shard_map/ppermute | solution.py:20
  8.2 5.6 %collective-permute-start.3 = (bf16[360,256]{1,0:T(8,128)(2,1)S(1)}, bf16[360,256]{1,0:T(8,128)(2,1)S(1)}, u32[]{:S(2)}, u32[]{:S(2)}) collective-permute-start(bf16[360,256]{1,0:T(8,128)(2,1)S(1)} %get-tuple-element.91), channel_id=1, source_target_pairs={{0,16},{1,17},{2,18},{3,19},{4,8},{5,9},{6,10},{7,11},{8,4},{9,5},... | collective-permute-start | bytes 552968 | tf_op jit(solution)/shard_map/ppermute | solution.py:34
  15.8 1.4 %collective-permute-start.4 = (f32[2,152,128]{2,1,0:T(8,128)S(1)}, f32[2,152,128]{2,1,0:T(8,128)S(1)}, u32[]{:S(2)}, u32[]{:S(2)}) collective-permute-start(f32[2,152,128]{2,1,0:T(8,128)S(1)} %slice_bitcast_fusion), channel_id=1, source_target_pairs={{0,4},{4,0},{8,12},{12,8},{1,5},{5,1},{9,13},{13,9},{2,6},{6,2},{1... | collective-permute-start | bytes 466952 | tf_op jit(solution)/shard_map/ppermute | solution.py:458
  17.3 3.6 %collective-permute-start.5 = (bf16[1,152,128]{2,1,0:T(8,128)(2,1)S(1)}, bf16[1,152,128]{2,1,0:T(8,128)(2,1)S(1)}, u32[]{:S(2)}, u32[]{:S(2)}) collective-permute-start(bf16[1,152,128]{2,1,0:T(8,128)(2,1)S(1)} %slice.15), channel_id=1, source_target_pairs={{0,20},{1,21},{2,22},{3,23},{4,16},{5,17},{6,18},{7,19},{8,28},{9,... | collective-permute-start | bytes 116744 | tf_op jit(solution)/shard_map/ppermute | solution.py:365
  20.9 3.5 %collective-permute-start.6 = (bf16[152,128]{1,0:T(8,128)(2,1)S(1)}, bf16[152,128]{1,0:T(8,128)(2,1)S(1)}, u32[]{:S(2)}, u32[]{:S(2)}) collective-permute-start(bf16[152,128]{1,0:T(8,128)(2,1)S(1)} %fusion.1), channel_id=1, source_target_pairs={{0,12},{1,7},{2,4},{3,15},{4,2},{5,9},{6,10},{7,1},{8,14},{9,5},{1... | collective-permute-start | bytes 116744 | tf_op jit(solution)/shard_map/ppermute | solution.py:365
  24.3 4.4 %collective-permute-start.7 = (bf16[152,128]{1,0:T(8,128)(2,1)S(1)}, bf16[152,128]{1,0:T(8,128)(2,1)S(1)}, u32[]{:S(2)}, u32[]{:S(2)}) collective-permute-start(bf16[152,128]{1,0:T(8,128)(2,1)S(1)} %add_convert_fusion.1), channel_id=1, source_target_pairs={{0,6},{1,4},{2,7},{3,5},{4,1},{5,3},{6,0},{7,2},{8,13},{9,15},{10,... | collective-permute-start | bytes 116744 | tf_op jit(solution)/shard_map/ppermute | solution.py:365
  28.7 3.5 %collective-permute-start.8 = (bf16[152,128]{1,0:T(8,128)(2,1)S(1)}, bf16[152,128]{1,0:T(8,128)(2,1)S(1)}, u32[]{:S(2)}, u32[]{:S(2)}) collective-permute-start(bf16[152,128]{1,0:T(8,128)(2,1)S(1)} %add_convert_fusion), channel_id=1, source_target_pairs={{0,5},{1,13},{2,14},{3,6},{4,8},{5,0},{6,3},{7,11},{8,4},{9,12},{1... | collective-permute-start | bytes 116744 | tf_op jit(solution)/shard_map/ppermute | solution.py:365
  32.3 1.3 %collective-permute-start.9 = (f32[152,128]{1,0:T(8,128)S(1)}, f32[152,128]{1,0:T(8,128)S(1)}, u32[]{:S(2)}, u32[]{:S(2)}) collective-permute-start(f32[152,128]{1,0:T(8,128)S(1)} %convert_add_fusion.a_ref), channel_id=1, source_target_pairs={{0,4},{4,0},{8,12},{12,8},{1,5},{5,1},{9,13},{13,9},{2,6},{6,2},{1... | collective-permute-start | bytes 233480 | tf_op jit(solution)/shard_map/ppermute | solution.py:502

commit v9 on v8

--- a/solution.py
+++ b/solution.py
@@ -12,7 +12,7 @@
 F32 = jnp.float32
 EDGE = 2
 STRIP = 16
-GROUP_ROWS = 24
+GROUP_ROWS = 16
 
 
 def swap_edges(to_even, to_odd, axis):
@@ -308,8 +308,11 @@
                 h * three : (h + 1) * three, k * inner : (k + 1) * inner
             ]
         group = gw2 if h == 0 else pltpu.roll(gw2, inner - h * three, 1)
-        share_ref[at[0], slot, one : one + GROUP_ROWS, :] = group[0:GROUP_ROWS]
-        share_ref[at[1], slot, one : one + GROUP_ROWS, :] = group[GROUP_ROWS : 2 * GROUP_ROWS]
+        part, half = 3 * group_ch, inner // 2
+        left = lax.broadcasted_iota(jnp.int32, (GROUP_ROWS, inner), 1) < half
+        beside = pltpu.roll(group, half, 1)[part : part + GROUP_ROWS]
+        share_ref[at[0], slot, one : one + GROUP_ROWS, :] = jnp.where(left, group[0:GROUP_ROWS], beside)
+        share_ref[at[1], slot, one : one + GROUP_ROWS, :] = group[2 * part : 2 * part + GROUP_ROWS]
 
 
 def out_kernel(g1_in, g1_rim, back_in, back_rim, w1_ref, out_ref, *, rows, cols, chans):
@@ -343,10 +346,10 @@
         e_ref[:, k * inner : (k + 1) * inner] = second[k * three : (k + 1) * three]
     copies[1].start()
     for t in range(9):
-        at = t * group_ch
-        part = first[one + at : one + at + group_ch] if at < GROUP_ROWS else second[
-            one + at - GROUP_ROWS : one + at - GROUP_ROWS + group_ch]
-        g_ref[t // 3, t % 3] = part[:, 0:three]
+        at = one + t % 3 * group_ch
+        side = inner // 2 if t // 3 == 1 else 0
+        part = (second if t // 3 == 2 else first)[at : at + group_ch]
+        g_ref[t // 3, t % 3] = part[:, side : side + three]
     copies[2].start()
     for copy in copies:
         copy.wait()

time: 34.5 us -> 34.4 us (level)
  no operation moved by 1% of the time
where the time goes in v9:
time: 34.4 us; the launch traced here: 34.2 us
  starting transfers between devices  12.6 us (37%)
  waiting for transfers between devices  11.5 us (33%)
  Pallas kernels  9.32 us (27%)
  between operations  0.73 us (2%)
    ppermute x4, waiting for transfers between devices, crossed(): return lax.ppermute(value, names, perm)  8.05 us
    ppermute x4, starting transfers between devices, crossed(): return lax.ppermute(value, names, perm)  5.64 us
    ppermute x2, starting transfers between devices, swap_edges(): got_even = lax.ppermute(to_even, axis, [(i, i ^ 1) for i in range(count)])  4.22 us
    pallas_call x1, Pallas kernels, body(): pl.pallas_call(functools.partial(inner_kernel, inner=inner, **sizes), out...  3.04 us
    ppermute x2, starting transfers between devices, swap_edges(): got_odd = lax.ppermute(to_odd, names, perm)  2.1 us
    pallas_call x1, Pallas kernels, body(): pl.pallas_call(functools.partial(rim_kernel, inner=inner, group_ch=group_...  1.95 us
    pallas_call x1, Pallas kernels, body(): pl.pallas_call(functools.partial(load_kernel, inner=inner, group_ch=group...  1.4 us
    ppermute x1, waiting for transfers between devices, body(): shares = (shares[0] + lax.ppermute(shares[1], 'row', near)).astype(BF)  1.26 us
  transfers between devices with their start and end apart: 10, of which 8 were waited for; matrix products, arithmetic and copies ran while one was open for 0% of the time, Pallas kernels for 16%

profile of v9, /device:TPU:0, one launch (start us, length us, event | category | flops | bytes accessed | tf_op | source)
XLA Modules:
  0.0 34.2 jit_solution(9802685014231738483)
XLA Ops:
  0.6 0.9 %cut.1 = (bf16[16,2,256]{2,1,0:T(2,128)(2,1)S(1)}, bf16[16,2,256]{2,1,0:T(2,128)(2,1)S(1)}) custom-call(bf16[8,128,256]{2,1,0:T(8,128)(2,1)} %bitcast.18, bf16[8,128,256]{2,1,0:T(8,128)(2,1)} %bitcast.20), custom_call_target="tpu_custom_call" | custom-call | tf_op jit(solution)/shard_map/cut/pallas_call | solution.py:390
  1.5 0.5 %collective-permute-start = (bf16[16,2,256]{2,1,0:T(2,128)(2,1)S(1)}, bf16[16,2,256]{2,1,0:T(2,128)(2,1)S(1)}, u32[]{:S(2)}, u32[]{:S(2)}) collective-permute-start(bf16[16,2,256]{2,1,0:T(2,128)(2,1)S(1)} %get-tuple-element.58), channel_id=1, source_target_pairs={{0,4},{1,2},{2,1},{3,7},{4,0},{5,6},{6,5},{7,3},{8,12},{9,10},{10,... | collective-permute-start | bytes 49160 | tf_op jit(solution)/shard_map/ppermute | solution.py:34
  2.0 4.1 %collective-permute-start.1 = (bf16[16,2,256]{2,1,0:T(2,128)(2,1)S(1)}, bf16[16,2,256]{2,1,0:T(2,128)(2,1)S(1)}, u32[]{:S(2)}, u32[]{:S(2)}) collective-permute-start(bf16[16,2,256]{2,1,0:T(2,128)(2,1)S(1)} %get-tuple-element.59), channel_id=1, source_target_pairs={{0,1},{1,0},{2,3},{3,2},{4,5},{5,4},{6,7},{7,6},{8,9},{9,8},{10,11... | collective-permute-start | bytes 49160 | tf_op jit(solution)/shard_map/ppermute | solution.py:20
  6.2 1.4 %load.1 = (bf16[128,256]{1,0:T(8,128)(2,1)S(1)}, bf16[256,128]{1,0:T(8,128)(2,1)S(1)}, bf16[8,128,256]{2,1,0:T(8,128)(2,1)S(1)}, bf16[8,128,256]{2,1,0:T(8,128)(...) custom-call(bf16[3,3,4,128]{3,2,1,0:T(4,128)(2,1)} %refs_0_.1, ...), custom_call_target="tpu_custom_call" | custom-call | tf_op jit(solution)/shard_map/load/pallas_call | solution.py:404
  7.6 0.3 collective-permute-done.1.col_even
  7.9 0.2 edges.1
  8.2 1.6 %collective-permute-start.3 = (bf16[360,256]{1,0:T(8,128)(2,1)S(1)}, bf16[360,256]{1,0:T(8,128)(2,1)S(1)}, u32[]{:S(2)}, u32[]{:S(2)}) collective-permute-start(bf16[360,256]{1,0:T(8,128)(2,1)S(1)} %get-tuple-element.91), channel_id=1, source_target_pairs={{0,16},{1,17},{2,18},{3,19},{4,8},{5,9},{6,10},{7,11},{8,4},{9,5},... | collective-permute-start | bytes 552968 | tf_op jit(solution)/shard_map/ppermute | solution.py:34
  9.8 3.0 %inner.1 = (bf16[8,144,384]{2,1,0:T(8,128)(2,1)S(1)}, bf16[6,144,384]{2,1,0:T(8,128)(2,1)S(1)}, f32[1024,128]{1,0:T(8,128)S(1)}, f32[768,256]{1,0:T(8,128)S(1)},...) custom-call(bf16[8,128,256]{2,1,0:T(8,128)(2,1)S(1)} %get-tuple-elem, ...), custom_call_target="tpu_custom_call" | custom-call | tf_op jit(solution)/shard_map/inner/pallas_call | solution.py:428
  12.9 1.0 %collective-permute-done.3.row_odd = bf16[360,256]{1,0:T(8,128)(2,1)S(1)} collective-permute-done((bf16[360,256]{1,0:T(8,128)(2,1)S(1)}, bf16[360,256]{1,0:T(8,128)(2,1)S(1)}, u32[]{:S(2)}, u32[]{:S(2)}) %collective-permute-start.3) | collective-permute-done | bytes 184352 | tf_op jit(solution)/shard_map/ppermute | solution.py:34
  13.8 2.0 %rim.1 = (f32[2,2,144,128]{3,2,1,0:T(8,128)S(1)}, bf16[512,128]{1,0:T(8,128)(2,1)S(1)}, f32[256,256]{1,0:T(8,128)S(1)}) custom-call(bf16[8,128,256]{2,1,0:T(8,128)(2,1)S(1)} %get-tuple-element.73.x_ref, bf16[8,128,256]{2,1,0:T(8,128)(2,1)S(1)} %get-tuple-element.74.c_ref, bf16[16,16,256]{2,1,0:T(8,128)(2,1)S(1)} %get-tuple-element.80.strip_ref, ...), custom_call_target="tpu_custom_call" | custom-call | tf_op jit(solution)/shard_map/rim/pallas_call | solution.py:447
  15.8 0.2 collective-permute-start.4
  16.0 1.3 %collective-permute-done.4 = f32[2,144,128]{2,1,0:T(8,128)S(1)} collective-permute-done((f32[2,144,128]{2,1,0:T(8,128)S(1)}, f32[2,144,128]{2,1,0:T(8,128)S(1)}, u32[]{:S(2)}, u32[]{:S(2)}) %collective-permute-start.4) | collective-permute-done | bytes 147488 | tf_op jit(solution)/shard_map/ppermute | solution.py:461
  17.3 1.3 %collective-permute-start.5 = (bf16[1,144,128]{2,1,0:T(8,128)(2,1)S(1)}, bf16[1,144,128]{2,1,0:T(8,128)(2,1)S(1)}, u32[]{:S(2)}, u32[]{:S(2)}) collective-permute-start(bf16[1,144,128]{2,1,0:T(8,128)(2,1)S(1)} %slice.15), channel_id=1, source_target_pairs={{0,20},{1,21},{2,22},{3,23},{4,16},{5,17},{6,18},{7,19},{8,28},{9,... | collective-permute-start | bytes 110600 | tf_op jit(solution)/shard_map/ppermute | solution.py:368
  18.6 2.2 %collective-permute-done.5 = bf16[1,144,128]{2,1,0:T(8,128)(2,1)S(1)} collective-permute-done((bf16[1,144,128]{2,1,0:T(8,128)(2,1)S(1)}, bf16[1,144,128]{2,1,0:T(8,128)(2,1)S(1)}, u32[]{:S(2)}, u32[]{:S(2)}) %collective-permute-start.5) | collective-permute-done | bytes 36896 | tf_op jit(solution)/shard_map/ppermute | solution.py:368
  20.8 0.7 %collective-permute-start.6 = (bf16[144,128]{1,0:T(8,128)(2,1)S(1)}, bf16[144,128]{1,0:T(8,128)(2,1)S(1)}, u32[]{:S(2)}, u32[]{:S(2)}) collective-permute-start(bf16[144,128]{1,0:T(8,128)(2,1)S(1)} %fusion.1), channel_id=1, source_target_pairs={{0,12},{1,7},{2,4},{3,15},{4,2},{5,9},{6,10},{7,1},{8,14},{9,5},{1... | collective-permute-start | bytes 110600 | tf_op jit(solution)/shard_map/ppermute | solution.py:368
  21.5 1.1 %out.1 = bf16[8,128,256]{2,1,0:T(8,128)(2,1)} custom-call(bf16[512,128]{1,0:T(8,128)(2,1)S(1)} %get-tuple-element.89.g1_in, bf16[512,128]{1,0:T(8,128)(2,1)S(1)} %get-tuple-element.103.g1_rim, f32[768,256]{1,0:T(8,128)S(1)} %get-tuple-element.104.back_in, f32[256,256]{1,0:T(8,128)S(1)} %get-tuple-element.105.back_rim, ...), custom_call_target="tpu_custom_call" | custom-call | tf_op jit(solution)/shard_map/out/pallas_call | solution.py:463
  22.6 1.6 %collective-permute-done.6 = bf16[144,128]{1,0:T(8,128)(2,1)S(1)} collective-permute-done((bf16[144,128]{1,0:T(8,128)(2,1)S(1)}, bf16[144,128]{1,0:T(8,128)(2,1)S(1)}, u32[]{:S(2)}, u32[]{:S(2)}) %collective-permute-start.6) | collective-permute-done | bytes 36896 | tf_op jit(solution)/shard_map/ppermute | solution.py:368
  24.3 1.7 %collective-permute-start.7 = (bf16[144,128]{1,0:T(8,128)(2,1)S(1)}, bf16[144,128]{1,0:T(8,128)(2,1)S(1)}, u32[]{:S(2)}, u32[]{:S(2)}) collective-permute-start(bf16[144,128]{1,0:T(8,128)(2,1)S(1)} %add_convert_fusion.1), channel_id=1, source_target_pairs={{0,6},{1,4},{2,7},{3,5},{4,1},{5,3},{6,0},{7,2},{8,13},{9,15},{10,... | collective-permute-start | bytes 110600 | tf_op jit(solution)/shard_map/ppermute | solution.py:368
  26.0 2.6 %collective-permute-done.7 = bf16[144,128]{1,0:T(8,128)(2,1)S(1)} collective-permute-done((bf16[144,128]{1,0:T(8,128)(2,1)S(1)}, bf16[144,128]{1,0:T(8,128)(2,1)S(1)}, u32[]{:S(2)}, u32[]{:S(2)}) %collective-permute-start.7) | collective-permute-done | bytes 36896 | tf_op jit(solution)/shard_map/ppermute | solution.py:368
  28.6 1.8 %collective-permute-start.8 = (bf16[144,128]{1,0:T(8,128)(2,1)S(1)}, bf16[144,128]{1,0:T(8,128)(2,1)S(1)}, u32[]{:S(2)}, u32[]{:S(2)}) collective-permute-start(bf16[144,128]{1,0:T(8,128)(2,1)S(1)} %add_convert_fusion), channel_id=1, source_target_pairs={{0,5},{1,13},{2,14},{3,6},{4,8},{5,0},{6,3},{7,11},{8,4},{9,12},{1... | collective-permute-start | bytes 110600 | tf_op jit(solution)/shard_map/ppermute | solution.py:368
  30.5 1.6 %collective-permute-done.8 = bf16[144,128]{1,0:T(8,128)(2,1)S(1)} collective-permute-done((bf16[144,128]{1,0:T(8,128)(2,1)S(1)}, bf16[144,128]{1,0:T(8,128)(2,1)S(1)}, u32[]{:S(2)}, u32[]{:S(2)}) %collective-permute-start.8) | collective-permute-done | bytes 36896 | tf_op jit(solution)/shard_map/ppermute | solution.py:368
  32.1 0.4 %collective-permute-start.9 = (f32[144,128]{1,0:T(8,128)S(1)}, f32[144,128]{1,0:T(8,128)S(1)}, u32[]{:S(2)}, u32[]{:S(2)}) collective-permute-start(f32[144,128]{1,0:T(8,128)S(1)} %convert_add_fusion.a_ref), channel_id=1, source_target_pairs={{0,4},{4,0},{8,12},{12,8},{1,5},{5,1},{9,13},{13,9},{2,6},{6,2},{1... | collective-permute-start | bytes 221192 | tf_op jit(solution)/shard_map/ppermute | solution.py:505
  32.6 0.9 %collective-permute-done.9.b_ref = f32[144,128]{1,0:T(8,128)S(1)} collective-permute-done((f32[144,128]{1,0:T(8,128)S(1)}, f32[144,128]{1,0:T(8,128)S(1)}, u32[]{:S(2)}, u32[]{:S(2)}) %collective-permute-start.9) | collective-permute-done | bytes 73760 | tf_op jit(solution)/shard_map/ppermute | solution.py:505
  33.5 0.7 %last.1 = (f32[128,128]{1,0:T(8,128)}, f32[3,3,4,64]{3,2,1,0:T(4,128)}, f32[64,256]{1,0:T(8,128)}) custom-call(f32[144,128]{1,0:T(8,128)S(1)} %convert_add_fusion.a_ref, f32[144,128]{1,0:T(8,128)S(1)} %collective-permute-done.9.b_ref), custom_call_target="tpu_custom_call" | custom-call | tf_op jit(solution)/shard_map/last/pallas_call | solution.py:486
  (10 shorter events, 0.2 us)
Async XLA Ops:
  1.5 6.1 %collective-permute-start = (bf16[16,2,256]{2,1,0:T(2,128)(2,1)S(1)}, bf16[16,2,256]{2,1,0:T(2,128)(2,1)S(1)}, u32[]{:S(2)}, u32[]{:S(2)}) collective-permute-start(bf16[16,2,256]{2,1,0:T(2,128)(2,1)S(1)} %get-tuple-element.58), channel_id=1, source_target_pairs={{0,4},{1,2},{2,1},{3,7},{4,0},{5,6},{6,5},{7,3},{8,12},{9,10},{10,... | collective-permute-start | bytes 49160 | tf_op jit(solution)/shard_map/ppermute | solution.py:34
  2.0 5.9 %collective-permute-start.1 = (bf16[16,2,256]{2,1,0:T(2,128)(2,1)S(1)}, bf16[16,2,256]{2,1,0:T(2,128)(2,1)S(1)}, u32[]{:S(2)}, u32[]{:S(2)}) collective-permute-start(bf16[16,2,256]{2,1,0:T(2,128)(2,1)S(1)} %get-tuple-element.59), channel_id=1, source_target_pairs={{0,1},{1,0},{2,3},{3,2},{4,5},{5,4},{6,7},{7,6},{8,9},{9,8},{10,11... | collective-permute-start | bytes 49160 | tf_op jit(solution)/shard_map/ppermute | solution.py:20
  8.1 4.7 %collective-permute-start.2 = (bf16[360,256]{1,0:T(8,128)(2,1)S(1)}, bf16[360,256]{1,0:T(8,128)(2,1)S(1)}, u32[]{:S(2)}, u32[]{:S(2)}) collective-permute-start(bf16[360,256]{1,0:T(8,128)(2,1)S(1)} %get-tuple-element.90), channel_id=1, source_target_pairs={{0,4},{4,0},{8,12},{12,8},{1,5},{5,1},{9,13},{13,9},{2,6},{6,2},{1... | collective-permute-start | bytes 552968 | tf_op jit(solution)/shard_map/ppermute | solution.py:20
  8.2 5.6 %collective-permute-start.3 = (bf16[360,256]{1,0:T(8,128)(2,1)S(1)}, bf16[360,256]{1,0:T(8,128)(2,1)S(1)}, u32[]{:S(2)}, u32[]{:S(2)}) collective-permute-start(bf16[360,256]{1,0:T(8,128)(2,1)S(1)} %get-tuple-element.91), channel_id=1, source_target_pairs={{0,16},{1,17},{2,18},{3,19},{4,8},{5,9},{6,10},{7,11},{8,4},{9,5},... | collective-permute-start | bytes 552968 | tf_op jit(solution)/shard_map/ppermute | solution.py:34
  15.8 1.4 %collective-permute-start.4 = (f32[2,144,128]{2,1,0:T(8,128)S(1)}, f32[2,144,128]{2,1,0:T(8,128)S(1)}, u32[]{:S(2)}, u32[]{:S(2)}) collective-permute-start(f32[2,144,128]{2,1,0:T(8,128)S(1)} %slice_bitcast_fusion), channel_id=1, source_target_pairs={{0,4},{4,0},{8,12},{12,8},{1,5},{5,1},{9,13},{13,9},{2,6},{6,2},{1... | collective-permute-start | bytes 442376 | tf_op jit(solution)/shard_map/ppermute | solution.py:461
  17.3 3.5 %collective-permute-start.5 = (bf16[1,144,128]{2,1,0:T(8,128)(2,1)S(1)}, bf16[1,144,128]{2,1,0:T(8,128)(2,1)S(1)}, u32[]{:S(2)}, u32[]{:S(2)}) collective-permute-start(bf16[1,144,128]{2,1,0:T(8,128)(2,1)S(1)} %slice.15), channel_id=1, source_target_pairs={{0,20},{1,21},{2,22},{3,23},{4,16},{5,17},{6,18},{7,19},{8,28},{9,... | collective-permute-start | bytes 110600 | tf_op jit(solution)/shard_map/ppermute | solution.py:368
  20.8 3.4 %collective-permute-start.6 = (bf16[144,128]{1,0:T(8,128)(2,1)S(1)}, bf16[144,128]{1,0:T(8,128)(2,1)S(1)}, u32[]{:S(2)}, u32[]{:S(2)}) collective-permute-start(bf16[144,128]{1,0:T(8,128)(2,1)S(1)} %fusion.1), channel_id=1, source_target_pairs={{0,12},{1,7},{2,4},{3,15},{4,2},{5,9},{6,10},{7,1},{8,14},{9,5},{1... | collective-permute-start | bytes 110600 | tf_op jit(solution)/shard_map/ppermute | solution.py:368
  24.3 4.3 %collective-permute-start.7 = (bf16[144,128]{1,0:T(8,128)(2,1)S(1)}, bf16[144,128]{1,0:T(8,128)(2,1)S(1)}, u32[]{:S(2)}, u32[]{:S(2)}) collective-permute-start(bf16[144,128]{1,0:T(8,128)(2,1)S(1)} %add_convert_fusion.1), channel_id=1, source_target_pairs={{0,6},{1,4},{2,7},{3,5},{4,1},{5,3},{6,0},{7,2},{8,13},{9,15},{10,... | collective-permute-start | bytes 110600 | tf_op jit(solution)/shard_map/ppermute | solution.py:368
  28.6 3.5 %collective-permute-start.8 = (bf16[144,128]{1,0:T(8,128)(2,1)S(1)}, bf16[144,128]{1,0:T(8,128)(2,1)S(1)}, u32[]{:S(2)}, u32[]{:S(2)}) collective-permute-start(bf16[144,128]{1,0:T(8,128)(2,1)S(1)} %add_convert_fusion), channel_id=1, source_target_pairs={{0,5},{1,13},{2,14},{3,6},{4,8},{5,0},{6,3},{7,11},{8,4},{9,12},{1... | collective-permute-start | bytes 110600 | tf_op jit(solution)/shard_map/ppermute | solution.py:368
  32.1 1.3 %collective-permute-start.9 = (f32[144,128]{1,0:T(8,128)S(1)}, f32[144,128]{1,0:T(8,128)S(1)}, u32[]{:S(2)}, u32[]{:S(2)}) collective-permute-start(f32[144,128]{1,0:T(8,128)S(1)} %convert_add_fusion.a_ref), channel_id=1, source_target_pairs={{0,4},{4,0},{8,12},{12,8},{1,5},{5,1},{9,13},{13,9},{2,6},{6,2},{1... | collective-permute-start | bytes 221192 | tf_op jit(solution)/shard_map/ppermute | solution.py:505

commit v10 on v8

--- a/solution.py
+++ b/solution.py
@@ -455,7 +455,7 @@
         name="rim",
     )(x, c, strip, row_even, row_odd, *shared, acts, gcat, d1, gw3, full, gw1, xt, same, pick)
     near = [(i, i ^ 1) for i in range(n_row)]
-    shares = (shares[0] + lax.ppermute(shares[1], "row", near)).astype(BF)
+    shares = (shares[0] + lax.ppermute(shares[1].astype(BF), "row", near).astype(F32)).astype(BF)
     g1_rim, shares = lax.optimization_barrier((g1_rim, shares))
     input_grad = pl.pallas_call(
         functools.partial(out_kernel, **sizes),

time: 34.5 us -> 34.4 us (level)
  no operation moved by 1% of the time
where the time goes in v10:
time: 34.4 us; the launch traced here: 34.2 us
  starting transfers between devices  12.6 us (37%)
  waiting for transfers between devices  11.5 us (33%)
  Pallas kernels  9.27 us (27%)
  between operations  0.73 us (2%)
    ppermute x4, waiting for transfers between devices, crossed(): return lax.ppermute(value, names, perm)  8.13 us
    ppermute x4, starting transfers between devices, crossed(): return lax.ppermute(value, names, perm)  5.69 us
    ppermute x2, starting transfers between devices, swap_edges(): got_even = lax.ppermute(to_even, axis, [(i, i ^ 1) for i in range(count)])  4.22 us
    pallas_call x1, Pallas kernels, body(): pl.pallas_call(functools.partial(inner_kernel, inner=inner, **sizes), out...  3.04 us
    ppermute x2, starting transfers between devices, swap_edges(): got_odd = lax.ppermute(to_odd, names, perm)  2.1 us
    pallas_call x1, Pallas kernels, body(): pl.pallas_call(functools.partial(rim_kernel, inner=inner, group_ch=group_...  1.94 us
    pallas_call x1, Pallas kernels, body(): pl.pallas_call(functools.partial(load_kernel, inner=inner, group_ch=group...  1.4 us
    ppermute x1, waiting for transfers between devices, body(): lax.ppermute(shares[1].astype(BF), 'row', near).astype(F32)  1.16 us
  transfers between devices with their start and end apart: 10, of which 8 were waited for; matrix products, arithmetic and copies ran while one was open for 0% of the time, Pallas kernels for 16%

profile of v10, /device:TPU:0, one launch (start us, length us, event | category | flops | bytes accessed | tf_op | source)
XLA Modules:
  0.0 34.2 jit_solution(3594497203191174206)
XLA Ops:
  0.6 0.9 %cut.1 = (bf16[16,2,256]{2,1,0:T(2,128)(2,1)S(1)}, bf16[16,2,256]{2,1,0:T(2,128)(2,1)S(1)}) custom-call(bf16[8,128,256]{2,1,0:T(8,128)(2,1)} %bitcast.18, bf16[8,128,256]{2,1,0:T(8,128)(2,1)} %bitcast.20), custom_call_target="tpu_custom_call" | custom-call | tf_op jit(solution)/shard_map/cut/pallas_call | solution.py:387
  1.5 0.5 %collective-permute-start = (bf16[16,2,256]{2,1,0:T(2,128)(2,1)S(1)}, bf16[16,2,256]{2,1,0:T(2,128)(2,1)S(1)}, u32[]{:S(2)}, u32[]{:S(2)}) collective-permute-start(bf16[16,2,256]{2,1,0:T(2,128)(2,1)S(1)} %get-tuple-element.58), channel_id=1, source_target_pairs={{0,4},{1,2},{2,1},{3,7},{4,0},{5,6},{6,5},{7,3},{8,12},{9,10},{10,... | collective-permute-start | bytes 49160 | tf_op jit(solution)/shard_map/ppermute | solution.py:34
  2.0 4.1 %collective-permute-start.1 = (bf16[16,2,256]{2,1,0:T(2,128)(2,1)S(1)}, bf16[16,2,256]{2,1,0:T(2,128)(2,1)S(1)}, u32[]{:S(2)}, u32[]{:S(2)}) collective-permute-start(bf16[16,2,256]{2,1,0:T(2,128)(2,1)S(1)} %get-tuple-element.59), channel_id=1, source_target_pairs={{0,1},{1,0},{2,3},{3,2},{4,5},{5,4},{6,7},{7,6},{8,9},{9,8},{10,11... | collective-permute-start | bytes 49160 | tf_op jit(solution)/shard_map/ppermute | solution.py:20
  6.2 1.4 %load.1 = (bf16[128,256]{1,0:T(8,128)(2,1)S(1)}, bf16[256,128]{1,0:T(8,128)(2,1)S(1)}, bf16[8,128,256]{2,1,0:T(8,128)(2,1)S(1)}, bf16[8,128,256]{2,1,0:T(8,128)(...) custom-call(bf16[3,3,4,128]{3,2,1,0:T(4,128)(2,1)} %refs_0_.1, ...), custom_call_target="tpu_custom_call" | custom-call | tf_op jit(solution)/shard_map/load/pallas_call | solution.py:401
  7.6 0.3 collective-permute-done.1.col_even
  7.9 0.2 edges.1
  8.2 1.6 %collective-permute-start.3 = (bf16[360,256]{1,0:T(8,128)(2,1)S(1)}, bf16[360,256]{1,0:T(8,128)(2,1)S(1)}, u32[]{:S(2)}, u32[]{:S(2)}) collective-permute-start(bf16[360,256]{1,0:T(8,128)(2,1)S(1)} %get-tuple-element.91), channel_id=1, source_target_pairs={{0,16},{1,17},{2,18},{3,19},{4,8},{5,9},{6,10},{7,11},{8,4},{9,5},... | collective-permute-start | bytes 552968 | tf_op jit(solution)/shard_map/ppermute | solution.py:34
  9.8 3.0 %inner.1 = (bf16[8,144,384]{2,1,0:T(8,128)(2,1)S(1)}, bf16[6,144,384]{2,1,0:T(8,128)(2,1)S(1)}, f32[1024,128]{1,0:T(8,128)S(1)}, f32[768,256]{1,0:T(8,128)S(1)},...) custom-call(bf16[8,128,256]{2,1,0:T(8,128)(2,1)S(1)} %get-tuple-elem, ...), custom_call_target="tpu_custom_call" | custom-call | tf_op jit(solution)/shard_map/inner/pallas_call | solution.py:425
  12.9 1.0 %collective-permute-done.3.row_odd = bf16[360,256]{1,0:T(8,128)(2,1)S(1)} collective-permute-done((bf16[360,256]{1,0:T(8,128)(2,1)S(1)}, bf16[360,256]{1,0:T(8,128)(2,1)S(1)}, u32[]{:S(2)}, u32[]{:S(2)}) %collective-permute-start.3) | collective-permute-done | bytes 184352 | tf_op jit(solution)/shard_map/ppermute | solution.py:34
  13.8 1.9 %rim.1 = (f32[2,2,152,128]{3,2,1,0:T(8,128)S(1)}, bf16[512,128]{1,0:T(8,128)(2,1)S(1)}, f32[256,256]{1,0:T(8,128)S(1)}) custom-call(bf16[8,128,256]{2,1,0:T(8,128)(2,1)S(1)} %get-tuple-element.73.x_ref, bf16[8,128,256]{2,1,0:T(8,128)(2,1)S(1)} %get-tuple-element.74.c_ref, bf16[16,16,256]{2,1,0:T(8,128)(2,1)S(1)} %get-tuple-element.80.strip_ref, ...), custom_call_target="tpu_custom_call" | custom-call | tf_op jit(solution)/shard_map/rim/pallas_call | solution.py:444
  15.8 0.2 collective-permute-start.4
  16.0 1.2 %collective-permute-done.4 = bf16[2,152,128]{2,1,0:T(8,128)(2,1)S(1)} collective-permute-done((bf16[2,152,128]{2,1,0:T(8,128)(2,1)S(1)}, bf16[2,152,128]{2,1,0:T(8,128)(2,1)S(1)}, u32[]{:S(2)}, u32[]{:S(2)}) %collective-permute-start.4) | collective-permute-done | bytes 77856 | tf_op jit(solution)/shard_map/ppermute | solution.py:458
  17.2 1.3 %collective-permute-start.5 = (bf16[1,152,128]{2,1,0:T(8,128)(2,1)S(1)}, bf16[1,152,128]{2,1,0:T(8,128)(2,1)S(1)}, u32[]{:S(2)}, u32[]{:S(2)}) collective-permute-start(bf16[1,152,128]{2,1,0:T(8,128)(2,1)S(1)} %slice.16), channel_id=1, source_target_pairs={{0,20},{1,21},{2,22},{3,23},{4,16},{5,17},{6,18},{7,19},{8,28},{9,... | collective-permute-start | bytes 116744 | tf_op jit(solution)/shard_map/ppermute | solution.py:365
  18.5 2.2 %collective-permute-done.5 = bf16[1,152,128]{2,1,0:T(8,128)(2,1)S(1)} collective-permute-done((bf16[1,152,128]{2,1,0:T(8,128)(2,1)S(1)}, bf16[1,152,128]{2,1,0:T(8,128)(2,1)S(1)}, u32[]{:S(2)}, u32[]{:S(2)}) %collective-permute-start.5) | collective-permute-done | bytes 38944 | tf_op jit(solution)/shard_map/ppermute | solution.py:365
  20.7 0.7 %collective-permute-start.6 = (bf16[152,128]{1,0:T(8,128)(2,1)S(1)}, bf16[152,128]{1,0:T(8,128)(2,1)S(1)}, u32[]{:S(2)}, u32[]{:S(2)}) collective-permute-start(bf16[152,128]{1,0:T(8,128)(2,1)S(1)} %fusion.2), channel_id=1, source_target_pairs={{0,12},{1,7},{2,4},{3,15},{4,2},{5,9},{6,10},{7,1},{8,14},{9,5},{1... | collective-permute-start | bytes 116744 | tf_op jit(solution)/shard_map/ppermute | solution.py:365
  21.5 1.1 %out.1 = bf16[8,128,256]{2,1,0:T(8,128)(2,1)} custom-call(bf16[512,128]{1,0:T(8,128)(2,1)S(1)} %get-tuple-element.89.g1_in, bf16[512,128]{1,0:T(8,128)(2,1)S(1)} %get-tuple-element.103.g1_rim, f32[768,256]{1,0:T(8,128)S(1)} %get-tuple-element.104.back_in, f32[256,256]{1,0:T(8,128)S(1)} %get-tuple-element.105.back_rim, ...), custom_call_target="tpu_custom_call" | custom-call | tf_op jit(solution)/shard_map/out/pallas_call | solution.py:460
  22.6 1.6 %collective-permute-done.6 = bf16[152,128]{1,0:T(8,128)(2,1)S(1)} collective-permute-done((bf16[152,128]{1,0:T(8,128)(2,1)S(1)}, bf16[152,128]{1,0:T(8,128)(2,1)S(1)}, u32[]{:S(2)}, u32[]{:S(2)}) %collective-permute-start.6) | collective-permute-done | bytes 38944 | tf_op jit(solution)/shard_map/ppermute | solution.py:365
  24.2 1.7 %collective-permute-start.7 = (bf16[152,128]{1,0:T(8,128)(2,1)S(1)}, bf16[152,128]{1,0:T(8,128)(2,1)S(1)}, u32[]{:S(2)}, u32[]{:S(2)}) collective-permute-start(bf16[152,128]{1,0:T(8,128)(2,1)S(1)} %add_convert_fusion.1), channel_id=1, source_target_pairs={{0,6},{1,4},{2,7},{3,5},{4,1},{5,3},{6,0},{7,2},{8,13},{9,15},{10,... | collective-permute-start | bytes 116744 | tf_op jit(solution)/shard_map/ppermute | solution.py:365
  26.0 2.6 %collective-permute-done.7 = bf16[152,128]{1,0:T(8,128)(2,1)S(1)} collective-permute-done((bf16[152,128]{1,0:T(8,128)(2,1)S(1)}, bf16[152,128]{1,0:T(8,128)(2,1)S(1)}, u32[]{:S(2)}, u32[]{:S(2)}) %collective-permute-start.7) | collective-permute-done | bytes 38944 | tf_op jit(solution)/shard_map/ppermute | solution.py:365
  28.6 1.9 %collective-permute-start.8 = (bf16[152,128]{1,0:T(8,128)(2,1)S(1)}, bf16[152,128]{1,0:T(8,128)(2,1)S(1)}, u32[]{:S(2)}, u32[]{:S(2)}) collective-permute-start(bf16[152,128]{1,0:T(8,128)(2,1)S(1)} %add_convert_fusion), channel_id=1, source_target_pairs={{0,5},{1,13},{2,14},{3,6},{4,8},{5,0},{6,3},{7,11},{8,4},{9,12},{1... | collective-permute-start | bytes 116744 | tf_op jit(solution)/shard_map/ppermute | solution.py:365
  30.5 1.7 %collective-permute-done.8 = bf16[152,128]{1,0:T(8,128)(2,1)S(1)} collective-permute-done((bf16[152,128]{1,0:T(8,128)(2,1)S(1)}, bf16[152,128]{1,0:T(8,128)(2,1)S(1)}, u32[]{:S(2)}, u32[]{:S(2)}) %collective-permute-start.8) | collective-permute-done | bytes 38944 | tf_op jit(solution)/shard_map/ppermute | solution.py:365
  32.1 0.4 %collective-permute-start.9 = (f32[152,128]{1,0:T(8,128)S(1)}, f32[152,128]{1,0:T(8,128)S(1)}, u32[]{:S(2)}, u32[]{:S(2)}) collective-permute-start(f32[152,128]{1,0:T(8,128)S(1)} %convert_add_fusion.a_ref), channel_id=1, source_target_pairs={{0,4},{4,0},{8,12},{12,8},{1,5},{5,1},{9,13},{13,9},{2,6},{6,2},{1... | collective-permute-start | bytes 233480 | tf_op jit(solution)/shard_map/ppermute | solution.py:502
  32.6 0.9 %collective-permute-done.9.b_ref = f32[152,128]{1,0:T(8,128)S(1)} collective-permute-done((f32[152,128]{1,0:T(8,128)S(1)}, f32[152,128]{1,0:T(8,128)S(1)}, u32[]{:S(2)}, u32[]{:S(2)}) %collective-permute-start.9) | collective-permute-done | bytes 77856 | tf_op jit(solution)/shard_map/ppermute | solution.py:502
  33.5 0.7 %last.1 = (f32[128,128]{1,0:T(8,128)}, f32[3,3,4,64]{3,2,1,0:T(4,128)}, f32[64,256]{1,0:T(8,128)}) custom-call(f32[152,128]{1,0:T(8,128)S(1)} %convert_add_fusion.a_ref, f32[152,128]{1,0:T(8,128)S(1)} %collective-permute-done.9.b_ref), custom_call_target="tpu_custom_call" | custom-call | tf_op jit(solution)/shard_map/last/pallas_call | solution.py:483
  (10 shorter events, 0.2 us)
Async XLA Ops:
  1.5 6.1 %collective-permute-start = (bf16[16,2,256]{2,1,0:T(2,128)(2,1)S(1)}, bf16[16,2,256]{2,1,0:T(2,128)(2,1)S(1)}, u32[]{:S(2)}, u32[]{:S(2)}) collective-permute-start(bf16[16,2,256]{2,1,0:T(2,128)(2,1)S(1)} %get-tuple-element.58), channel_id=1, source_target_pairs={{0,4},{1,2},{2,1},{3,7},{4,0},{5,6},{6,5},{7,3},{8,12},{9,10},{10,... | collective-permute-start | bytes 49160 | tf_op jit(solution)/shard_map/ppermute | solution.py:34
  2.0 5.9 %collective-permute-start.1 = (bf16[16,2,256]{2,1,0:T(2,128)(2,1)S(1)}, bf16[16,2,256]{2,1,0:T(2,128)(2,1)S(1)}, u32[]{:S(2)}, u32[]{:S(2)}) collective-permute-start(bf16[16,2,256]{2,1,0:T(2,128)(2,1)S(1)} %get-tuple-element.59), channel_id=1, source_target_pairs={{0,1},{1,0},{2,3},{3,2},{4,5},{5,4},{6,7},{7,6},{8,9},{9,8},{10,11... | collective-permute-start | bytes 49160 | tf_op jit(solution)/shard_map/ppermute | solution.py:20
  8.1 4.7 %collective-permute-start.2 = (bf16[360,256]{1,0:T(8,128)(2,1)S(1)}, bf16[360,256]{1,0:T(8,128)(2,1)S(1)}, u32[]{:S(2)}, u32[]{:S(2)}) collective-permute-start(bf16[360,256]{1,0:T(8,128)(2,1)S(1)} %get-tuple-element.90), channel_id=1, source_target_pairs={{0,4},{4,0},{8,12},{12,8},{1,5},{5,1},{9,13},{13,9},{2,6},{6,2},{1... | collective-permute-start | bytes 552968 | tf_op jit(solution)/shard_map/ppermute | solution.py:20
  8.2 5.6 %collective-permute-start.3 = (bf16[360,256]{1,0:T(8,128)(2,1)S(1)}, bf16[360,256]{1,0:T(8,128)(2,1)S(1)}, u32[]{:S(2)}, u32[]{:S(2)}) collective-permute-start(bf16[360,256]{1,0:T(8,128)(2,1)S(1)} %get-tuple-element.91), channel_id=1, source_target_pairs={{0,16},{1,17},{2,18},{3,19},{4,8},{5,9},{6,10},{7,11},{8,4},{9,5},... | collective-permute-start | bytes 552968 | tf_op jit(solution)/shard_map/ppermute | solution.py:34
  15.8 1.3 %collective-permute-start.4 = (bf16[2,152,128]{2,1,0:T(8,128)(2,1)S(1)}, bf16[2,152,128]{2,1,0:T(8,128)(2,1)S(1)}, u32[]{:S(2)}, u32[]{:S(2)}) collective-permute-start(bf16[2,152,128]{2,1,0:T(8,128)(2,1)S(1)} %fusion.1), channel_id=1, source_target_pairs={{0,4},{4,0},{8,12},{12,8},{1,5},{5,1},{9,13},{13,9},{2,6},{6,2},{1... | collective-permute-start | bytes 233480 | tf_op jit(solution)/shard_map/ppermute | solution.py:458
  17.2 3.5 %collective-permute-start.5 = (bf16[1,152,128]{2,1,0:T(8,128)(2,1)S(1)}, bf16[1,152,128]{2,1,0:T(8,128)(2,1)S(1)}, u32[]{:S(2)}, u32[]{:S(2)}) collective-permute-start(bf16[1,152,128]{2,1,0:T(8,128)(2,1)S(1)} %slice.16), channel_id=1, source_target_pairs={{0,20},{1,21},{2,22},{3,23},{4,16},{5,17},{6,18},{7,19},{8,28},{9,... | collective-permute-start | bytes 116744 | tf_op jit(solution)/shard_map/ppermute | solution.py:365
  20.7 3.5 %collective-permute-start.6 = (bf16[152,128]{1,0:T(8,128)(2,1)S(1)}, bf16[152,128]{1,0:T(8,128)(2,1)S(1)}, u32[]{:S(2)}, u32[]{:S(2)}) collective-permute-start(bf16[152,128]{1,0:T(8,128)(2,1)S(1)} %fusion.2), channel_id=1, source_target_pairs={{0,12},{1,7},{2,4},{3,15},{4,2},{5,9},{6,10},{7,1},{8,14},{9,5},{1... | collective-permute-start | bytes 116744 | tf_op jit(solution)/shard_map/ppermute | solution.py:365
  24.2 4.4 %collective-permute-start.7 = (bf16[152,128]{1,0:T(8,128)(2,1)S(1)}, bf16[152,128]{1,0:T(8,128)(2,1)S(1)}, u32[]{:S(2)}, u32[]{:S(2)}) collective-permute-start(bf16[152,128]{1,0:T(8,128)(2,1)S(1)} %add_convert_fusion.1), channel_id=1, source_target_pairs={{0,6},{1,4},{2,7},{3,5},{4,1},{5,3},{6,0},{7,2},{8,13},{9,15},{10,... | collective-permute-start | bytes 116744 | tf_op jit(solution)/shard_map/ppermute | solution.py:365
  28.6 3.5 %collective-permute-start.8 = (bf16[152,128]{1,0:T(8,128)(2,1)S(1)}, bf16[152,128]{1,0:T(8,128)(2,1)S(1)}, u32[]{:S(2)}, u32[]{:S(2)}) collective-permute-start(bf16[152,128]{1,0:T(8,128)(2,1)S(1)} %add_convert_fusion), channel_id=1, source_target_pairs={{0,5},{1,13},{2,14},{3,6},{4,8},{5,0},{6,3},{7,11},{8,4},{9,12},{1... | collective-permute-start | bytes 116744 | tf_op jit(solution)/shard_map/ppermute | solution.py:365
  32.1 1.3 %collective-permute-start.9 = (f32[152,128]{1,0:T(8,128)S(1)}, f32[152,128]{1,0:T(8,128)S(1)}, u32[]{:S(2)}, u32[]{:S(2)}) collective-permute-start(f32[152,128]{1,0:T(8,128)S(1)} %convert_add_fusion.a_ref), channel_id=1, source_target_pairs={{0,4},{4,0},{8,12},{12,8},{1,5},{5,1},{9,13},{13,9},{2,6},{6,2},{1... | collective-permute-start | bytes 233480 | tf_op jit(solution)/shard_map/ppermute | solution.py:502
